TPU v7x, 256 devices: a whole 4x4x8 slice. The times are simulated.
256 devices in a mesh: temp: 8 (over y, core), dom: 32 (over x, z).
Axes of the slice: x: 4, y: 4, z: 8, core: 2. Of those that a mesh axis runs over, the one named last changes fastest.
Arguments:
- particles: bfloat16 [8, 16384, 3072], P('temp', 'dom'), may hold values from -6 to 6
- log_weights: float32 [8, 16384], P('temp', 'dom'), may hold values from -200 to 200
- offspring: int32 [8, 256], P('temp', 'dom'), may hold values from 0 to 2, as said below
- even_pairs: int32 [8, 256], P('temp', 'dom'), may hold values from 0 to 1, as said below
- odd_pairs: int32 [8, 256], P('temp', 'dom'), may hold values from 0 to 1, as said below
- inverse_temp: float32 [8], P('temp'), may hold values from 0.5 to 4
- flow_in: bfloat16 [1536, 512], replicated, may hold values from -0.15625 to 0.15625
- flow_mid: bfloat16 [512, 512], replicated, may hold values from -0.25 to 0.25
- flow_out: bfloat16 [512, 3072], replicated, may hold values from -0.25 to 0.25
- energy_in: bfloat16 [3072, 512], replicated, may hold values from -0.109375 to 0.109375
- energy_mid: bfloat16 [512, 512], replicated, may hold values from -0.25 to 0.25
- energy_out: float32 [512], replicated, may hold values from -0.25 to 0.25
Outputs:
- new_particles: bfloat16 [8, 16384, 3072], P('temp', 'dom')
- new_log_weights: float32 [8, 16384], P('temp', 'dom')
- log_ess: float32 [8], P('temp')
Inputs may be any that keep to these rules, and one draw needn't show every extreme that they name: `offspring`: counts are 0, 1 or 2 and each group's counts sum to 256. Of the 8 blocks of one device at most 1 have count 2 and at most 1 have count 0; in every group some device has exactly 1 with count 2 and some device exactly 1 with count 0. `even_pairs`: groups 2i and 2i + 1 carry equal rows. At most 2 of the 8 blocks of one device are 1, and in every pair some device has exactly 2. `odd_pairs`: groups 2i + 1 and 2i + 2 carry equal rows; groups 0 and 7 are all 0. At most 2 of the 8 blocks of one device are 1, and in every pair some device has exactly 2.
All inputs are finite; a program needn't handle non-finite values.
Results may differ from a plain program's by a relative error of at most 0.0024.
Values may be sent and summed in bfloat16 or wider, within the bound.
No kernel may reach another device: no remote copies, remote signals or barrier semaphores. Data moves between devices by JAX's collectives and lax.ppermute only.
A program may use at most 128 MiB of HBM per device.

v0:
```python
import jax
import jax.numpy as jnp
from jax import lax
from jax.sharding import PartitionSpec as P

SURPLUS = 1
SWAPS = 2


old_level = 0.5
new_level = 0.75
scale_limit = 0.05


def with_halo(block, sides, width):
    for axis, dim in sides:
        count = lax.axis_size(axis)
        forward = [(i, i + 1) for i in range(count - 1)]
        backward = [(target, source) for source, target in forward]
        low = lax.ppermute(
            lax.slice_in_dim(block, block.shape[dim] - width, None, axis=dim), axis, forward
        )
        high = lax.ppermute(lax.slice_in_dim(block, 0, width, axis=dim), axis, backward)
        block = jnp.concatenate([low, block, high], axis=dim)
    return block


def transport(row_data, flow_in, flow_mid, flow_out):
    half_width = row_data.shape[1] // 2
    kept_half = row_data[:, :half_width]
    moved_half = row_data[:, half_width:]
    hidden_one = jax.nn.gelu(
        jnp.dot(kept_half, flow_in, preferred_element_type=jnp.float32)
    ).astype(jnp.bfloat16)
    hidden_two = jax.nn.gelu(
        jnp.dot(hidden_one, flow_mid, preferred_element_type=jnp.float32)
    ).astype(jnp.bfloat16)
    scale_shift = jnp.dot(hidden_two, flow_out, preferred_element_type=jnp.float32)
    log_scale = scale_limit * jnp.tanh(scale_shift[:, :half_width])
    offset_rows = (
        moved_half.astype(jnp.float32) * jnp.exp(log_scale) + scale_shift[:, half_width:]
    ).astype(jnp.bfloat16)
    return (jnp.concatenate([kept_half, offset_rows], axis=1), jnp.sum(log_scale, axis=1))


def energy(row_data, energy_in, energy_mid, energy_out):
    layer_one = jax.nn.gelu(
        jnp.dot(row_data, energy_in, preferred_element_type=jnp.float32)
    ).astype(jnp.bfloat16)
    layer_two = jax.nn.gelu(jnp.dot(layer_one, energy_mid, preferred_element_type=jnp.float32))
    return jnp.sum(layer_two * energy_out[None, :], axis=1)


def table_lookup(table, index):
    positions = jnp.arange(table.shape[0], dtype=jnp.int32)
    index = jnp.asarray(index)
    return jnp.sum(jnp.where(positions == index[..., None], table, 0), axis=-1)


def pick_rows(flags, rank_order, slot_count):
    slot_ids = jnp.arange(slot_count, dtype=jnp.int32)
    positions = jnp.arange(flags.shape[0], dtype=jnp.int32)
    matches = (flags[None, :] == 1) & (rank_order[None, :] == slot_ids[:, None])
    return jnp.sum(jnp.where(matches, positions[None, :], 0), axis=1)


def neighbour_swap(blocks, swap_mask, parity):
    block_rows = blocks.shape[1]
    features = blocks.shape[2]
    rank_order = jnp.cumsum(swap_mask) - 1
    chosen = pick_rows(swap_mask, rank_order, SWAPS)
    packed = jnp.take(blocks, chosen, axis=0).reshape(SWAPS * block_rows, features)
    extended = with_halo(packed, (("temp", 0),), SWAPS * block_rows)
    from_lower = extended[: SWAPS * block_rows]
    from_upper = extended[2 * SWAPS * block_rows :]
    upper_side = lax.axis_index("temp") % 2 == parity
    received = jnp.where(upper_side, from_upper, from_lower).reshape(SWAPS, block_rows, features)
    placed_at = jnp.clip(rank_order, 0, SWAPS - 1)
    return jnp.where((swap_mask == 1)[:, None, None], jnp.take(received, placed_at, axis=0), blocks)


def per_device(
    particles,
    log_weights,
    offspring,
    even_pairs,
    odd_pairs,
    inverse_temp,
    flow_in,
    flow_mid,
    flow_out,
    energy_in,
    energy_mid,
    energy_out,
):
    block_count = offspring.shape[1]
    features = particles.shape[2]
    block_rows = particles.shape[1] // block_count
    spare_rows = SURPLUS * block_rows
    blocks = particles[0].reshape(block_count, block_rows, features)
    counts = offspring[0]
    doubled = (counts == 2).astype(jnp.int32)
    discarded_rows = (counts == 0).astype(jnp.int32)
    spare_rank = jnp.cumsum(doubled) - 1
    vacant_rank = jnp.cumsum(discarded_rows) - 1
    weights = (
        log_weights[0].reshape(block_count, block_rows)
        - jnp.log(jnp.maximum(counts, 1).astype(jnp.float32))[:, None]
    )
    spare_ids = pick_rows(doubled, spare_rank, SURPLUS)
    spare_blocks = jnp.take(blocks, spare_ids, axis=0).reshape(spare_rows, features)
    spare_weights = jnp.take(weights, spare_ids, axis=0)
    own_tally = (
        jnp.stack([jnp.sum(doubled), jnp.sum(discarded_rows)]).astype(jnp.float32).reshape(1, 2)
    )
    all_tallies, all_spare_weights = (
        lax.all_gather(own_tally, "dom", axis=0, tiled=True),
        lax.all_gather(spare_weights, "dom", axis=0, tiled=True),
    )
    tally_ints = all_tallies.astype(jnp.int32)
    dom_count = lax.axis_size("dom")
    self_index = lax.axis_index("dom")
    spare_end = jnp.cumsum(tally_ints[:, 0])
    spare_start = spare_end - tally_ints[:, 0]
    vacant_start = jnp.cumsum(tally_ints[:, 1]) - tally_ints[:, 1]
    slot_ids = jnp.arange(SURPLUS, dtype=jnp.int32)
    own_rank = table_lookup(vacant_start, self_index) + slot_ids
    is_live = slot_ids < table_lookup(tally_ints[:, 1], self_index)
    device = jnp.sum((spare_end <= own_rank[..., None]).astype(jnp.int32), axis=-1)
    device = jnp.clip(device, 0, dom_count - 1)
    source_slot = own_rank - table_lookup(spare_start, device)
    wanted = device * SURPLUS + jnp.clip(source_slot, 0, SURPLUS - 1)
    wanted_rows = (
        wanted[:, None] * block_rows + jnp.arange(block_rows, dtype=jnp.int32)[None, :]
    ).reshape(spare_rows)
    flat_weights = all_spare_weights.reshape(-1)
    filled_weights = jnp.take(flat_weights, jnp.clip(wanted_rows, 0, flat_weights.shape[0] - 1))
    live_rows = jnp.repeat(is_live, block_rows)
    shard_rows = lax.all_gather(spare_blocks, "dom", axis=0, tiled=True)
    row_numbers = jnp.arange(shard_rows.shape[0], dtype=jnp.int32)
    matches = ((wanted_rows[:, None] == row_numbers[None, :]) & live_rows[:, None]).astype(
        jnp.bfloat16
    )
    filled = jnp.dot(matches, shard_rows, preferred_element_type=jnp.float32)
    fill_at = jnp.clip(vacant_rank, 0, SURPLUS - 1)
    vacant = discarded_rows == 1
    filled_blocks = filled.astype(jnp.bfloat16).reshape(SURPLUS, block_rows, features)
    blocks = jnp.where(vacant[:, None, None], jnp.take(filled_blocks, fill_at, axis=0), blocks)
    weights = jnp.where(
        vacant[:, None],
        jnp.take(filled_weights.reshape(SURPLUS, block_rows), fill_at, axis=0),
        weights,
    )
    blocks = neighbour_swap(blocks, even_pairs[0], 0)
    blocks = neighbour_swap(blocks, odd_pairs[0], 1)
    row_data = blocks.reshape(block_count * block_rows, features)
    moved, log_det = transport(row_data, flow_in, flow_mid, flow_out)
    before = energy(row_data, energy_in, energy_mid, energy_out)
    after = energy(moved, energy_in, energy_mid, energy_out)
    updated = (
        weights.reshape(-1) + log_det - inverse_temp[0] * (new_level * after - old_level * before)
    )
    peak = lax.pmax(jnp.max(updated), "dom")
    first_sum, second_sum = lax.psum(
        (jnp.sum(jnp.exp(updated - peak)), jnp.sum(jnp.exp(2.0 * (updated - peak)))), "dom"
    )
    particle_total = updated.shape[0] * dom_count
    new_log_weights = updated - (peak + jnp.log(first_sum))
    log_ess = 2.0 * jnp.log(first_sum) - jnp.log(second_sum) - jnp.log(jnp.float32(particle_total))
    return (moved.reshape(1, -1, features), new_log_weights.reshape(1, -1), log_ess.reshape(1))


def solution(mesh):
    in_specs = (
        P("temp", "dom", None),
        P("temp", "dom"),
        P("temp", "dom"),
        P("temp", "dom"),
        P("temp", "dom"),
        P("temp"),
        P(),
        P(),
        P(),
        P(),
        P(),
        P(),
    )
    out_specs = (P("temp", "dom", None), P("temp", "dom"), P("temp"))
    return jax.shard_map(
        per_device, mesh=mesh, in_specs=in_specs, out_specs=out_specs, check_vma=False
    )
```

profile of v0, /device:TPU:16, one launch (start us, length us, event | category | flops | bytes accessed | tf_op | source)
XLA Modules:
  0.0 420.5 jit_solution(16230202601258679156)
XLA Ops:
  7.2 0.8 compare_convert_fusion
  8.2 1.4 fusion.123
  11.5 1.8 dynamic-slice_select_fusion
  13.5 1.3 fusion.100
  14.8 41.8 %all-gather.1 = f32[32,1,2]{2,1,0:T(1,128)S(1)} all-gather(f32[1,1,2]{2,1,0:T(1,128)S(1)} %fusion.100), channel_id=1, replica_groups=mesh['temp'=8,'dom'=32] {'dom'}, dimensions={0}, use_global_device_ids=true | all-gather | bytes 264 | tf_op jit(solution)/shard_map/all_gather | solution.py:117
  57.2 0.7 fusion.97
  57.9 1.3 subtract_reduce_fusion
  59.9 0.7 fusion.98
  62.5 0.8 reduce-window.38
  63.3 0.8 reduce-window.37
  64.8 1.4 reduce.27
  67.5 0.7 compare_bitcast_fusion.2
  69.4 1.2 log_bitcast_fusion
  71.2 63.9 %all-gather.5.cloned.1.call-done = bf16[1,2048,3072]{2,1,0:T(8,128)(2,1)} async-done(((bf16[1,64,3072]{2,1,0:T(8,128)(2,1)}), bf16[1,2048,3072]{2,1,0:T(8,128)(2,1)}) %all-gather.5.cloned.1.call-update) | async-done | bytes 12582928 | tf_op jit(solution)/shard_map/all_gather | solution.py:139
  135.1 7.1 %fusion.2 = bf16[64,3072]{1,0:T(8,128)(2,1)S(1)} fusion(bf16[1,2048,3072]{2,1,0:T(8,128)(2,1)} %all-gather.5.cloned.1.call-done, s32[64]{0:T(128)} %iota_add_fusion, pred[]{:T(512)S(6)} %lt.54), kind=kOutput, calls=%fused_computation.7 | convolution fusion | flops 805765120 | bytes 12976385 | tf_op jit(solution)/shard_map/dot_general | solution.py:144
  142.2 2.3 select_select_fusion.2
  144.5 3.4 gather_fusion.1
  147.9 2.2 broadcast_select_fusion.1
  150.0 1.9 collective-permute-start
  151.9 2.4 collective-permute-start.1
  155.7 1.1 compare_and_fusion.2
  157.4 4.3 %collective-permute-done = bf16[128,3072]{1,0:T(8,128)(2,1)} collective-permute-done((bf16[128,3072]{1,0:T(8,128)(2,1)}, bf16[128,3072]{1,0:T(8,128)(2,1)}, u32[]{:S(2)}, u32[]{:S(2)}) %collective-permute-start) | collective-permute-done | bytes 786464 | tf_op jit(solution)/shard_map/ppermute | solution.py:23
  161.7 3.8 collective-permute-done.1
  165.6 2.1 broadcast_select_fusion.2
  167.7 3.5 gather_fusion.2
  171.2 5.2 %select_select_fusion.1 = bf16[8,64,3072]{2,1,0:T(8,128)(2,1)} fusion(bf16[8,64,3072]{2,1,0:T(8,128)(2,1)} %gather_fusion.2, pred[8]{0:T(512)(128)(4,1)} %get-tuple-element.43, pred[8]{0:T(512)(128)(4,1)} %copy-done.14, bf16[8,64,3072]{2,1,0:T(8,128)(2,1)} %bitcast.80, bf16[64,3072]{1,0:T(8,128)(2,1)S(1)} %fusion.2, pred[8]{0:T(512)(128)(4,1)} %copy-done.6, ...), kind=kLoop, calls=%fused_computation.14 | loop fusion | flops 6291456 | bytes 9830432 | tf_op jit(solution)/shard_map/jit(_where)/select_n | solution.py:79
  176.4 3.4 gather_fusion.3
  179.8 2.2 broadcast_select_fusion
  182.0 1.9 collective-permute-start.2
  183.9 2.4 collective-permute-start.3
  186.3 37.7 %all-gather.2 = f32[32,1,64]{2,1,0:T(1,128)S(1)} all-gather(f32[1,1,64]{2,1,0:T(1,128)S(1)} %copy-done.11), channel_id=1, replica_groups=mesh['temp'=8,'dom'=32] {'dom'}, dimensions={0}, use_global_device_ids=true | all-gather | bytes 8448 | tf_op jit(solution)/shard_map/all_gather | solution.py:118
  224.0 0.7 reduce.28
  224.8 0.8 gather_fusion
  226.8 2.1 broadcast_select_fusion.3
  228.9 3.5 gather_fusion.4
  232.5 3.3 select_select_fusion
  235.8 1.3 slice.53
  237.0 0.9 copy-done.2
  238.3 2.0 fusion.124
  240.3 6.4 %fusion.65 = f32[512,3072]{1,0:T(8,128)} fusion(bf16[512,3072]{1,0:T(8,128)(2,1)S(1)} %copy-done, bf16[512,512]{1,0:T(8,128)(2,1)} %param.23, f32[512,512]{1,0:T(8,128)} %fusion.124), kind=kOutput, calls=%fused_computation.81 | convolution fusion | flops 1883766784 | bytes 11010048 | tf_op jit(solution)/shard_map/dot_general | solution.py:38
  246.7 4.7 %fusion.7 = (f32[512]{0:T(512)S(1)}, bf16[512,1536]{1,0:T(8,128)(2,1)S(1)}) fusion(f32[512,3072]{1,0:T(8,128)} %fusion.65, bf16[512,3072]{1,0:T(8,128)(2,1)} %bitcast.84), kind=kLoop, calls=%fused_computation.16 | loop fusion | flops 4718080 | bytes 9439232 | tf_op jit(solution)/shard_map/reduce_sum | solution.py:43
  251.3 1.1 copy-done.3
  252.5 2.1 fusion.9
  254.6 5.4 %fusion.60 = f32[512]{0:T(512)S(1)} fusion(bf16[512,512]{1,0:T(8,128)(2,1)} %param.26, f32[512]{0:T(512)S(1)} %copy-done.17, bf16[512,3072]{1,0:T(8,128)(2,1)} %bitcast.85, bf16[3072,512]{1,0:T(8,128)(2,1)} %param.25), kind=kOutput, calls=%fused_computation.75 | convolution fusion | flops 1884028416 | bytes 6819840 | tf_op jit(solution)/shard_map/dot_general | solution.py:50
  260.1 5.5 %fusion.43 = f32[512]{0:T(512)S(1)} fusion(bf16[512,512]{1,0:T(8,128)(2,1)} %param.26, bf16[3072,512]{1,0:T(8,128)(2,1)} %param.25, bf16[512,1536]{1,0:T(8,128)(2,1)} %copy-done.3, bf16[512,1536]{1,0:T(8,128)(2,1)} %slice.53, f32[512]{0:T(512)S(1)} %copy-done.17), kind=kOutput, calls=%fused_computation.58 | convolution fusion | flops 1890319872 | bytes 6819840 | tf_op jit(solution)/shard_map/dot_general | solution.py:50
  266.2 71.4 %pmax.7 = f32[]{:T(128)} all-reduce(f32[]{:T(128)} %get-tuple-element.38), channel_id=1, replica_groups=mesh['temp'=8,'dom'=32] {'dom'}, use_global_device_ids=true, to_apply=%region_19.22 | all-reduce | flops 1 | bytes 8 | tf_op jit(solution)/shard_map/pmax | solution.py:163
  337.6 1.3 exponential_reduce_fusion
  338.9 71.1 %all-reduce = (f32[]{:T(128)}, f32[]{:T(128)}) all-reduce(f32[]{:T(128)} %get-tuple-element.30, f32[]{:T(128)} %get-tuple-element.29), channel_id=1, replica_groups=mesh['temp'=8,'dom'=32] {'dom'}, use_global_device_ids=true, to_apply=%region_21.24 | all-reduce | flops 2 | bytes 16 | tf_op jit(solution)/shard_map/psum | solution.py:164
  (87 shorter events, 8.8 us)
Async XLA Ops:
  7.2 233.1 %copy-start = (bf16[512,3072]{1,0:T(8,128)(2,1)S(1)}, bf16[512,3072]{1,0:T(8,128)(2,1)}, u32[]{:S(2)}) copy-start(bf16[512,3072]{1,0:T(8,128)(2,1)} %param.24) | copy-start | bytes 9437188
  7.2 127.9 %all-gather.5.cloned.1.call-start = ((), (), s32[]{:S(2)}) async-start(), calls=%async_computation | async-start | bytes 12976128 | tf_op jit(solution)/shard_map/all_gather | solution.py:139
  8.0 146.4 %copy-start.8 = (pred[8]{0:T(512)(128)(4,1)}, pred[8]{0:T(512)(128)(4,1)S(1)}, u32[]{:S(2)}) copy-start(pred[8]{0:T(512)(128)(4,1)S(1)} %get-tuple-element.51) | copy-start | bytes 28
  63.3 4.1 copy-start.18
  64.2 7.1 %copy-start.20 = (s32[8,1]{0,1:T(1,128)}, s32[8,1]{0,1:T(1,128)S(1)}, u32[]{:S(2)}) copy-start(s32[8,1]{0,1:T(1,128)S(1)} %reduce-window.37) | copy-start | bytes 100
  67.4 2.0 copy-start.12
  68.2 0.6 copy-start.14
  70.7 71.5 %copy-start.6 = (pred[8]{0:T(512)(128)(4,1)}, pred[8]{0:T(512)(128)(4,1)S(1)}, u32[]{:S(2)}) copy-start(pred[8]{0:T(512)(128)(4,1)S(1)} %compare_bitcast_fusion) | copy-start | bytes 28
  135.1 7.1 %copy-start.1 = (bf16[1,512,3072]{2,1,0:T(8,128)(2,1)S(1)}, bf16[1,512,3072]{2,1,0:T(8,128)(2,1)}, u32[]{:S(2)}) copy-start(bf16[1,512,3072]{2,1,0:T(8,128)(2,1)} %param.16) | copy-start | bytes 9437188
  144.5 9.9 %copy-start.9 = (f32[8]{0:T(128)S(1)}, f32[8]{0:T(128)}, u32[]{:S(2)}) copy-start(f32[8]{0:T(128)} %log_bitcast_fusion) | copy-start | bytes 100
  150.0 11.7 %collective-permute-start = (bf16[128,3072]{1,0:T(8,128)(2,1)}, bf16[128,3072]{1,0:T(8,128)(2,1)}, u32[]{:S(2)}, u32[]{:S(2)}) collective-permute-start(bf16[128,3072]{1,0:T(8,128)(2,1)} %bitcast.19), channel_id=1, source_target_pairs={{32,0},{64,32},{96,64},{128,96},{160,128},{192,160},{224,192},{33,... | collective-permute-start | bytes 2359304 | tf_op jit(solution)/shard_map/ppermute | solution.py:23
  151.9 13.6 %collective-permute-start.1 = (bf16[128,3072]{1,0:T(8,128)(2,1)}, bf16[128,3072]{1,0:T(8,128)(2,1)}, u32[]{:S(2)}, u32[]{:S(2)}) collective-permute-start(bf16[128,3072]{1,0:T(8,128)(2,1)} %bitcast.19), channel_id=1, source_target_pairs={{0,32},{32,64},{64,96},{96,128},{128,160},{160,192},{192,224},{1,3... | collective-permute-start | bytes 2359304 | tf_op jit(solution)/shard_map/ppermute | solution.py:20
  176.4 9.9 %copy-start.11 = (f32[1,1,64]{2,1,0:T(1,128)S(1)}, f32[1,1,64]{2,1,0:T(1,128)}, u32[]{:S(2)}) copy-start(f32[1,1,64]{2,1,0:T(1,128)} %fusion.95) | copy-start | bytes 772
  176.4 49.2 %copy-start.7 = (pred[8]{0:T(512)(128)(4,1)S(1)}, pred[8]{0:T(512)(128)(4,1)}, u32[]{:S(2)}) copy-start(pred[8]{0:T(512)(128)(4,1)} %copy-done.6) | copy-start | bytes 28
  176.4 49.4 %copy-start.10 = (f32[8]{0:T(128)S(1)}, f32[8]{0:T(128)}, u32[]{:S(2)}) copy-start(f32[8]{0:T(128)} %log_bitcast_fusion) | copy-start | bytes 100
  176.4 50.3 %copy-start.19 = (s32[8,1]{0,1:T(1,128)S(1)}, s32[8,1]{0,1:T(1,128)}, u32[]{:S(2)}) copy-start(s32[8,1]{0,1:T(1,128)} %copy-done.18) | copy-start | bytes 100
  182.0 44.8 %collective-permute-start.2 = (bf16[128,3072]{1,0:T(8,128)(2,1)}, bf16[128,3072]{1,0:T(8,128)(2,1)}, u32[]{:S(2)}, u32[]{:S(2)}) collective-permute-start(bf16[128,3072]{1,0:T(8,128)(2,1)} %bitcast.21), channel_id=1, source_target_pairs={{32,0},{64,32},{96,64},{128,96},{160,128},{192,160},{224,192},{33,... | collective-permute-start | bytes 2359304 | tf_op jit(solution)/shard_map/ppermute | solution.py:23
  183.9 42.9 %collective-permute-start.3 = (bf16[128,3072]{1,0:T(8,128)(2,1)}, bf16[128,3072]{1,0:T(8,128)(2,1)}, u32[]{:S(2)}, u32[]{:S(2)}) collective-permute-start(bf16[128,3072]{1,0:T(8,128)(2,1)} %bitcast.21), channel_id=1, source_target_pairs={{0,32},{32,64},{64,96},{96,128},{128,160},{160,192},{192,224},{1,3... | collective-permute-start | bytes 2359304 | tf_op jit(solution)/shard_map/ppermute | solution.py:20
  228.9 3.6 copy-start.13
  235.7 2.2 copy-start.2
  235.7 2.6 copy-start.16
  246.7 5.8 %copy-start.4 = (bf16[512,1536]{1,0:T(8,128)(2,1)S(1)}, bf16[512,1536]{1,0:T(8,128)(2,1)}, u32[]{:S(2)}) copy-start(bf16[512,1536]{1,0:T(8,128)(2,1)} %slice.53) | copy-start | bytes 4718596
  251.3 1.2 copy-start.3
  252.5 2.1 copy-start.17
  260.1 5.5 %copy-start.5 = (f32[1,512]{1,0:T(1,128)S(1)}, f32[1,512]{1,0:T(1,128)}, u32[]{:S(2)}) copy-start(f32[1,512]{1,0:T(1,128)} %param.17) | copy-start | bytes 6148
  260.1 5.5 %copy-start.15 = (pred[512]{0:T(512)(128)(4,1)S(1)}, pred[512]{0:T(512)(128)(4,1)}, u32[]{:S(2)}) copy-start(pred[512]{0:T(512)(128)(4,1)} %broadcast_in_dim.169) | copy-start | bytes 1540
Sparse Core Ops, SparseCore 0:
  13.5 121.6 all-gather.4
where the time goes:
time: 422 us; the launch traced here: 421 us
  blocking collectives  222 us (53%)
  waiting for transfers between devices  72 us (17%)
  other arithmetic  47.8 us (11%)
  matrix products  26.3 us (6%)
  between operations  22.6 us (5%)
  local copies, waits for them, and re-layouts  21.1 us (5%)
  starting transfers between devices  8.67 us (2%)
    pmax x1, blocking collectives, per_device(): peak = lax.pmax(jnp.max(updated), 'dom')  71.4 us
    psum x1, blocking collectives, per_device(): lax.psum((jnp.sum(jnp.exp(updated - peak)), jnp.sum(jnp.exp(2.0 * (update...  71.1 us
    all_gather x1, waiting for transfers between devices, per_device(): shard_rows = lax.all_gather(spare_blocks, 'dom', axis=0, tiled=True)  63.9 us
    all_gather x1, blocking collectives, per_device(): lax.all_gather(own_tally, 'dom', axis=0, tiled=True)  41.8 us
    all_gather x1, blocking collectives, per_device(): lax.all_gather(spare_weights, 'dom', axis=0, tiled=True)  37.7 us
    dot_general x2, matrix products, energy(): jnp.dot(layer_one, energy_mid, preferred_element_type=jnp.float32)  10.9 us
    select_n x2, other arithmetic, neighbour_swap(): jnp.where((swap_mask == 1)[:, None, None], jnp.take(received, placed_at,...  8.46 us
  transfers between devices with their start and end apart: 5, of which 3 were waited for; matrix products, arithmetic and copies ran while one was open for 4% of the time, Pallas kernels for 0%

commit v1 on v0

v1 whole, which is shorter than its diff:
```python
import jax
import jax.numpy as jnp
from jax import lax
from jax.sharding import PartitionSpec as P

SURPLUS = 1
SWAPS = 2


old_level = 0.5
new_level = 0.75
scale_limit = 0.05


def transport(row_data, flow_in, flow_mid, flow_out):
    half_width = row_data.shape[1] // 2
    kept_half = row_data[:, :half_width]
    moved_half = row_data[:, half_width:]
    hidden_one = jax.nn.gelu(
        jnp.dot(kept_half, flow_in, preferred_element_type=jnp.float32)
    ).astype(jnp.bfloat16)
    hidden_two = jax.nn.gelu(
        jnp.dot(hidden_one, flow_mid, preferred_element_type=jnp.float32)
    ).astype(jnp.bfloat16)
    scale_shift = jnp.dot(hidden_two, flow_out, preferred_element_type=jnp.float32)
    log_scale = scale_limit * jnp.tanh(scale_shift[:, :half_width])
    offset_rows = (
        moved_half.astype(jnp.float32) * jnp.exp(log_scale) + scale_shift[:, half_width:]
    ).astype(jnp.bfloat16)
    return (jnp.concatenate([kept_half, offset_rows], axis=1), jnp.sum(log_scale, axis=1))


def energy(row_data, energy_in, energy_mid, energy_out):
    layer_one = jax.nn.gelu(
        jnp.dot(row_data, energy_in, preferred_element_type=jnp.float32)
    ).astype(jnp.bfloat16)
    layer_two = jax.nn.gelu(jnp.dot(layer_one, energy_mid, preferred_element_type=jnp.float32))
    return jnp.sum(layer_two * energy_out[None, :], axis=1)


def pick_rows(flags, rank_order, slot_count):
    slot_ids = jnp.arange(slot_count, dtype=jnp.int32)
    positions = jnp.arange(flags.shape[0], dtype=jnp.int32)
    matches = (flags[None, :] == 1) & (rank_order[None, :] == slot_ids[:, None])
    return jnp.sum(jnp.where(matches, positions[None, :], 0), axis=1)


def broadcast_rows(row, count):
    stacked = jnp.broadcast_to(row[None], (count,) + row.shape)
    return lax.all_to_all(stacked, "dom", 0, 0, tiled=True)


def to_pieces(block):
    rows, features = block.shape
    cut = block.reshape(rows // 8, 8, 4, features // 4)
    return cut.transpose(0, 2, 1, 3).reshape(rows // 2, 8, features // 4)


def from_pieces(pieces):
    count, _, width = pieces.shape
    cut = pieces.reshape(count // 4, 4, 8, width)
    return cut.transpose(0, 2, 1, 3).reshape(count * 2, width * 4)


def neighbour_swap(blocks, swap_mask, pairs):
    rank_order = jnp.cumsum(swap_mask) - 1
    chosen = pick_rows(swap_mask, rank_order, SWAPS)
    packed = jnp.concatenate([lax.dynamic_slice_in_dim(blocks, chosen[i], 1) for i in range(SWAPS)])
    received = lax.ppermute(packed, "temp", pairs)
    for i in range(SWAPS):
        hit = (swap_mask == 1) & (rank_order == i)
        blocks = jnp.where(hit[:, None, None], received[i][None], blocks)
    return blocks


def per_device(
    particles,
    log_weights,
    offspring,
    even_pairs,
    odd_pairs,
    inverse_temp,
    flow_in,
    flow_mid,
    flow_out,
    energy_in,
    energy_mid,
    energy_out,
):
    block_count = offspring.shape[1]
    features = particles.shape[2]
    block_rows = particles.shape[1] // block_count
    spare_rows = SURPLUS * block_rows
    blocks = particles[0].reshape(block_count, block_rows, features)
    counts = offspring[0]
    doubled = (counts == 2).astype(jnp.int32)
    discarded_rows = (counts == 0).astype(jnp.int32)
    spare_rank = jnp.cumsum(doubled) - 1
    vacant_rank = jnp.cumsum(discarded_rows) - 1
    weights = (
        log_weights[0].reshape(block_count, block_rows)
        - jnp.log(jnp.maximum(counts, 1).astype(jnp.float32))[:, None]
    )
    spare_ids = pick_rows(doubled, spare_rank, SURPLUS)
    spare_blocks = jnp.take(blocks, spare_ids, axis=0).reshape(spare_rows, features)
    spare_weights = jnp.take(weights, spare_ids, axis=0)
    dom_count = lax.axis_size("dom")
    self_index = lax.axis_index("dom")
    tally = jnp.stack([jnp.sum(doubled), jnp.sum(discarded_rows)]).astype(jnp.float32)
    own_row = jnp.concatenate(
        [spare_weights.reshape(-1), tally, jnp.zeros((128 - block_rows - 2,), jnp.float32)]
    ).reshape(1, 128)
    all_rows = broadcast_rows(own_row, dom_count).reshape(dom_count, 128)
    tallies = all_rows[:, block_rows : block_rows + 2].astype(jnp.int32)
    before_mask = jnp.tril(jnp.ones((dom_count, dom_count), jnp.int32), -1)
    starts = jnp.sum(before_mask[:, :, None] * tallies[None], axis=1)
    wanted = (
        (tallies[:, 1] == 1)[:, None]
        & (tallies[:, 0] == 1)[None, :]
        & (starts[:, 1][:, None] == starts[:, 0][None, :])
    )
    held = lax.all_to_all(to_pieces(spare_blocks), "dom", 0, 0, tiled=True)
    piece_shape = held.shape
    routed = jnp.dot(
        wanted.astype(jnp.bfloat16),
        held.reshape(dom_count, -1),
        preferred_element_type=jnp.float32,
    ).astype(jnp.bfloat16)
    filled = from_pieces(lax.all_to_all(routed.reshape(piece_shape), "dom", 0, 0, tiled=True))
    own_wanted = lax.dynamic_slice_in_dim(wanted, self_index, 1)[0]
    filled_weights = jnp.sum(
        jnp.where(own_wanted[:, None], all_rows[:, :block_rows], 0.0), axis=0
    )
    vacant = discarded_rows == 1
    blocks = jnp.where(vacant[:, None, None], filled[None], blocks)
    weights = jnp.where(vacant[:, None], filled_weights[None], weights)
    groups = lax.axis_size("temp")
    even = [(i, i + 1 - 2 * (i % 2)) for i in range(groups)]
    odd = [(i, i - 1 + 2 * (i % 2)) for i in range(1, groups - 1)]
    blocks = neighbour_swap(blocks, even_pairs[0], even)
    blocks = neighbour_swap(blocks, odd_pairs[0], odd)
    row_data = blocks.reshape(block_count * block_rows, features)
    moved, log_det = transport(row_data, flow_in, flow_mid, flow_out)
    before = energy(row_data, energy_in, energy_mid, energy_out)
    after = energy(moved, energy_in, energy_mid, energy_out)
    updated = (
        weights.reshape(-1) + log_det - inverse_temp[0] * (new_level * after - old_level * before)
    )
    own_peak = jnp.max(updated)
    shifted = jnp.exp(updated - own_peak)
    own_stats = jnp.stack([own_peak, jnp.sum(shifted), jnp.sum(shifted * shifted)])
    own_stats = jnp.concatenate([own_stats, jnp.zeros((125,), jnp.float32)]).reshape(1, 128)
    stats = broadcast_rows(own_stats, dom_count).reshape(dom_count, 128)
    peak = jnp.max(stats[:, 0])
    factor = jnp.exp(stats[:, 0] - peak)
    first_sum = jnp.sum(stats[:, 1] * factor)
    second_sum = jnp.sum(stats[:, 2] * factor * factor)
    particle_total = updated.shape[0] * dom_count
    new_log_weights = updated - (peak + jnp.log(first_sum))
    log_ess = 2.0 * jnp.log(first_sum) - jnp.log(second_sum) - jnp.log(jnp.float32(particle_total))
    return (moved.reshape(1, -1, features), new_log_weights.reshape(1, -1), log_ess.reshape(1))


def solution(mesh):
    in_specs = (
        P("temp", "dom", None),
        P("temp", "dom"),
        P("temp", "dom"),
        P("temp", "dom"),
        P("temp", "dom"),
        P("temp"),
        P(),
        P(),
        P(),
        P(),
        P(),
        P(),
    )
    out_specs = (P("temp", "dom", None), P("temp", "dom"), P("temp"))
    return jax.shard_map(
        per_device, mesh=mesh, in_specs=in_specs, out_specs=out_specs, check_vma=False
    )
```

time: 422 us -> 166 us (0.39)
  blocking collectives: 222 us -> 0 us
  waiting for transfers between devices: 72 us -> 26.1 us
  starting transfers between devices: 8.67 us -> 28.9 us
  between operations: 22.6 us -> 14.6 us
  matrix products: 26.3 us -> 20.3 us
  local copies, waits for them, and re-layouts: 21.1 us -> 26.9 us
    all_gather x2 -> x0, blocking collectives: 79.6 us -> none  [the longest x1 41.8 us: per_device(): lax.all_gather(own_tally, 'dom', axis=0, tiled=True)]
    pmax x1 -> x0, blocking collectives: 71.4 us -> none  [per_device(): peak = lax.pmax(jnp.max(updated), 'dom')]
    psum x1 -> x0, blocking collectives: 71.1 us -> none  [per_device(): lax.psum((jnp.sum(jnp.exp(updated - peak)), jnp.sum(jnp.exp(2.0 * (update...]
    all_gather x1 -> x0, waiting for transfers between devices: 63.9 us -> none  [per_device(): shard_rows = lax.all_gather(spare_blocks, 'dom', axis=0, tiled=True)]
    all_to_all x0 -> x4, starting transfers between devices: none -> 26.3 us  [the longest x2 17.2 us: broadcast_rows(): return lax.all_to_all(stacked, 'dom', 0, 0, tiled=True)]
    all_to_all x0 -> x4, waiting for transfers between devices: none -> 26.1 us  [the longest x2 13.2 us: broadcast_rows(): return lax.all_to_all(stacked, 'dom', 0, 0, tiled=True)]
    broadcast_in_dim x3 -> x21, local copies, waits for them, and re-layouts: 0.72 us -> 16.8 us  [the longest x10 12.1 us: neighbour_swap(): blocks = jnp.where(hit[:, None, None], received[i][None], blocks)]
    gather x5 -> x0, local copies, waits for them, and re-layouts: 14.6 us -> none  [the longest x2 7.09 us: neighbour_swap(): jnp.take(received, placed_at, axis=0)]
  transfers between devices with their start and end apart: 5 -> 6, of which waited for: 3 -> 4; matrix products, arithmetic and copies ran while one was open for 4% -> 22% of each run, Pallas kernels for 0% -> 0%
where the time goes in v1:
time: 166 us; the launch traced here: 164 us
  other arithmetic  46.7 us (28%)
  starting transfers between devices  28.9 us (17%)
  local copies, waits for them, and re-layouts  26.9 us (16%)
  waiting for transfers between devices  26.1 us (16%)
  matrix products  20.3 us (12%)
  between operations  14.6 us (9%)
    all_to_all x2, starting transfers between devices, broadcast_rows(): return lax.all_to_all(stacked, 'dom', 0, 0, tiled=True)  17.2 us
    all_to_all x2, waiting for transfers between devices, broadcast_rows(): return lax.all_to_all(stacked, 'dom', 0, 0, tiled=True)  13.2 us
    broadcast_in_dim x10, local copies, waits for them, and re-layouts, neighbour_swap(): blocks = jnp.where(hit[:, None, None], received[i][None], blocks)  12.1 us
    dot_general x2, matrix products, energy(): jnp.dot(layer_one, energy_mid, preferred_element_type=jnp.float32)  10.9 us
    all_to_all x1, waiting for transfers between devices, per_device(): held = lax.all_to_all(to_pieces(spare_blocks), 'dom', 0, 0, tiled=True)  8.98 us
    select_n x2, other arithmetic, neighbour_swap(): blocks = jnp.where(hit[:, None, None], received[i][None], blocks)  6.61 us
    dot_general x1, matrix products, transport(): jnp.dot(hidden_two, flow_out, preferred_element_type=jnp.float32)  6.38 us
    reduce_sum x1, other arithmetic, transport(): jnp.sum(log_scale, axis=1)  5.77 us
  transfers between devices with their start and end apart: 6, of which 4 were waited for; matrix products, arithmetic and copies ran while one was open for 22% of the time, Pallas kernels for 0%

profile of v1, /device:TPU:16, one launch (start us, length us, event | category | flops | bytes accessed | tf_op | source)
XLA Modules:
  0.0 163.7 jit_solution(17840375157387707015)
XLA Ops:
  0.6 1.3 compare_convert_fusion
  2.8 1.4 fusion.117
  6.7 1.3 reduce.29
  8.2 1.4 add_convert_fusion
  10.3 11.3 %all-to-all-start = ((f32[32,1,128]{2,1,0:T(1,128)}), f32[32,1,128]{2,1,0:T(1,128)S(1)}, u32[]{:S(2)}, u32[]{:S(2)}) async-start(f32[32,1,128]{2,1,0:T(1,128)} %broadcast_in_dim.233), calls=%async_computation | async-start | bytes 32768 | tf_op jit(solution)/shard_map/all_to_all | solution.py:50
  21.6 1.8 %dynamic-slice_select_fusion = bf16[1,64,3072]{2,1,0:T(8,128)(2,1)} fusion(bf16[8,64,3072]{2,1,0:T(8,128)(2,1)} %bitcast.112, s32[]{:T(128)} %bitcast.10, pred[]{:T(512)} %bitcast.8), kind=kLoop, calls=%fused_computation.94 | loop fusion | flops 196608 | bytes 786437 | tf_op jit(solution)/shard_map/jit(_take)/select_n | solution.py:105
  24.1 7.3 %all-to-all-done = f32[32,1,128]{2,1,0:T(1,128)S(1)} async-done(((f32[32,1,128]{2,1,0:T(1,128)}), f32[32,1,128]{2,1,0:T(1,128)S(1)}, u32[]{:S(2)}, u32[]{:S(2)}) %all-to-all-start) | async-done | bytes 16416 | tf_op jit(solution)/shard_map/all_to_all | solution.py:50
  31.4 3.9 %all-to-all-start.1 = ((bf16[32,8,768]{2,1,0:T(8,128)(2,1)}), bf16[32,8,768]{2,1,0:T(8,128)(2,1)S(1)}, u32[]{:S(2)}, u32[]{:S(2)}) async-start(bf16[32,8,768]{2,1,0:T(8,128)(2,1)} %bitcast.20), calls=%async_computation.1 | async-start | bytes 786432 | tf_op jit(solution)/shard_map/all_to_all | solution.py:122
  35.3 1.3 compare_bitcast_fusion.1
  39.6 9.0 %all-to-all-done.1 = bf16[32,8,768]{2,1,0:T(8,128)(2,1)S(1)} async-done(((bf16[32,8,768]{2,1,0:T(8,128)(2,1)}), bf16[32,8,768]{2,1,0:T(8,128)(2,1)S(1)}, u32[]{:S(2)}, u32[]{:S(2)}) %all-to-all-start.1) | async-done | bytes 393248 | tf_op jit(solution)/shard_map/all_to_all | solution.py:122
  48.7 1.0 convolution_convert_fusion
  50.5 5.2 %all-to-all-start.2 = ((bf16[32,8,768]{2,1,0:T(8,128)(2,1)}), bf16[32,8,768]{2,1,0:T(8,128)(2,1)S(1)}, u32[]{:S(2)}, u32[]{:S(2)}) async-start(bf16[32,8,768]{2,1,0:T(8,128)(2,1)} %bitcast.118), calls=%async_computation.2 | async-start | bytes 786432 | tf_op jit(solution)/shard_map/all_to_all | solution.py:129
  55.7 1.2 compare_bitcast_fusion.2
  64.6 3.9 %all-to-all-done.2 = bf16[32,8,768]{2,1,0:T(8,128)(2,1)S(1)} async-done(((bf16[32,8,768]{2,1,0:T(8,128)(2,1)}), bf16[32,8,768]{2,1,0:T(8,128)(2,1)S(1)}, u32[]{:S(2)}, u32[]{:S(2)}) %all-to-all-start.2) | async-done | bytes 393248 | tf_op jit(solution)/shard_map/all_to_all | solution.py:129
  68.5 2.3 %broadcast_select_fusion = bf16[8,64,3072]{2,1,0:T(8,128)(2,1)S(1)} fusion(bf16[8,64,3072]{2,1,0:T(8,128)(2,1)} %bitcast.113, pred[8]{0:T(512)(128)(4,1)S(1)} %copy-done.16, bf16[64,3072]{1,0:T(8,128)(2,1)S(1)} %bitcast.115), kind=kLoop, calls=%fused_computation.12 | loop fusion | flops 1572864 | bytes 6684680 | tf_op jit(solution)/shard_map/jit(_where)/select_n | solution.py:135
  70.9 0.9 pad_maximum_fusion.14
  77.0 1.2 slice_bitcast_fusion.3
  78.2 3.3 %select_select_fusion = bf16[8,64,3072]{2,1,0:T(8,128)(2,1)S(1)} fusion(pred[8]{0:T(512)(128)(4,1)S(1)} %get-tuple-element.55, pred[8]{0:T(512)(128)(4,1)S(1)} %get-tuple-element.54, bf16[64,3072]{1,0:T(8,128)(2,1)S(1)} %get-tuple-element.49, bf16[64,3072]{1,0:T(8,128)(2,1)S(1)} %get-tuple-element.48, bf16[8,64,3072]{2,1,0:T(8,128)(2,1)} %bitcast.114, ...), kind=kLoop, calls=%fused_computation.11 | loop fusion | flops 4718592 | bytes 7471128 | tf_op jit(solution)/shard_map/jit(_where)/select_n | solution.py:72
  81.6 0.9 pad_maximum_fusion.15
  82.6 2.6 %collective-permute-start.1 = (bf16[2,64,3072]{2,1,0:T(8,128)(2,1)}, bf16[2,64,3072]{2,1,0:T(8,128)(2,1)}, u32[]{:S(2)}, u32[]{:S(2)}) collective-permute-start(bf16[2,64,3072]{2,1,0:T(8,128)(2,1)} %pad_maximum_fusion.15), channel_id=1, source_target_pairs={{32,64},{64,32},{96,128},{128,96},{160,192},{192,160},{33,65},{65,... | collective-permute-start | bytes 2359304 | tf_op jit(solution)/shard_map/ppermute | solution.py:69
  85.9 1.3 broadcast_in_dim.266
  87.1 1.4 broadcast_in_dim.269
  88.5 1.3 sub.123
  89.8 1.3 sub.129
  91.1 1.3 sub.125
  92.5 1.3 broadcast_in_dim.257
  93.8 1.3 broadcast_in_dim.258
  95.1 1.3 broadcast_in_dim.261
  96.3 1.3 broadcast_in_dim.262
  97.6 1.2 compare_and_fusion.4
  99.5 1.3 broadcast_in_dim.225
  100.8 1.3 broadcast_in_dim.251
  102.2 1.3 broadcast_in_dim.252
  105.2 1.2 slice_bitcast_fusion.1
  106.4 3.3 %fusion.5 = bf16[512,3072]{1,0:T(8,128)(2,1)S(1)} fusion(bf16[1,512,3072]{2,1,0:T(8,128)(2,1)} %param.12, pred[512]{0:T(512)(128)(4,1)} %broadcast_in_dim.266, pred[512]{0:T(512)(128)(4,1)} %broadcast_in_dim.262, pred[512]{0:T(512)(128)(4,1)} %broadcast_in_dim.258, pred[512]{0:T(512)(128)(4,1)} %broadcast_in_dim.252, pred[512]{0:T(512)(128)(4,1)} %broadcast_in_dim.225, ...), kind=kLoop, calls=%fused_computation.10 | loop fusion | flops 7864320 | bytes 8260096 | tf_op jit(solution)/shard_map/jit(_where)/select_n | solution.py:72
  109.7 1.2 slice.108
  111.0 0.9 copy-done.1
  112.3 2.1 %fusion.118 = f32[512,512]{1,0:T(8,128)} fusion(bf16[1536,512]{1,0:T(8,128)(2,1)S(1)} %copy-done.20, bf16[512,3072]{1,0:T(8,128)(2,1)S(1)} %fusion.5), kind=kOutput, calls=%fused_computation.167 | convolution fusion | flops 805306368 | bytes 4194304 | tf_op jit(solution)/shard_map/dot_general | solution.py:20
  114.4 6.4 %fusion.64 = f32[512,3072]{1,0:T(8,128)} fusion(bf16[512,3072]{1,0:T(8,128)(2,1)S(1)} %copy-done, bf16[512,512]{1,0:T(8,128)(2,1)} %param.19, f32[512,512]{1,0:T(8,128)} %fusion.118), kind=kOutput, calls=%fused_computation.76 | convolution fusion | flops 1883766784 | bytes 11010048 | tf_op jit(solution)/shard_map/dot_general | solution.py:25
  120.8 5.8 %fusion.6 = (f32[512]{0:T(512)S(1)}, bf16[512,1536]{1,0:T(8,128)(2,1)}) fusion(f32[512,3072]{1,0:T(8,128)} %fusion.64, bf16[512,3072]{1,0:T(8,128)(2,1)} %copy-done.1), kind=kLoop, calls=%fused_computation.13 | loop fusion | flops 4718080 | bytes 9439232 | tf_op jit(solution)/shard_map/reduce_sum | solution.py:30
  126.5 5.4 %fusion.59 = f32[512]{0:T(512)S(1)} fusion(bf16[512,512]{1,0:T(8,128)(2,1)} %param.22, f32[512]{0:T(512)S(1)} %copy-done.21, bf16[512,3072]{1,0:T(8,128)(2,1)} %copy-done.1, bf16[3072,512]{1,0:T(8,128)(2,1)} %param.21), kind=kOutput, calls=%fused_computation.72 | convolution fusion | flops 1884028416 | bytes 6819840 | tf_op jit(solution)/shard_map/dot_general | solution.py:37
  132.0 5.5 %fusion.42 = f32[512]{0:T(512)S(1)} fusion(bf16[512,512]{1,0:T(8,128)(2,1)} %param.22, bf16[3072,512]{1,0:T(8,128)(2,1)} %param.21, bf16[512,1536]{1,0:T(8,128)(2,1)} %get-tuple-element.41, bf16[512,1536]{1,0:T(8,128)(2,1)} %slice.108, f32[512]{0:T(512)S(1)} %copy-done.21), kind=kOutput, calls=%fused_computation.55 | convolution fusion | flops 1890319872 | bytes 6819840 | tf_op jit(solution)/shard_map/dot_general | solution.py:37
  138.1 1.3 fusion.92
  139.4 2.0 %pad_maximum_fusion.17 = f32[128]{0:T(128)S(1)} fusion(f32[125]{0:T(128)S(1)} %broadcast_in_dim.276, f32[1]{0:T(128)} %bitcast.46, f32[1]{0:T(128)} %bitcast.45, f32[1]{0:T(128)} %bitcast.44), kind=kLoop, calls=%fused_computation.143 | loop fusion | flops 384 | bytes 1024 | tf_op jit(solution)/shard_map/concatenate | solution.py:152
  142.0 5.9 %all-to-all-start.3 = ((f32[32,1,128]{2,1,0:T(1,128)}), f32[32,1,128]{2,1,0:T(1,128)S(1)}, u32[]{:S(2)}, u32[]{:S(2)}) async-start(f32[32,1,128]{2,1,0:T(1,128)} %broadcast_in_dim.277), calls=%async_computation.3 | async-start | bytes 32768 | tf_op jit(solution)/shard_map/all_to_all | solution.py:50
  147.9 3.9 %fusion.8 = bf16[1,512,3072]{2,1,0:T(8,128)(2,1)} fusion(bf16[512,1536]{1,0:T(8,128)(2,1)} %get-tuple-element.41, bf16[512,1536]{1,0:T(8,128)(2,1)} %slice.108), kind=kLoop, calls=%fused_computation.15 | loop fusion | flops 6291456 | bytes 6291456 | tf_op jit(solution)/shard_map/reshape | solution.py:161
  151.8 5.9 %all-to-all-done.3 = f32[32,1,128]{2,1,0:T(1,128)S(1)} async-done(((f32[32,1,128]{2,1,0:T(1,128)}), f32[32,1,128]{2,1,0:T(1,128)S(1)}, u32[]{:S(2)}, u32[]{:S(2)}) %all-to-all-start.3) | async-done | bytes 16416 | tf_op jit(solution)/shard_map/all_to_all | solution.py:50
  158.3 0.9 slice_reduce_fusion
  (88 shorter events, 17.9 us)
Async XLA Ops:
  0.6 113.7 %copy-start = (bf16[512,3072]{1,0:T(8,128)(2,1)S(1)}, bf16[512,3072]{1,0:T(8,128)(2,1)}, u32[]{:S(2)}) copy-start(bf16[512,3072]{1,0:T(8,128)(2,1)} %param.20) | copy-start | bytes 9437188
  2.6 28.8 %copy-start.15 = (f32[8]{0:T(128)}, f32[8]{0:T(128)S(1)}, u32[]{:S(2)}) copy-start(f32[8]{0:T(128)S(1)} %log_bitcast_fusion) | copy-start | bytes 100
  10.3 21.1 %all-to-all-start = ((f32[32,1,128]{2,1,0:T(1,128)}), f32[32,1,128]{2,1,0:T(1,128)S(1)}, u32[]{:S(2)}, u32[]{:S(2)}) async-start(f32[32,1,128]{2,1,0:T(1,128)} %broadcast_in_dim.233), calls=%async_computation | async-start | bytes 32768 | tf_op jit(solution)/shard_map/all_to_all | solution.py:50
  31.4 5.1 %copy-start.4 = (f32[32,1,128]{2,1,0:T(1,128)}, f32[32,1,128]{2,1,0:T(1,128)S(1)}, u32[]{:S(2)}) copy-start(f32[32,1,128]{2,1,0:T(1,128)S(1)} %all-to-all-done) | copy-start | bytes 49156
  31.4 17.2 %all-to-all-start.1 = ((bf16[32,8,768]{2,1,0:T(8,128)(2,1)}), bf16[32,8,768]{2,1,0:T(8,128)(2,1)S(1)}, u32[]{:S(2)}, u32[]{:S(2)}) async-start(bf16[32,8,768]{2,1,0:T(8,128)(2,1)} %bitcast.20), calls=%async_computation.1 | async-start | bytes 786432 | tf_op jit(solution)/shard_map/all_to_all | solution.py:122
  39.6 17.3 %copy-start.18 = (s32[1,8]{1,0:T(1,128)S(1)}, s32[1,8]{1,0:T(1,128)}, u32[]{:S(2)}) copy-start(s32[1,8]{1,0:T(1,128)} %param.15) | copy-start | bytes 100
  39.6 28.9 %copy-start.16 = (pred[8]{0:T(512)(128)(4,1)S(1)}, pred[8]{0:T(512)(128)(4,1)}, u32[]{:S(2)}) copy-start(pred[8]{0:T(512)(128)(4,1)} %get-tuple-element.61) | copy-start | bytes 28
  39.6 31.2 %copy-start.10 = (s32[32]{0:T(128)}, s32[32]{0:T(128)S(1)}, u32[]{:S(2)}) copy-start(s32[32]{0:T(128)S(1)} %get-tuple-element.50) | copy-start | bytes 388
  39.6 31.2 %copy-start.11 = (s32[32]{0:T(128)}, s32[32]{0:T(128)S(1)}, u32[]{:S(2)}) copy-start(s32[32]{0:T(128)S(1)} %get-tuple-element.51) | copy-start | bytes 388
  50.5 18.0 %all-to-all-start.2 = ((bf16[32,8,768]{2,1,0:T(8,128)(2,1)}), bf16[32,8,768]{2,1,0:T(8,128)(2,1)S(1)}, u32[]{:S(2)}, u32[]{:S(2)}) async-start(bf16[32,8,768]{2,1,0:T(8,128)(2,1)} %bitcast.118), calls=%async_computation.2 | async-start | bytes 786432 | tf_op jit(solution)/shard_map/all_to_all | solution.py:129
  58.5 0.7 copy-start.19
  71.9 5.1 %collective-permute-start = (bf16[2,64,3072]{2,1,0:T(8,128)(2,1)}, bf16[2,64,3072]{2,1,0:T(8,128)(2,1)}, u32[]{:S(2)}, u32[]{:S(2)}) collective-permute-start(bf16[2,64,3072]{2,1,0:T(8,128)(2,1)} %pad_maximum_fusion.14), channel_id=1, source_target_pairs={{0,32},{32,0},{64,96},{96,64},{128,160},{160,128},{192,224},{224,1... | collective-permute-start | bytes 2359304 | tf_op jit(solution)/shard_map/ppermute | solution.py:69
  77.0 4.5 %copy-start.13 = (pred[8]{0:T(512)(128)(4,1)}, pred[8]{0:T(512)(128)(4,1)S(1)}, u32[]{:S(2)}) copy-start(pred[8]{0:T(512)(128)(4,1)S(1)} %get-tuple-element.55) | copy-start | bytes 28
  77.0 4.5 %copy-start.14 = (pred[8]{0:T(512)(128)(4,1)}, pred[8]{0:T(512)(128)(4,1)S(1)}, u32[]{:S(2)}) copy-start(pred[8]{0:T(512)(128)(4,1)S(1)} %get-tuple-element.54) | copy-start | bytes 28
  78.2 3.3 %copy-start.2 = (bf16[64,3072]{1,0:T(8,128)(2,1)}, bf16[64,3072]{1,0:T(8,128)(2,1)S(1)}, u32[]{:S(2)}) copy-start(bf16[64,3072]{1,0:T(8,128)(2,1)S(1)} %get-tuple-element.48) | copy-start | bytes 1179652
  78.2 3.3 %copy-start.3 = (bf16[64,3072]{1,0:T(8,128)(2,1)}, bf16[64,3072]{1,0:T(8,128)(2,1)S(1)}, u32[]{:S(2)}) copy-start(bf16[64,3072]{1,0:T(8,128)(2,1)S(1)} %get-tuple-element.49) | copy-start | bytes 1179652
  81.5 3.7 %copy-start.17 = (pred[8]{0:T(512)(128)(4,1)S(1)}, pred[8]{0:T(512)(128)(4,1)}, u32[]{:S(2)}) copy-start(pred[8]{0:T(512)(128)(4,1)} %get-tuple-element.61) | copy-start | bytes 28
  81.5 23.4 %copy-start.5 = (f32[32,1,128]{2,1,0:T(1,128)S(1)}, f32[32,1,128]{2,1,0:T(1,128)}, u32[]{:S(2)}) copy-start(f32[32,1,128]{2,1,0:T(1,128)} %copy-done.4) | copy-start | bytes 49156
  82.6 22.6 %collective-permute-start.1 = (bf16[2,64,3072]{2,1,0:T(8,128)(2,1)}, bf16[2,64,3072]{2,1,0:T(8,128)(2,1)}, u32[]{:S(2)}, u32[]{:S(2)}) collective-permute-start(bf16[2,64,3072]{2,1,0:T(8,128)(2,1)} %pad_maximum_fusion.15), channel_id=1, source_target_pairs={{32,64},{64,32},{96,128},{128,96},{160,192},{192,160},{33,65},{65,... | collective-permute-start | bytes 2359304 | tf_op jit(solution)/shard_map/ppermute | solution.py:69
  109.7 2.2 %copy-start.1 = (bf16[512,3072]{1,0:T(8,128)(2,1)}, bf16[512,3072]{1,0:T(8,128)(2,1)S(1)}, u32[]{:S(2)}) copy-start(bf16[512,3072]{1,0:T(8,128)(2,1)S(1)} %fusion.5) | copy-start | bytes 9437188
  109.7 2.6 %copy-start.20 = (bf16[1536,512]{1,0:T(8,128)(2,1)S(1)}, bf16[1536,512]{1,0:T(8,128)(2,1)}, u32[]{:S(2)}) copy-start(bf16[1536,512]{1,0:T(8,128)(2,1)} %param.18) | copy-start | bytes 4718596
  120.8 5.8 %copy-start.21 = (f32[512]{0:T(512)S(1)}, f32[512]{0:T(512)}, u32[]{:S(2)}) copy-start(f32[512]{0:T(512)} %param.23) | copy-start | bytes 6148
  132.0 5.5 %copy-start.6 = (f32[1,512]{1,0:T(1,128)S(1)}, f32[1,512]{1,0:T(1,128)}, u32[]{:S(2)}) copy-start(f32[1,512]{1,0:T(1,128)} %param.13) | copy-start | bytes 6148
  132.0 5.5 %copy-start.7 = (f32[512]{0:T(512)S(1)}, f32[512]{0:T(512)}, u32[]{:S(2)}) copy-start(f32[512]{0:T(512)} %sub.129) | copy-start | bytes 6148
  132.0 5.5 %copy-start.12 = (pred[512]{0:T(512)(128)(4,1)S(1)}, pred[512]{0:T(512)(128)(4,1)}, u32[]{:S(2)}) copy-start(pred[512]{0:T(512)(128)(4,1)} %broadcast_in_dim.266) | copy-start | bytes 1540
  142.0 15.7 %all-to-all-start.3 = ((f32[32,1,128]{2,1,0:T(1,128)}), f32[32,1,128]{2,1,0:T(1,128)S(1)}, u32[]{:S(2)}, u32[]{:S(2)}) async-start(f32[32,1,128]{2,1,0:T(1,128)} %broadcast_in_dim.277), calls=%async_computation.3 | async-start | bytes 32768 | tf_op jit(solution)/shard_map/all_to_all | solution.py:50
  147.9 14.0 %copy-start.8 = (f32[1,512]{1,0:T(1,128)S(1)}, f32[1,512]{1,0:T(1,128)}, u32[]{:S(2)}) copy-start(f32[1,512]{1,0:T(1,128)} %sub.125) | copy-start | bytes 6148
  147.9 14.0 %copy-start.9 = (pred[1,512]{1,0:T(4,128)(4,1)S(1)}, pred[1,512]{1,0:T(4,128)(4,1)}, u32[]{:S(2)}) copy-start(pred[1,512]{1,0:T(4,128)(4,1)} %broadcast_in_dim.269) | copy-start | bytes 1540

commit v2 on v1

v2 whole, which is shorter than its diff:
```python
import functools

import jax
import jax.numpy as jnp
from jax import lax
from jax.experimental import pallas as pl
from jax.experimental.pallas import tpu as pltpu
from jax.sharding import PartitionSpec as P

SWAPS = 2
TILE = 8
LANES = 128

old_level = 0.5
new_level = 0.75
scale_limit = 0.05

F32 = jnp.float32
BF16 = jnp.bfloat16
SMEM = pl.BlockSpec(memory_space=pltpu.SMEM)
VMEM = pl.BlockSpec(memory_space=pltpu.VMEM)
ANY = pl.BlockSpec(memory_space=pl.ANY)


def gelu(x):
    return x * (0.5 * (1.0 + jnp.tanh(0.7978845608028654 * (x + 0.044715 * (x * x * x)))))


def inside(x):
    return pltpu.with_memory_space_constraint(x, pltpu.VMEM)


def mul(a, b):
    return jnp.dot(a, b, preferred_element_type=F32)


def find(flags, value):
    slot = jnp.int32(-1)
    for b in range(flags.shape[1]):
        slot = jnp.where(flags[0, b] == value, b, slot)
    return slot


def find_two(flags):
    count = flags.shape[1]
    first, second = jnp.int32(count), jnp.int32(count)
    for b in reversed(range(count)):
        hit = flags[0, b] == 1
        second = jnp.where(hit, first, second)
        first = jnp.where(hit, b, first)
    return first, second


def spread(flags, width):
    count = flags.shape[1]
    slot = lax.broadcasted_iota(jnp.int32, (1, width), 1) // (width // count)
    row = jnp.zeros((1, width), jnp.int32)
    for b in range(count):
        row = jnp.where(slot == b, flags[0, b], row)
    return row


def step_rows(rows, weights, read_out, ready, keep, chunk):
    flow_in, flow_mid, flow_out, energy_in, energy_mid = weights
    half = rows.shape[1] // 2
    kept = rows[:, :half]
    ready(0)
    hidden = gelu(mul(kept, flow_in[...])).astype(BF16)
    ready(1)
    hidden = gelu(mul(hidden, flow_mid[...])).astype(BF16)
    ready(2)
    log_det = jnp.zeros((rows.shape[0], 1), F32)
    parts = []
    for at in range(0, half, chunk):
        log_scale = scale_limit * jnp.tanh(mul(hidden, flow_out[:, at : at + chunk]))
        shift = mul(hidden, flow_out[:, half + at : half + at + chunk])
        log_det += jnp.sum(log_scale, axis=1, keepdims=True)
        moved = rows[:, half + at : half + at + chunk].astype(F32)
        moved = (moved * jnp.exp(log_scale) + shift).astype(BF16)
        keep(half + at, moved)
        parts.append(moved)
    ready(3)
    base = mul(kept, energy_in[:half, :])
    before = base + mul(rows[:, half:], energy_in[half:, :])
    after = base + mul(jnp.concatenate(parts, axis=1), energy_in[half:, :])
    ready(4)
    levels = []
    for value in (before, after):
        unit = gelu(mul(gelu(value).astype(BF16), energy_mid[...]))
        levels.append(jnp.sum(unit * read_out, axis=1, keepdims=True))
    return log_det, new_level * levels[1] - old_level * levels[0]


def fetches(sources, targets, sems):
    return [
        pltpu.make_async_copy(source, target, sems.at[i])
        for i, (source, target) in enumerate(zip(sources, targets, strict=True))
    ]


def split(value, terms):
    parts = []
    for _ in range(terms):
        part = value.astype(BF16).astype(F32)
        parts.append(part)
        value = value - part
    return parts


def spare_kernel(
    counts, log_weights, read_out, particles, w0, w1, w2, w3, w4, out, rows, s0, s1, s2, s3, s4, sems, row_sem
):
    scratch = (s0, s1, s2, s3, s4)
    copies = fetches((w0, w1, w2, w3, w4), scratch, sems)
    block_rows = rows.shape[0]
    spare, vacant = find(counts, 2), find(counts, 0)
    slot = jnp.maximum(spare, 0)
    own = pltpu.make_async_copy(
        particles.at[pl.ds(pl.multiple_of(slot * block_rows, block_rows), block_rows), :], rows, row_sem
    )
    own.start()
    for copy in copies:
        copy.start()
    own.wait()
    width = rows.shape[1] // 4

    def keep(at, moved):
        done = 0
        while done < moved.shape[1]:
            c, start = divmod(at + done, width)
            size = min(moved.shape[1] - done, width - start)
            out[c * block_rows : (c + 1) * block_rows, start : start + size] = moved[:, done : done + size]
            done += size

    log_det, level = step_rows(
        rows, scratch, read_out[...], lambda i: copies[i].wait(), keep, width
    )
    for c in range(2):
        out[c * block_rows : (c + 1) * block_rows, :width] = rows[:, c * width : (c + 1) * width]
    lane = lax.broadcasted_iota(jnp.int32, (block_rows, LANES), 1)
    table = jnp.where(lane == 0, log_det, jnp.where(lane == 1, level, 0.0))
    table = jnp.concatenate([table] * (LANES // block_rows), axis=0).T
    weight = jnp.zeros((1, LANES), F32)
    for j in range(log_weights.shape[1] // LANES):
        weight = jnp.where(slot // 2 == j, log_weights[:, j * LANES : (j + 1) * LANES], weight)
    weight = jnp.where(slot % 2 == 0, weight, pltpu.roll(weight, LANES // 2, 1))
    weight = weight - jnp.log(jnp.full((1, LANES), 2.0, F32))
    terms = split(weight, 3) + split(table[0:1, :], 2) + split(table[1:2, :], 3)
    row = lax.broadcasted_iota(jnp.int32, (TILE, LANES), 0)
    lane = lax.broadcasted_iota(jnp.int32, (TILE, LANES), 1)
    extra = jnp.zeros((TILE, LANES), F32)
    for i, term in enumerate(terms):
        extra = jnp.where(row == i, term, extra)
    flag = jnp.where(lane < 96, (spare >= 0).astype(F32), (vacant >= 0).astype(F32))
    extra = jnp.where(lane < LANES // 2, extra, flag)
    out[:, width:] = jnp.concatenate([extra] * (out.shape[0] // TILE), axis=0).astype(BF16)


def rows_kernel(
    read_out, rows, w0, w1, w2, w3, w4, out, scalars, s0, s1, s2, s3, s4, sems
):
    scratch = (s0, s1, s2, s3, s4)
    copies = fetches((w0, w1, w2, w3, w4), scratch, sems)
    first = pl.program_id(0) == 0

    @pl.when(first)
    def _():
        for copy in copies:
            copy.start()

    def ready(i):
        @pl.when(first)
        def _():
            copies[i].wait()

    def keep(at, moved):
        out[:, at : at + moved.shape[1]] = moved

    half = rows.shape[1] // 2
    out[:, :half] = rows[:, :half]
    log_det, level = step_rows(rows, scratch, read_out[...], ready, keep, 512)
    lane = lax.broadcasted_iota(jnp.int32, (rows.shape[0], LANES), 1)
    table = jnp.where(lane == 0, log_det, jnp.where(lane == 1, level, 0.0)).T
    scalars[...] = table[:TILE, :]


def route_kernel(me, counts, log_weights, held, scalars, out, mine, tags):
    size = held.shape[0]
    width = out.shape[1]
    tag = held[:, width:]
    flags = tag.astype(F32)
    turned = flags.T
    half, late = LANES // 2, 96
    spare_col, vacant_col = flags[:, half : half + 1], flags[:, late : late + 1]
    spare_row, vacant_row = turned[half : half + 1, :], turned[late : late + 1, :]
    to = lax.broadcasted_iota(jnp.int32, (size, size), 0)
    source = lax.broadcasted_iota(jnp.int32, (size, size), 1)
    to_dev, source_dev = to // TILE, source // TILE
    vacant_rank = jnp.sum(jnp.where(source_dev < to_dev, vacant_row, 0.0), axis=1, keepdims=True)
    spare_rank = jnp.sum(jnp.where(to_dev < source_dev, spare_col, 0.0), axis=0, keepdims=True)
    hit = (vacant_rank == spare_rank) & (to % TILE == source % TILE)
    hit = hit & (vacant_col > 0.5) & (spare_row > 0.5)
    pick = jnp.where(hit, 1.0, 0.0).astype(BF16)
    out[...] = mul(pick, held[:, :width]).astype(BF16)
    tags[...] = mul(pick, tag)
    got = tags[pl.ds(pl.multiple_of(me[0] * TILE, TILE), TILE), :]
    total = log_weights.shape[1]

    def lay(value):
        lane = lax.broadcasted_iota(jnp.int32, (1, LANES), 1)
        value = jnp.where(lane < half, value, pltpu.roll(value, half, 1))
        return jnp.concatenate([value] * (total // LANES), axis=1)

    count = spread(counts, total)
    vacant = count == 0
    weight = log_weights[...] - jnp.log(jnp.maximum(count, 1).astype(F32))
    weight = jnp.where(vacant, lay(got[0:1] + got[1:2] + got[2:3]), weight)
    log_det = jnp.where(vacant, lay(got[3:4] + got[4:5]), scalars[0:1, :])
    level = jnp.where(vacant, lay(got[5:6] + got[6:7] + got[7:8]), scalars[1:2, :])
    row = lax.broadcasted_iota(jnp.int32, (TILE, total), 0)
    mine[...] = jnp.where(row == 0, log_det, jnp.where(row == 1, level, jnp.where(row == 2, weight, 0.0)))


def mix_kernel(flags, own, other, out):
    total = own.shape[1]
    take = spread(flags, total) == 1
    row = lax.broadcasted_iota(jnp.int32, own.shape, 0)
    out[...] = jnp.where(take & (row < 2), other[...], own[...])


def stats_kernel(flags, inverse_temp, own, other, updated, stats):
    take = spread(flags, own.shape[1]) == 1
    log_det = jnp.where(take, other[0:1, :], own[0:1, :])
    level = jnp.where(take, other[1:2, :], own[1:2, :])
    new = own[2:3, :] + log_det - inverse_temp[0] * level
    updated[...] = new
    peak = jnp.max(new, axis=1, keepdims=True)
    shifted = jnp.exp(new - peak)
    one = jnp.sum(shifted, axis=1, keepdims=True)
    two = jnp.sum(shifted * shifted, axis=1, keepdims=True)
    lane = lax.broadcasted_iota(jnp.int32, stats.shape, 1)
    stats[...] = jnp.where(lane == 0, peak, jnp.where(lane == 1, one, two))


def final_kernel(particle_total, updated, stats, new_weights, ess):
    table = stats[...]
    peaks = table[:, 0:1]
    peak = jnp.max(peaks, axis=0, keepdims=True)
    factor = jnp.exp(peaks - peak)
    one = jnp.sum(table[:, 1:2] * factor, axis=0, keepdims=True) * (1.0 / TILE)
    two = jnp.sum(table[:, 2:3] * factor * factor, axis=0, keepdims=True) * (1.0 / TILE)
    log_one = jnp.log(one)
    new_weights[...] = updated[...] - (peak + log_one)
    count = jnp.log(jnp.full((1, 1), particle_total, F32))
    ess[0] = jnp.max(2.0 * log_one - jnp.log(two) - count)


def at_slot(ref, slot, block_rows):
    return ref.at[pl.ds(pl.multiple_of(slot * block_rows, block_rows), block_rows), :]


def run(copies):
    for go, copy in copies:

        @pl.when(go)
        def _():
            copy.start()

    for go, copy in copies:

        @pl.when(go)
        def _():
            copy.wait()


def fill_kernel(counts, pairs, rows_in, pieces, later, rows, packed, sems):
    del rows_in, later
    block_rows = packed.shape[0] // SWAPS
    width = pieces.shape[1]
    slots = counts.shape[1]
    vacant = find(counts, 0)
    target = at_slot(rows, jnp.maximum(vacant, 0), block_rows)
    copies = []
    for c in range(4):
        source = pieces.at[c * block_rows : (c + 1) * block_rows, :]
        to = target.at[:, c * width : (c + 1) * width]
        copies.append((vacant >= 0, pltpu.make_async_copy(source, to, sems.at[c])))
    for i, slot in enumerate(find_two(pairs)):
        part = slice(i * block_rows, (i + 1) * block_rows)
        source = at_slot(rows, jnp.minimum(slot, slots - 1), block_rows)
        go = (slot < slots) & (slot != vacant)
        copies.append((go, pltpu.make_async_copy(source, packed.at[part, :], sems.at[4 + i])))

        @pl.when(slot == vacant)
        def _():
            for c in range(4):
                packed[part, c * width : (c + 1) * width] = pieces[c * block_rows : (c + 1) * block_rows, :]

    run(copies)


def swap_kernel(flags, next_flags, rows_in, received, rows, packed, sems):
    del rows_in
    block_rows = received.shape[0] // SWAPS
    slots = flags.shape[1]
    chosen = find_two(flags)
    parts = [slice(i * block_rows, (i + 1) * block_rows) for i in range(SWAPS)]
    copies = []
    for i, slot in enumerate(chosen):
        to = at_slot(rows, jnp.minimum(slot, slots - 1), block_rows)
        copies.append((slot < slots, pltpu.make_async_copy(received.at[parts[i], :], to, sems.at[i])))
    for i, slot in enumerate(find_two(next_flags)):
        source = at_slot(rows, jnp.minimum(slot, slots - 1), block_rows)
        go = (slot < slots) & (slot != chosen[0]) & (slot != chosen[1])
        copies.append((go, pltpu.make_async_copy(source, packed.at[parts[i], :], sems.at[SWAPS + i])))
        for j in range(SWAPS):

            @pl.when((slot < slots) & (slot == chosen[j]))
            def _():
                packed[parts[i], :] = received[parts[j], :]

    run(copies)


def last_kernel(flags, rows_in, received, rows, sems):
    del rows_in
    block_rows = received.shape[0] // SWAPS
    slots = flags.shape[1]
    copies = []
    for i, slot in enumerate(find_two(flags)):
        source = received.at[i * block_rows : (i + 1) * block_rows, :]
        to = at_slot(rows, jnp.minimum(slot, slots - 1), block_rows)
        copies.append((slot < slots, pltpu.make_async_copy(source, to, sems.at[i])))
    run(copies)


def per_device(
    particles,
    log_weights,
    offspring,
    even_pairs,
    odd_pairs,
    inverse_temp,
    flow_in,
    flow_mid,
    flow_out,
    energy_in,
    energy_mid,
    energy_out,
):
    block_count = offspring.shape[1]
    total, features = particles.shape[1:]
    block_rows = total // block_count
    hidden = flow_mid.shape[0]
    dom_count = lax.axis_size("dom")
    groups = lax.axis_size("temp")
    width = features // 4
    rows = particles.reshape(total, features)
    weights = (flow_in, flow_mid, flow_out, energy_in, energy_mid)
    read_out = energy_out.reshape(1, hidden)
    held_rows = dom_count * TILE
    weight_scratch = [pltpu.VMEM(w.shape, w.dtype) for w in weights]
    shape = jax.ShapeDtypeStruct
    weight_bytes = sum(2 * w.size for w in weights)

    def cost(count):
        flops = 2 * count * (sum(w.size for w in weights) + energy_in.size // 2)
        return pl.CostEstimate(
            flops=flops, transcendentals=count * features * 2, bytes_accessed=weight_bytes
        )

    pieces = pl.pallas_call(
        spare_kernel,
        out_shape=shape((held_rows, width + LANES), BF16),
        in_specs=[SMEM, VMEM, VMEM, ANY] + [ANY] * 5,
        out_specs=VMEM,
        scratch_shapes=[pltpu.VMEM((block_rows, features), BF16)]
        + weight_scratch
        + [pltpu.SemaphoreType.DMA((5,)), pltpu.SemaphoreType.DMA(())],
        cost_estimate=cost(block_rows),
        name="spare",
    )(offspring, log_weights, read_out, rows, *weights)

    def exchange(x):
        cut = x.reshape(dom_count, TILE, x.shape[1])
        return lax.all_to_all(cut, "dom", 0, 0, tiled=True).reshape(x.shape)

    held = exchange(pieces)
    step = total // 2
    done, scalars = pl.pallas_call(
        rows_kernel,
        out_shape=(shape((total, features), BF16), shape((TILE, total), F32)),
        grid=(2,),
        in_specs=[
            pl.BlockSpec((1, hidden), lambda i: (0, 0)),
            pl.BlockSpec((step, features), lambda i: (i, 0)),
        ]
        + [ANY] * 5,
        out_specs=(
            pl.BlockSpec((step, features), lambda i: (i, 0)),
            pl.BlockSpec((TILE, step), lambda i: (0, i)),
        ),
        scratch_shapes=weight_scratch + [pltpu.SemaphoreType.DMA((5,))],
        cost_estimate=cost(total),
        name="rows",
    )(read_out, rows, *weights)

    me = lax.axis_index("dom").astype(jnp.int32).reshape(1)
    routed, mine = pl.pallas_call(
        route_kernel,
        out_shape=(shape((held_rows, width), BF16), shape((TILE, total), F32)),
        in_specs=[SMEM, SMEM, VMEM, VMEM, VMEM],
        out_specs=(VMEM, VMEM),
        scratch_shapes=[pltpu.VMEM((held_rows, LANES), F32)],
        name="route",
    )(me, offspring, log_weights, inside(held), inside(scalars))
    filled = exchange(routed)

    even = [(i, i + 1 - 2 * (i % 2)) for i in range(groups)]
    odd = [(i, i - 1 + 2 * (i % 2)) for i in range(1, groups - 1)]
    other = lax.ppermute(mine, "temp", even)
    mixed = pl.pallas_call(
        mix_kernel,
        out_shape=shape((TILE, total), F32),
        in_specs=[SMEM, VMEM, VMEM],
        out_specs=VMEM,
        name="mix",
    )(even_pairs, mine, inside(other))
    other = lax.ppermute(mixed, "temp", odd)
    updated, stats = pl.pallas_call(
        stats_kernel,
        out_shape=(shape((1, total), F32), shape((held_rows, LANES), F32)),
        in_specs=[SMEM, SMEM, VMEM, VMEM],
        out_specs=(VMEM, VMEM),
        name="stats",
    )(odd_pairs, inverse_temp, mixed, inside(other))
    stats = exchange(stats)
    new_log_weights, log_ess = pl.pallas_call(
        functools.partial(final_kernel, float(total * dom_count)),
        out_shape=(shape((1, total), F32), shape((1,), F32)),
        in_specs=[VMEM, VMEM],
        out_specs=(VMEM, SMEM),
        name="final",
    )(updated, inside(stats))

    whole = shape((total, features), BF16)
    pack = shape((SWAPS * block_rows, features), BF16)
    done, packed = pl.pallas_call(
        fill_kernel,
        out_shape=(whole, pack),
        in_specs=[SMEM, SMEM, ANY, VMEM, ANY],
        out_specs=(ANY, VMEM),
        scratch_shapes=[pltpu.SemaphoreType.DMA((4 + SWAPS,))],
        input_output_aliases={2: 0},
        name="fill",
    )(offspring, even_pairs, done, inside(filled), updated)
    received = lax.ppermute(packed, "temp", even)
    done, packed = pl.pallas_call(
        swap_kernel,
        out_shape=(whole, pack),
        in_specs=[SMEM, SMEM, ANY, VMEM],
        out_specs=(ANY, VMEM),
        scratch_shapes=[pltpu.SemaphoreType.DMA((2 * SWAPS,))],
        input_output_aliases={2: 0},
        name="even",
    )(even_pairs, odd_pairs, done, inside(received))
    received = lax.ppermute(packed, "temp", odd)
    done = pl.pallas_call(
        last_kernel,
        out_shape=whole,
        in_specs=[SMEM, ANY, VMEM],
        out_specs=ANY,
        scratch_shapes=[pltpu.SemaphoreType.DMA((SWAPS,))],
        input_output_aliases={1: 0},
        name="odd",
    )(odd_pairs, done, inside(received))
    return done.reshape(1, total, features), new_log_weights, log_ess


def solution(mesh):
    in_specs = (
        P("temp", "dom", None),
        P("temp", "dom"),
        P("temp", "dom"),
        P("temp", "dom"),
        P("temp", "dom"),
        P("temp"),
        P(),
        P(),
        P(),
        P(),
        P(),
        P(),
    )
    out_specs = (P("temp", "dom", None), P("temp", "dom"), P("temp"))
    return jax.shard_map(
        per_device, mesh=mesh, in_specs=in_specs, out_specs=out_specs, check_vma=False
    )
```

time: 166 us -> 90.3 us (0.54)
  other arithmetic: 46.7 us -> 0 us
  Pallas kernels: 0 us -> 34.1 us
  local copies, waits for them, and re-layouts: 26.9 us -> 0.72 us
  matrix products: 20.3 us -> 0 us
  blocking collectives: 0 us -> 16.9 us
  between operations: 14.6 us -> 1.39 us
  waiting for transfers between devices: 26.1 us -> 13.4 us
  starting transfers between devices: 28.9 us -> 22.8 us
    pallas_call x0 -> x9, Pallas kernels: none -> 34.1 us  [the longest x1 12.5 us: per_device(): pl.pallas_call(rows_kernel, out_shape=(shape((total, features), BF16), sh...]
    dot_general x5 -> x0, matrix products: 20.3 us -> none  [the longest x2 10.9 us: energy(): jnp.dot(layer_one, energy_mid, preferred_element_type=jnp.float32)]
    all_to_all x4 -> x2, waiting for transfers between devices: 26.1 us -> 7.02 us  [exchange(): return lax.all_to_all(cut, 'dom', 0, 0, tiled=True).reshape(x.shape)]
    all_to_all x0 -> x1, blocking collectives: none -> 16.9 us  [exchange(): return lax.all_to_all(cut, 'dom', 0, 0, tiled=True).reshape(x.shape)]
    broadcast_in_dim x21 -> x0, local copies, waits for them, and re-layouts: 16.8 us -> none  [the longest x10 12.1 us: neighbour_swap(): blocks = jnp.where(hit[:, None, None], received[i][None], blocks)]
    select_n x6 -> x0, other arithmetic: 11.4 us -> none  [the longest x2 6.61 us: neighbour_swap(): blocks = jnp.where(hit[:, None, None], received[i][None], blocks)]
    reduce_sum x7 -> x0, other arithmetic: 10.9 us -> none  [the longest x1 5.77 us: transport(): jnp.sum(log_scale, axis=1)]
    all_to_all x4 -> x2, starting transfers between devices: 26.3 us -> 18.3 us  [exchange(): return lax.all_to_all(cut, 'dom', 0, 0, tiled=True).reshape(x.shape)]
  transfers between devices with their start and end apart: 6 -> 6, of which waited for: 4 -> 5; matrix products, arithmetic and copies ran while one was open for 22% -> 0% of each run, Pallas kernels for 0% -> 19%
where the time goes in v2:
time: 90.3 us; the launch traced here: 89.3 us
  Pallas kernels  34.1 us (38%)
  starting transfers between devices  22.8 us (25%)
  blocking collectives  16.9 us (19%)
  waiting for transfers between devices  13.4 us (15%)
  between operations  1.39 us (2%)
    all_to_all x2, starting transfers between devices, exchange(): return lax.all_to_all(cut, 'dom', 0, 0, tiled=True).reshape(x.shape)  18.3 us
    all_to_all x1, blocking collectives, exchange(): return lax.all_to_all(cut, 'dom', 0, 0, tiled=True).reshape(x.shape)  16.9 us
    pallas_call x1, Pallas kernels, per_device(): pl.pallas_call(rows_kernel, out_shape=(shape((total, features), BF16), sh...  12.5 us
    pallas_call x1, Pallas kernels, per_device(): pl.pallas_call(spare_kernel, out_shape=shape((held_rows, width + LANES),...  7.9 us
    all_to_all x2, waiting for transfers between devices, exchange(): return lax.all_to_all(cut, 'dom', 0, 0, tiled=True).reshape(x.shape)  7.02 us
    pallas_call x1, Pallas kernels, per_device(): pl.pallas_call(swap_kernel, out_shape=(whole, pack), in_specs=[SMEM, SMEM...  2.92 us
    pallas_call x1, Pallas kernels, per_device(): pl.pallas_call(fill_kernel, out_shape=(whole, pack), in_specs=[SMEM, SMEM...  2.8 us
    ppermute x1, waiting for transfers between devices, per_device(): received = lax.ppermute(packed, 'temp', even)  2.48 us
  transfers between devices with their start and end apart: 6, of which 5 were waited for; matrix products, arithmetic and copies ran while one was open for 0% of the time, Pallas kernels for 19%

profile of v2, /device:TPU:16, one launch (start us, length us, event | category | flops | bytes accessed | tf_op | source)
XLA Modules:
  0.0 89.3 jit_solution(11133748283622577229)
XLA Ops:
  0.6 7.9 %spare.1 = bf16[256,896]{1,0:T(8,128)(2,1)} custom-call(s32[1,8]{1,0:T(1,128)} %counts.5, f32[1,512]{1,0:T(1,128)} %log_weights.3, f32[1,512]{1,0:T(1,128)} %bitcast.19, bf16[512,3072]{1,0:T(8,128)(2,1)} %bitcast.14, bf16[1536,512]{1,0:T(8,128)(2,1)} %w0.3, bf16[512,512]{1,0:T(8,128)(2,1)} %w1.3, bf16[512,3072]{1,0:T(8,128)(2,1)} %w2.3, ...), custom_call_target="tpu_custom_call" | custom-call | flops 671088640 | bytes 8912896 | tf_op jit(solution)/shard_map/spare/pallas_call | solution.py:372
  8.5 11.3 %all-to-all-start = ((bf16[32,8,896]{2,1,0:T(8,128)(2,1)}), bf16[32,8,896]{2,1,0:T(8,128)(2,1)S(1)}, u32[]{:S(2)}, u32[]{:S(2)}) async-start(bf16[32,8,896]{2,1,0:T(8,128)(2,1)} %bitcast.16), calls=%async_computation | async-start | bytes 917504 | tf_op jit(solution)/shard_map/all_to_all | solution.py:386
  19.9 12.5 %rows.1 = (bf16[512,3072]{1,0:T(8,128)(2,1)}, f32[8,512]{1,0:T(8,128)}) custom-call(f32[1,512]{1,0:T(1,128)} %bitcast.20, bf16[512,3072]{1,0:T(8,128)(2,1)} %bitcast.15, bf16[1536,512]{1,0:T(8,128)(2,1)} %w0.3, bf16[512,512]{1,0:T(8,128)(2,1)} %w1.3, bf16[512,3072]{1,0:T(8,128)(2,1)} %w2.3, bf16[3072,512]{1,0:T(8,128)(2,1)} %w3.3, bf16[512,512]{1,0:T(8,128)(2,1)} %w4.3), custom_call_target="tpu_custom_call" | custom-call | flops 5368709120 | bytes 8912896 | tf_op jit(solution)/shard_map/rows/pallas_call | solution.py:390
  32.4 2.8 %all-to-all-done = bf16[32,8,896]{2,1,0:T(8,128)(2,1)S(1)} async-done(((bf16[32,8,896]{2,1,0:T(8,128)(2,1)}), bf16[32,8,896]{2,1,0:T(8,128)(2,1)S(1)}, u32[]{:S(2)}, u32[]{:S(2)}) %all-to-all-start) | async-done | bytes 458784 | tf_op jit(solution)/shard_map/all_to_all | solution.py:386
  35.2 0.0 copy-start
  35.2 0.7 copy-done
  35.9 1.9 %route.1 = (bf16[256,768]{1,0:T(8,128)(2,1)}, f32[8,512]{1,0:T(8,128)}) custom-call(s32[1]{0:T(128)} %bitcast.2.me, s32[1,8]{1,0:T(1,128)} %counts.5, f32[1,512]{1,0:T(1,128)} %log_weights.3, bf16[256,896]{1,0:T(8,128)(2,1)S(1)} %bitcast.10, f32[8,512]{1,0:T(8,128)S(1)} %copy-done), custom_call_target="tpu_custom_call" | custom-call | tf_op jit(solution)/shard_map/route/pallas_call | solution.py:409
  37.8 7.0 %all-to-all-start.1 = ((bf16[32,8,768]{2,1,0:T(8,128)(2,1)}), bf16[32,8,768]{2,1,0:T(8,128)(2,1)S(1)}, u32[]{:S(2)}, u32[]{:S(2)}) async-start(bf16[32,8,768]{2,1,0:T(8,128)(2,1)} %bitcast.17), calls=%async_computation.1 | async-start | bytes 786432 | tf_op jit(solution)/shard_map/all_to_all | solution.py:386
  44.9 0.1 collective-permute-start
  45.0 1.4 %collective-permute-done.other = f32[8,512]{1,0:T(8,128)S(1)} collective-permute-done((f32[8,512]{1,0:T(8,128)}, f32[8,512]{1,0:T(8,128)S(1)}, u32[]{:S(2)}, u32[]{:S(2)}) %collective-permute-start) | collective-permute-done | bytes 16416 | tf_op jit(solution)/shard_map/ppermute | solution.py:421
  46.3 1.3 %mix.1.own = f32[8,512]{1,0:T(8,128)} custom-call(s32[1,8]{1,0:T(1,128)} %flags.6, f32[8,512]{1,0:T(8,128)} %get-tuple-element.18.own, f32[8,512]{1,0:T(8,128)S(1)} %collective-permute-done.other), custom_call_target="tpu_custom_call" | custom-call | tf_op jit(solution)/shard_map/mix/pallas_call | solution.py:422
  47.7 2.1 %collective-permute-start.1 = (f32[8,512]{1,0:T(8,128)}, f32[8,512]{1,0:T(8,128)S(1)}, u32[]{:S(2)}, u32[]{:S(2)}) collective-permute-start(f32[8,512]{1,0:T(8,128)} %mix.1.own), channel_id=1, source_target_pairs={{32,64},{64,32},{96,128},{128,96},{160,192},{192,160},{33,65},{65,... | collective-permute-start | bytes 49160 | tf_op jit(solution)/shard_map/ppermute | solution.py:429
  50.5 2.5 %collective-permute-done.1.other = f32[8,512]{1,0:T(8,128)S(1)} collective-permute-done((f32[8,512]{1,0:T(8,128)}, f32[8,512]{1,0:T(8,128)S(1)}, u32[]{:S(2)}, u32[]{:S(2)}) %collective-permute-start.1) | collective-permute-done | bytes 16416 | tf_op jit(solution)/shard_map/ppermute | solution.py:429
  52.9 1.6 %stats.1 = (f32[1,512]{1,0:T(1,128)}, f32[256,128]{1,0:T(8,128)}) custom-call(s32[1,8]{1,0:T(1,128)} %flags.7, f32[1]{0:T(128)S(6)} %copy.21.inverse_temp, f32[8,512]{1,0:T(8,128)} %mix.1.own, f32[8,512]{1,0:T(8,128)S(1)} %collective-permute-done.1.other), custom_call_target="tpu_custom_call" | custom-call | tf_op jit(solution)/shard_map/stats/pallas_call | solution.py:430
  54.5 4.2 %all-to-all-done.1 = bf16[32,8,768]{2,1,0:T(8,128)(2,1)S(1)} async-done(((bf16[32,8,768]{2,1,0:T(8,128)(2,1)}), bf16[32,8,768]{2,1,0:T(8,128)(2,1)S(1)}, u32[]{:S(2)}, u32[]{:S(2)}) %all-to-all-start.1) | async-done | bytes 393248 | tf_op jit(solution)/shard_map/all_to_all | solution.py:386
  58.7 0.0 copy-start.1
  58.7 2.8 %fill.1 = (bf16[512,3072]{1,0:T(8,128)(2,1)}, bf16[128,3072]{1,0:T(8,128)(2,1)}) custom-call(s32[1,8]{1,0:T(1,128)} %counts.5, s32[1,8]{1,0:T(1,128)} %flags.6, bf16[512,3072]{1,0:T(8,128)(2,1)} %get-tuple-element.15.rows_in, bf16[256,768]{1,0:T(8,128)(2,1)S(1)} %bitcast.11, f32[1,512]{1,0:T(1,128)} %get-tuple-element.19.later.updated), custom_call_target="tpu_custom_call", output_to_operand_aliasing={{0}: (2, {})} | custom-call | tf_op jit(solution)/shard_map/fill/pallas_call | solution.py:448
  61.6 0.1 collective-permute-start.2
  61.7 2.5 %collective-permute-done.2.received = bf16[128,3072]{1,0:T(8,128)(2,1)S(1)} collective-permute-done((bf16[128,3072]{1,0:T(8,128)(2,1)}, bf16[128,3072]{1,0:T(8,128)(2,1)S(1)}, u32[]{:S(2)}, u32[]{:S(2)}) %collective-permute-start.2) | collective-permute-done | bytes 786464 | tf_op jit(solution)/shard_map/ppermute | solution.py:457
  64.1 2.9 %even.1 = (bf16[512,3072]{1,0:T(8,128)(2,1)}, bf16[128,3072]{1,0:T(8,128)(2,1)}) custom-call(s32[1,8]{1,0:T(1,128)} %flags.6, s32[1,8]{1,0:T(1,128)} %flags.7, bf16[512,3072]{1,0:T(8,128)(2,1)} %get-tuple-element.20.rows_in, bf16[128,3072]{1,0:T(8,128)(2,1)S(1)} %collective-permute-done.2.received), custom_call_target="tpu_custom_call", output_to_operand_aliasing={{0}: (2, {})} | custom-call | tf_op jit(solution)/shard_map/even/pallas_call | solution.py:458
  67.1 2.1 %collective-permute-start.3 = (bf16[128,3072]{1,0:T(8,128)(2,1)}, bf16[128,3072]{1,0:T(8,128)(2,1)S(1)}, u32[]{:S(2)}, u32[]{:S(2)}) collective-permute-start(bf16[128,3072]{1,0:T(8,128)(2,1)} %get-tuple-element.23), channel_id=1, source_target_pairs={{32,64},{64,32},{96,128},{128,96},{160,192},{192,160},{33,65},{65,... | collective-permute-start | bytes 2359304 | tf_op jit(solution)/shard_map/ppermute | solution.py:467
  69.2 0.0 copy-done.1
  69.2 16.9 %all_to_all.15 = f32[32,8,128]{2,1,0:T(8,128)S(1)} all-to-all(f32[32,8,128]{2,1,0:T(8,128)S(1)} %bitcast.18), channel_id=1, replica_groups=mesh['temp'=8,'dom'=32] {'dom'}, dimensions={0} | all-to-all | bytes 262144 | tf_op jit(solution)/shard_map/all_to_all | solution.py:386
  86.1 1.6 %final.1 = (f32[1,512]{1,0:T(1,128)}, f32[1]{0:T(128)}) custom-call(f32[1,512]{1,0:T(1,128)} %get-tuple-element.19.later.updated, f32[256,128]{1,0:T(8,128)S(1)} %bitcast.12), custom_call_target="tpu_custom_call" | custom-call | tf_op jit(solution)/shard_map/final/pallas_call | solution.py:438
  87.7 0.0 collective-permute-done.3.received
  87.7 1.6 %odd.1 = bf16[512,3072]{1,0:T(8,128)(2,1)} custom-call(s32[1,8]{1,0:T(1,128)} %flags.7, bf16[512,3072]{1,0:T(8,128)(2,1)} %get-tuple-element.22.rows_in, bf16[128,3072]{1,0:T(8,128)(2,1)S(1)} %collective-permute-done.3.received), custom_call_target="tpu_custom_call", output_to_operand_aliasing={{}: (1, {})} | custom-call | tf_op jit(solution)/shard_map/odd/pallas_call | solution.py:468
Async XLA Ops:
  8.5 26.6 %all-to-all-start = ((bf16[32,8,896]{2,1,0:T(8,128)(2,1)}), bf16[32,8,896]{2,1,0:T(8,128)(2,1)S(1)}, u32[]{:S(2)}, u32[]{:S(2)}) async-start(bf16[32,8,896]{2,1,0:T(8,128)(2,1)} %bitcast.16), calls=%async_computation | async-start | bytes 917504 | tf_op jit(solution)/shard_map/all_to_all | solution.py:386
  35.2 0.7 copy-start
  37.8 20.9 %all-to-all-start.1 = ((bf16[32,8,768]{2,1,0:T(8,128)(2,1)}), bf16[32,8,768]{2,1,0:T(8,128)(2,1)S(1)}, u32[]{:S(2)}, u32[]{:S(2)}) async-start(bf16[32,8,768]{2,1,0:T(8,128)(2,1)} %bitcast.17), calls=%async_computation.1 | async-start | bytes 786432 | tf_op jit(solution)/shard_map/all_to_all | solution.py:386
  44.9 1.5 %collective-permute-start = (f32[8,512]{1,0:T(8,128)}, f32[8,512]{1,0:T(8,128)S(1)}, u32[]{:S(2)}, u32[]{:S(2)}) collective-permute-start(f32[8,512]{1,0:T(8,128)} %get-tuple-element.18.own), channel_id=1, source_target_pairs={{0,32},{32,0},{64,96},{96,64},{128,160},{160,128},{192,224},{224,1... | collective-permute-start | bytes 49160 | tf_op jit(solution)/shard_map/ppermute | solution.py:421
  47.7 5.3 %collective-permute-start.1 = (f32[8,512]{1,0:T(8,128)}, f32[8,512]{1,0:T(8,128)S(1)}, u32[]{:S(2)}, u32[]{:S(2)}) collective-permute-start(f32[8,512]{1,0:T(8,128)} %mix.1.own), channel_id=1, source_target_pairs={{32,64},{64,32},{96,128},{128,96},{160,192},{192,160},{33,65},{65,... | collective-permute-start | bytes 49160 | tf_op jit(solution)/shard_map/ppermute | solution.py:429
  58.7 10.4 %copy-start.1 = (f32[256,128]{1,0:T(8,128)S(1)}, f32[256,128]{1,0:T(8,128)}, u32[]{:S(2)}) copy-start(f32[256,128]{1,0:T(8,128)} %get-tuple-element.24) | copy-start | bytes 393220
  61.6 2.6 %collective-permute-start.2 = (bf16[128,3072]{1,0:T(8,128)(2,1)}, bf16[128,3072]{1,0:T(8,128)(2,1)S(1)}, u32[]{:S(2)}, u32[]{:S(2)}) collective-permute-start(bf16[128,3072]{1,0:T(8,128)(2,1)} %get-tuple-element.21), channel_id=1, source_target_pairs={{0,32},{32,0},{64,96},{96,64},{128,160},{160,128},{192,224},{224,1... | collective-permute-start | bytes 2359304 | tf_op jit(solution)/shard_map/ppermute | solution.py:457
  67.1 20.6 %collective-permute-start.3 = (bf16[128,3072]{1,0:T(8,128)(2,1)}, bf16[128,3072]{1,0:T(8,128)(2,1)S(1)}, u32[]{:S(2)}, u32[]{:S(2)}) collective-permute-start(bf16[128,3072]{1,0:T(8,128)(2,1)} %get-tuple-element.23), channel_id=1, source_target_pairs={{32,64},{64,32},{96,128},{128,96},{160,192},{192,160},{33,65},{65,... | collective-permute-start | bytes 2359304 | tf_op jit(solution)/shard_map/ppermute | solution.py:467

commit v3 on v2

--- a/solution.py
+++ b/solution.py
@@ -7,6 +7,7 @@
 from jax.experimental.pallas import tpu as pltpu
 from jax.sharding import PartitionSpec as P
 
+
 SWAPS = 2
 TILE = 8
 LANES = 128
@@ -23,7 +24,9 @@
 
 
 def gelu(x):
-    return x * (0.5 * (1.0 + jnp.tanh(0.7978845608028654 * (x + 0.044715 * (x * x * x)))))
+    half = 0.5 * x
+    inner = x * (0.7978845608028654 + (0.7978845608028654 * 0.044715) * (x * x))
+    return half + half * jnp.tanh(inner)
 
 
 def inside(x):
@@ -70,18 +73,19 @@
     hidden = gelu(mul(hidden, flow_mid[...])).astype(BF16)
     ready(2)
     log_det = jnp.zeros((rows.shape[0], 1), F32)
-    parts = []
+    parts, olds = [], []
     for at in range(0, half, chunk):
         log_scale = scale_limit * jnp.tanh(mul(hidden, flow_out[:, at : at + chunk]))
         shift = mul(hidden, flow_out[:, half + at : half + at + chunk])
         log_det += jnp.sum(log_scale, axis=1, keepdims=True)
-        moved = rows[:, half + at : half + at + chunk].astype(F32)
-        moved = (moved * jnp.exp(log_scale) + shift).astype(BF16)
+        old = rows[:, half + at : half + at + chunk]
+        moved = (old.astype(F32) * jnp.exp(log_scale) + shift).astype(BF16)
         keep(half + at, moved)
         parts.append(moved)
+        olds.append(old)
     ready(3)
     base = mul(kept, energy_in[:half, :])
-    before = base + mul(rows[:, half:], energy_in[half:, :])
+    before = base + mul(jnp.concatenate(olds, axis=1), energy_in[half:, :])
     after = base + mul(jnp.concatenate(parts, axis=1), energy_in[half:, :])
     ready(4)
     levels = []
@@ -157,34 +161,49 @@
 
 
 def rows_kernel(
-    read_out, rows, w0, w1, w2, w3, w4, out, scalars, s0, s1, s2, s3, s4, sems
+    pairs, read_out, particles, w0, w1, w2, w3, w4, out, scalars, packed, s0, s1, s2, s3, s4, rows, sems, row_sem, out_sem
 ):
     scratch = (s0, s1, s2, s3, s4)
     copies = fetches((w0, w1, w2, w3, w4), scratch, sems)
-    first = pl.program_id(0) == 0
-
-    @pl.when(first)
-    def _():
-        for copy in copies:
-            copy.start()
+    half = rows.shape[1] // 2
+    parts = [slice(0, half), slice(half, 2 * half)]
+    loads = [pltpu.make_async_copy(particles.at[:, p], rows.at[:, p], row_sem.at[i]) for i, p in enumerate(parts)]
+    loads[0].start()
+    copies[0].start()
+    copies[1].start()
+    copies[2].start()
+    loads[1].start()
+    copies[3].start()
+    copies[4].start()
 
     def ready(i):
-        @pl.when(first)
-        def _():
-            copies[i].wait()
+        copies[i].wait()
+        if i == 2:
+            loads[1].wait()
+
+    loads[0].wait()
+    kept_out = pltpu.make_async_copy(rows.at[:, parts[0]], out.at[:, parts[0]], out_sem.at[0])
+    kept_out.start()
 
     def keep(at, moved):
-        out[:, at : at + moved.shape[1]] = moved
-
-    half = rows.shape[1] // 2
-    out[:, :half] = rows[:, :half]
+        rows[:, at : at + moved.shape[1]] = moved
+
     log_det, level = step_rows(rows, scratch, read_out[...], ready, keep, 512)
+    moved_out = pltpu.make_async_copy(rows.at[:, parts[1]], out.at[:, parts[1]], out_sem.at[1])
+    moved_out.start()
     lane = lax.broadcasted_iota(jnp.int32, (rows.shape[0], LANES), 1)
     table = jnp.where(lane == 0, log_det, jnp.where(lane == 1, level, 0.0)).T
     scalars[...] = table[:TILE, :]
-
-
-def route_kernel(me, counts, log_weights, held, scalars, out, mine, tags):
+    block_rows = packed.shape[0] // SWAPS
+    slots = pairs.shape[1]
+    for i, slot in enumerate(find_two(pairs)):
+        start = pl.multiple_of(jnp.minimum(slot, slots - 1) * block_rows, block_rows)
+        packed[i * block_rows : (i + 1) * block_rows, :] = rows[pl.ds(start, block_rows), :]
+    kept_out.wait()
+    moved_out.wait()
+
+
+def route_kernel(me, counts, pairs, log_weights, held, scalars, out, mine, tags):
     size = held.shape[0]
     width = out.shape[1]
     tag = held[:, width:]
@@ -218,21 +237,21 @@
     log_det = jnp.where(vacant, lay(got[3:4] + got[4:5]), scalars[0:1, :])
     level = jnp.where(vacant, lay(got[5:6] + got[6:7] + got[7:8]), scalars[1:2, :])
     row = lax.broadcasted_iota(jnp.int32, (TILE, total), 0)
-    mine[...] = jnp.where(row == 0, log_det, jnp.where(row == 1, level, jnp.where(row == 2, weight, 0.0)))
-
-
-def mix_kernel(flags, own, other, out):
+    table = jnp.where(row == 0, log_det, jnp.where(row == 1, level, weight))
+    mine[...] = jnp.where(row == 3, spread(pairs, total).astype(F32), table)
+
+
+def stats_kernel(even, odd, inverse_temp, own, from_even, from_odd, from_both, updated, stats):
     total = own.shape[1]
-    take = spread(flags, total) == 1
-    row = lax.broadcasted_iota(jnp.int32, own.shape, 0)
-    out[...] = jnp.where(take & (row < 2), other[...], own[...])
-
-
-def stats_kernel(flags, inverse_temp, own, other, updated, stats):
-    take = spread(flags, own.shape[1]) == 1
-    log_det = jnp.where(take, other[0:1, :], own[0:1, :])
-    level = jnp.where(take, other[1:2, :], own[1:2, :])
-    new = own[2:3, :] + log_det - inverse_temp[0] * level
+    take_even, take_odd = spread(even, total) == 1, spread(odd, total) == 1
+    beyond = from_odd[3:4, :] > 0.5
+
+    def settle(r):
+        line = slice(r, r + 1)
+        swapped = jnp.where(take_even, from_even[line, :], own[line, :])
+        return jnp.where(take_odd, jnp.where(beyond, from_both[line, :], from_odd[line, :]), swapped)
+
+    new = own[2:3, :] + settle(0) - inverse_temp[0] * settle(1)
     updated[...] = new
     peak = jnp.max(new, axis=1, keepdims=True)
     shifted = jnp.exp(new - peak)
@@ -259,67 +278,63 @@
     return ref.at[pl.ds(pl.multiple_of(slot * block_rows, block_rows), block_rows), :]
 
 
-def run(copies):
+def join_kernel(
+    counts, other_counts, even, odd, rows_in, filled, filled_other, received, later, rows, packed, sems
+):
+    del rows_in, later
+    block_rows = packed.shape[0] // SWAPS
+    width = filled.shape[1]
+    slots = counts.shape[1]
+    vacant, other_vacant = find(counts, 0), find(other_counts, 0)
+    pair, odd_pair = find_two(even), find_two(odd)
+    parts = [slice(i * block_rows, (i + 1) * block_rows) for i in range(SWAPS)]
+    copies = []
+
+    def spill(go, source, slot, sem):
+        to = at_slot(rows, jnp.clip(slot, 0, slots - 1), block_rows)
+        for c in range(4):
+            part = source.at[c * block_rows : (c + 1) * block_rows, :]
+            column = to.at[:, c * width : (c + 1) * width]
+            copies.append((go, pltpu.make_async_copy(part, column, sems.at[sem + c])))
+
+    def hold(go, source, i):
+        @pl.when(go)
+        def _():
+            for c in range(4):
+                packed[parts[i], c * width : (c + 1) * width] = source[c * block_rows : (c + 1) * block_rows, :]
+
+    spill((vacant >= 0) & (vacant != pair[0]) & (vacant != pair[1]), filled, vacant, 0)
+    spill((other_vacant >= 0) & ((other_vacant == pair[0]) | (other_vacant == pair[1])), filled_other, other_vacant, 4)
+    for i, slot in enumerate(pair):
+        to = at_slot(rows, jnp.minimum(slot, slots - 1), block_rows)
+        go = (slot < slots) & (slot != other_vacant)
+        copies.append((go, pltpu.make_async_copy(received.at[parts[i], :], to, sems.at[8 + i])))
+    for i, slot in enumerate(odd_pair):
+        swapped = (slot == pair[0]) | (slot == pair[1])
+        source = at_slot(rows, jnp.minimum(slot, slots - 1), block_rows)
+        go = (slot < slots) & (slot != vacant) & jnp.logical_not(swapped)
+        copies.append((go, pltpu.make_async_copy(source, packed.at[parts[i], :], sems.at[8 + SWAPS + i])))
     for go, copy in copies:
 
         @pl.when(go)
         def _():
             copy.start()
 
+    for i, slot in enumerate(odd_pair):
+        swapped = (slot == pair[0]) | (slot == pair[1])
+        hold((slot == vacant) & jnp.logical_not(swapped), filled, i)
+        hold((slot < slots) & swapped & (slot == other_vacant), filled_other, i)
+        for j in range(SWAPS):
+
+            @pl.when((slot < slots) & (slot == pair[j]) & (slot != other_vacant))
+            def _():
+                packed[parts[i], :] = received[parts[j], :]
+
     for go, copy in copies:
 
         @pl.when(go)
         def _():
             copy.wait()
-
-
-def fill_kernel(counts, pairs, rows_in, pieces, later, rows, packed, sems):
-    del rows_in, later
-    block_rows = packed.shape[0] // SWAPS
-    width = pieces.shape[1]
-    slots = counts.shape[1]
-    vacant = find(counts, 0)
-    target = at_slot(rows, jnp.maximum(vacant, 0), block_rows)
-    copies = []
-    for c in range(4):
-        source = pieces.at[c * block_rows : (c + 1) * block_rows, :]
-        to = target.at[:, c * width : (c + 1) * width]
-        copies.append((vacant >= 0, pltpu.make_async_copy(source, to, sems.at[c])))
-    for i, slot in enumerate(find_two(pairs)):
-        part = slice(i * block_rows, (i + 1) * block_rows)
-        source = at_slot(rows, jnp.minimum(slot, slots - 1), block_rows)
-        go = (slot < slots) & (slot != vacant)
-        copies.append((go, pltpu.make_async_copy(source, packed.at[part, :], sems.at[4 + i])))
-
-        @pl.when(slot == vacant)
-        def _():
-            for c in range(4):
-                packed[part, c * width : (c + 1) * width] = pieces[c * block_rows : (c + 1) * block_rows, :]
-
-    run(copies)
-
-
-def swap_kernel(flags, next_flags, rows_in, received, rows, packed, sems):
-    del rows_in
-    block_rows = received.shape[0] // SWAPS
-    slots = flags.shape[1]
-    chosen = find_two(flags)
-    parts = [slice(i * block_rows, (i + 1) * block_rows) for i in range(SWAPS)]
-    copies = []
-    for i, slot in enumerate(chosen):
-        to = at_slot(rows, jnp.minimum(slot, slots - 1), block_rows)
-        copies.append((slot < slots, pltpu.make_async_copy(received.at[parts[i], :], to, sems.at[i])))
-    for i, slot in enumerate(find_two(next_flags)):
-        source = at_slot(rows, jnp.minimum(slot, slots - 1), block_rows)
-        go = (slot < slots) & (slot != chosen[0]) & (slot != chosen[1])
-        copies.append((go, pltpu.make_async_copy(source, packed.at[parts[i], :], sems.at[SWAPS + i])))
-        for j in range(SWAPS):
-
-            @pl.when((slot < slots) & (slot == chosen[j]))
-            def _():
-                packed[parts[i], :] = received[parts[j], :]
-
-    run(copies)
 
 
 def last_kernel(flags, rows_in, received, rows, sems):
@@ -331,7 +346,17 @@
         source = received.at[i * block_rows : (i + 1) * block_rows, :]
         to = at_slot(rows, jnp.minimum(slot, slots - 1), block_rows)
         copies.append((slot < slots, pltpu.make_async_copy(source, to, sems.at[i])))
-    run(copies)
+    for go, copy in copies:
+
+        @pl.when(go)
+        def _():
+            copy.start()
+
+    for go, copy in copies:
+
+        @pl.when(go)
+        def _():
+            copy.wait()
 
 
 def per_device(
@@ -383,88 +408,90 @@
 
     def exchange(x):
         cut = x.reshape(dom_count, TILE, x.shape[1])
-        return lax.all_to_all(cut, "dom", 0, 0, tiled=True).reshape(x.shape)
+        cut = lax.all_to_all(cut, "dom", 0, 0, tiled=True)
+        return cut.reshape(x.shape)
+
+    def swap(x, pairs):
+        return lax.ppermute(x, "temp", pairs)
 
     held = exchange(pieces)
-    step = total // 2
-    done, scalars = pl.pallas_call(
+    pack = shape((SWAPS * block_rows, features), BF16)
+    done, scalars, packed = pl.pallas_call(
         rows_kernel,
-        out_shape=(shape((total, features), BF16), shape((TILE, total), F32)),
-        grid=(2,),
-        in_specs=[
-            pl.BlockSpec((1, hidden), lambda i: (0, 0)),
-            pl.BlockSpec((step, features), lambda i: (i, 0)),
-        ]
-        + [ANY] * 5,
-        out_specs=(
-            pl.BlockSpec((step, features), lambda i: (i, 0)),
-            pl.BlockSpec((TILE, step), lambda i: (0, i)),
-        ),
-        scratch_shapes=weight_scratch + [pltpu.SemaphoreType.DMA((5,))],
+        out_shape=(shape((total, features), BF16), shape((TILE, total), F32), pack),
+        in_specs=[SMEM, VMEM, ANY] + [ANY] * 5,
+        out_specs=(ANY, VMEM, VMEM),
+        scratch_shapes=weight_scratch
+        + [
+            pltpu.VMEM((total, features), BF16),
+            pltpu.SemaphoreType.DMA((5,)),
+            pltpu.SemaphoreType.DMA((2,)),
+            pltpu.SemaphoreType.DMA((2,)),
+        ],
         cost_estimate=cost(total),
         name="rows",
-    )(read_out, rows, *weights)
+    )(even_pairs, read_out, rows, *weights)
+    even = [(i, i + 1 - 2 * (i % 2)) for i in range(groups)]
+    odd = [(i, i - 1 + 2 * (i % 2)) for i in range(1, groups - 1)]
+    both = [(even[source][1], target) for source, target in odd]
+    received = swap(packed, even)
+    other_counts = swap(offspring, even)
 
     me = lax.axis_index("dom").astype(jnp.int32).reshape(1)
     routed, mine = pl.pallas_call(
         route_kernel,
         out_shape=(shape((held_rows, width), BF16), shape((TILE, total), F32)),
-        in_specs=[SMEM, SMEM, VMEM, VMEM, VMEM],
+        in_specs=[SMEM, SMEM, SMEM, VMEM, VMEM, VMEM],
         out_specs=(VMEM, VMEM),
         scratch_shapes=[pltpu.VMEM((held_rows, LANES), F32)],
         name="route",
-    )(me, offspring, log_weights, inside(held), inside(scalars))
+    )(me, offspring, even_pairs, log_weights, inside(held), scalars)
     filled = exchange(routed)
 
-    even = [(i, i + 1 - 2 * (i % 2)) for i in range(groups)]
-    odd = [(i, i - 1 + 2 * (i % 2)) for i in range(1, groups - 1)]
-    other = lax.ppermute(mine, "temp", even)
-    mixed = pl.pallas_call(
-        mix_kernel,
-        out_shape=shape((TILE, total), F32),
-        in_specs=[SMEM, VMEM, VMEM],
-        out_specs=VMEM,
-        name="mix",
-    )(even_pairs, mine, inside(other))
-    other = lax.ppermute(mixed, "temp", odd)
-    updated, stats = pl.pallas_call(
+    from_even = swap(mine, even)
+    from_odd = swap(mine, odd)
+    from_both = swap(mine, both)
+    settle = pl.pallas_call(
         stats_kernel,
         out_shape=(shape((1, total), F32), shape((held_rows, LANES), F32)),
-        in_specs=[SMEM, SMEM, VMEM, VMEM],
+        in_specs=[SMEM, SMEM, SMEM, VMEM, VMEM, VMEM, VMEM],
         out_specs=(VMEM, VMEM),
         name="stats",
-    )(odd_pairs, inverse_temp, mixed, inside(other))
+    )
+    lines = [inside(line) for line in (from_even, from_odd, from_both)]
+    updated, stats = settle(even_pairs, odd_pairs, inverse_temp, mine, *lines)
     stats = exchange(stats)
-    new_log_weights, log_ess = pl.pallas_call(
+    close = pl.pallas_call(
         functools.partial(final_kernel, float(total * dom_count)),
         out_shape=(shape((1, total), F32), shape((1,), F32)),
         in_specs=[VMEM, VMEM],
         out_specs=(VMEM, SMEM),
         name="final",
-    )(updated, inside(stats))
+    )
+    new_log_weights, log_ess = close(updated, inside(stats))
 
     whole = shape((total, features), BF16)
-    pack = shape((SWAPS * block_rows, features), BF16)
+    filled_other = swap(filled, even)
     done, packed = pl.pallas_call(
-        fill_kernel,
+        join_kernel,
         out_shape=(whole, pack),
-        in_specs=[SMEM, SMEM, ANY, VMEM, ANY],
+        in_specs=[SMEM] * 4 + [ANY] + [VMEM] * 3 + [ANY],
         out_specs=(ANY, VMEM),
-        scratch_shapes=[pltpu.SemaphoreType.DMA((4 + SWAPS,))],
-        input_output_aliases={2: 0},
-        name="fill",
-    )(offspring, even_pairs, done, inside(filled), updated)
-    received = lax.ppermute(packed, "temp", even)
-    done, packed = pl.pallas_call(
-        swap_kernel,
-        out_shape=(whole, pack),
-        in_specs=[SMEM, SMEM, ANY, VMEM],
-        out_specs=(ANY, VMEM),
-        scratch_shapes=[pltpu.SemaphoreType.DMA((2 * SWAPS,))],
-        input_output_aliases={2: 0},
-        name="even",
-    )(even_pairs, odd_pairs, done, inside(received))
-    received = lax.ppermute(packed, "temp", odd)
+        scratch_shapes=[pltpu.SemaphoreType.DMA((8 + 2 * SWAPS,))],
+        input_output_aliases={4: 0},
+        name="join",
+    )(
+        offspring,
+        other_counts,
+        even_pairs,
+        odd_pairs,
+        done,
+        inside(filled),
+        inside(filled_other),
+        inside(received),
+        updated,
+    )
+    received = swap(packed, odd)
     done = pl.pallas_call(
         last_kernel,
         out_shape=whole,
@@ -493,6 +520,5 @@
         P(),
     )
     out_specs = (P("temp", "dom", None), P("temp", "dom"), P("temp"))
-    return jax.shard_map(
-        per_device, mesh=mesh, in_specs=in_specs, out_specs=out_specs, check_vma=False
-    )
+
+    return jax.shard_map(per_device, mesh=mesh, in_specs=in_specs, out_specs=out_specs, check_vma=False)

time: 90.3 us -> 94.6 us (1.048)
  waiting for transfers between devices: 13.4 us -> 18.1 us
  starting transfers between devices: 22.8 us -> 26.7 us
  Pallas kernels: 34.1 us -> 30.5 us
  blocking collectives: 16.9 us -> 15.5 us
    all_to_all x2, waiting for transfers between devices: 7.02 us -> 16.1 us  [exchange(): cut = lax.all_to_all(cut, 'dom', 0, 0, tiled=True)]
    ppermute x4 -> x7, waiting for transfers between devices: 6.34 us -> 2 us  [swap(): return lax.ppermute(x, 'temp', pairs)]
    pallas_call x5 -> x3, Pallas kernels: 10.2 us -> 6.2 us  [the longest x1 3.03 us: per_device(): pl.pallas_call(join_kernel, out_shape=(whole, pack), in_specs=[SMEM] * 4...]
    ppermute x4 -> x7, starting transfers between devices: 4.41 us -> 7.92 us  [swap(): return lax.ppermute(x, 'temp', pairs)]
    all_to_all x1, blocking collectives: 16.9 us -> 15.5 us  [exchange(): cut = lax.all_to_all(cut, 'dom', 0, 0, tiled=True)]
  transfers between devices with their start and end apart: 6 -> 9, of which waited for: 5 -> 3; matrix products, arithmetic and copies ran while one was open for 0% -> 0% of each run, Pallas kernels for 19% -> 17%
where the time goes in v3:
time: 94.6 us; the launch traced here: 92.8 us
  Pallas kernels  30.5 us (32%)
  starting transfers between devices  26.7 us (28%)
  waiting for transfers between devices  18.1 us (19%)
  blocking collectives  15.5 us (16%)
  between operations  1.43 us (2%)
    all_to_all x2, starting transfers between devices, exchange(): cut = lax.all_to_all(cut, 'dom', 0, 0, tiled=True)  18.8 us
    all_to_all x2, waiting for transfers between devices, exchange(): cut = lax.all_to_all(cut, 'dom', 0, 0, tiled=True)  16.1 us
    all_to_all x1, blocking collectives, exchange(): cut = lax.all_to_all(cut, 'dom', 0, 0, tiled=True)  15.5 us
    pallas_call x1, Pallas kernels, per_device(): pl.pallas_call(rows_kernel, out_shape=(shape((total, features), BF16), sh...  12.9 us
    ppermute x7, starting transfers between devices, swap(): return lax.ppermute(x, 'temp', pairs)  7.92 us
    pallas_call x1, Pallas kernels, per_device(): pl.pallas_call(spare_kernel, out_shape=shape((held_rows, width + LANES),...  7.9 us
    pallas_call x1, Pallas kernels, per_device(): pl.pallas_call(join_kernel, out_shape=(whole, pack), in_specs=[SMEM] * 4...  3.03 us
    pallas_call x1, Pallas kernels, per_device(): pl.pallas_call(route_kernel, out_shape=(shape((held_rows, width), BF16),...  2.01 us
  transfers between devices with their start and end apart: 9, of which 3 were waited for; matrix products, arithmetic and copies ran while one was open for 0% of the time, Pallas kernels for 17%

profile of v3, /device:TPU:16, one launch (start us, length us, event | category | flops | bytes accessed | tf_op | source)
XLA Modules:
  0.0 92.8 jit_solution(837053772378880646)
XLA Ops:
  0.6 7.9 %spare.1 = bf16[256,896]{1,0:T(8,128)(2,1)} custom-call(s32[1,8]{1,0:T(1,128)} %counts.5, f32[1,512]{1,0:T(1,128)} %log_weights.3, f32[1,512]{1,0:T(1,128)} %bitcast.20, bf16[512,3072]{1,0:T(8,128)(2,1)} %bitcast.15, bf16[1536,512]{1,0:T(8,128)(2,1)} %w0.3, bf16[512,512]{1,0:T(8,128)(2,1)} %w1.3, bf16[512,3072]{1,0:T(8,128)(2,1)} %w2.3, ...), custom_call_target="tpu_custom_call" | custom-call | flops 671088640 | bytes 8912896 | tf_op jit(solution)/shard_map/spare/pallas_call | solution.py:397
  8.5 11.3 %all-to-all-start = ((bf16[32,8,896]{2,1,0:T(8,128)(2,1)}), bf16[32,8,896]{2,1,0:T(8,128)(2,1)S(1)}, u32[]{:S(2)}, u32[]{:S(2)}) async-start(bf16[32,8,896]{2,1,0:T(8,128)(2,1)} %bitcast.17), calls=%async_computation | async-start | bytes 917504 | tf_op jit(solution)/shard_map/all_to_all | solution.py:411
  19.9 0.0 copy-start.1
  19.9 12.9 %rows.1 = (bf16[512,3072]{1,0:T(8,128)(2,1)}, f32[8,512]{1,0:T(8,128)}, bf16[128,3072]{1,0:T(8,128)(2,1)}) custom-call(s32[1,8]{1,0:T(1,128)} %even.3, f32[1,512]{1,0:T(1,128)} %bitcast.21, bf16[512,3072]{1,0:T(8,128)(2,1)} %bitcast.16, bf16[1536,512]{1,0:T(8,128)(2,1)} %w0.3, bf16[512,512]{1,0:T(8,128)(2,1)} %w1.3, bf16[512,3072]{1,0:T(8,128)(2,1)} %w2.3, ...), custom_call_target="tpu_custom_call" | custom-call | flops 5368709120 | bytes 8912896 | tf_op jit(solution)/shard_map/rows/pallas_call | solution.py:419
  32.8 2.3 %all-to-all-done = bf16[32,8,896]{2,1,0:T(8,128)(2,1)S(1)} async-done(((bf16[32,8,896]{2,1,0:T(8,128)(2,1)}), bf16[32,8,896]{2,1,0:T(8,128)(2,1)S(1)}, u32[]{:S(2)}, u32[]{:S(2)}) %all-to-all-start) | async-done | bytes 458784 | tf_op jit(solution)/shard_map/all_to_all | solution.py:411
  35.2 2.0 %route.1 = (bf16[256,768]{1,0:T(8,128)(2,1)}, f32[8,512]{1,0:T(8,128)}) custom-call(s32[1]{0:T(128)} %bitcast.2.me, s32[1,8]{1,0:T(1,128)} %counts.5, s32[1,8]{1,0:T(1,128)} %even.3, f32[1,512]{1,0:T(1,128)} %log_weights.3, bf16[256,896]{1,0:T(8,128)(2,1)S(1)} %bitcast.10, f32[8,512]{1,0:T(8,128)} %get-tuple-element.15.scalars), custom_call_target="tpu_custom_call" | custom-call | tf_op jit(solution)/shard_map/route/pallas_call | solution.py:441
  37.2 7.5 %all-to-all-start.1 = ((bf16[32,8,768]{2,1,0:T(8,128)(2,1)}), bf16[32,8,768]{2,1,0:T(8,128)(2,1)S(1)}, u32[]{:S(2)}, u32[]{:S(2)}) async-start(bf16[32,8,768]{2,1,0:T(8,128)(2,1)} %bitcast.18), calls=%async_computation.1 | async-start | bytes 786432 | tf_op jit(solution)/shard_map/all_to_all | solution.py:411
  44.7 0.1 collective-permute-start.2
  44.8 13.8 %all-to-all-done.1 = bf16[32,8,768]{2,1,0:T(8,128)(2,1)S(1)} async-done(((bf16[32,8,768]{2,1,0:T(8,128)(2,1)}), bf16[32,8,768]{2,1,0:T(8,128)(2,1)S(1)}, u32[]{:S(2)}, u32[]{:S(2)}) %all-to-all-start.1) | async-done | bytes 393248 | tf_op jit(solution)/shard_map/all_to_all | solution.py:411
  58.5 0.0 collective-permute-start.1
  58.5 3.2 %collective-permute-start.5 = (f32[8,512]{1,0:T(8,128)}, f32[8,512]{1,0:T(8,128)S(1)}, u32[]{:S(2)}, u32[]{:S(2)}) collective-permute-start(f32[8,512]{1,0:T(8,128)} %get-tuple-element.18.own), channel_id=1, source_target_pairs={{0,64},{96,32},{64,128},{160,96},{128,192},{224,160},{1,65},{97,33... | collective-permute-start | bytes 49160 | tf_op jit(solution)/shard_map/ppermute | solution.py:415
  61.7 1.9 %collective-permute-start.4 = (f32[8,512]{1,0:T(8,128)}, f32[8,512]{1,0:T(8,128)S(1)}, u32[]{:S(2)}, u32[]{:S(2)}) collective-permute-start(f32[8,512]{1,0:T(8,128)} %get-tuple-element.18.own), channel_id=1, source_target_pairs={{32,64},{64,32},{96,128},{128,96},{160,192},{192,160},{33,65},{65,... | collective-permute-start | bytes 49160 | tf_op jit(solution)/shard_map/ppermute | solution.py:415
  63.6 0.1 collective-permute-start.3
  64.4 0.0 collective-permute-done.5.from_both
  64.4 0.0 copy-done.1
  64.4 0.6 collective-permute-start
  65.0 2.0 %collective-permute-done.4.from_odd = f32[8,512]{1,0:T(8,128)S(1)} collective-permute-done((f32[8,512]{1,0:T(8,128)}, f32[8,512]{1,0:T(8,128)S(1)}, u32[]{:S(2)}, u32[]{:S(2)}) %collective-permute-start.4) | collective-permute-done | bytes 16416 | tf_op jit(solution)/shard_map/ppermute | solution.py:415
  67.0 0.0 collective-permute-done.3.from_even
  67.0 1.6 %stats.1 = (f32[1,512]{1,0:T(1,128)}, f32[256,128]{1,0:T(8,128)}) custom-call(s32[1,8]{1,0:T(1,128)} %even.3, s32[1,8]{1,0:T(1,128)} %flags.1, f32[1]{0:T(128)S(6)} %copy.19.inverse_temp, f32[8,512]{1,0:T(8,128)} %get-tuple-element.18.own, f32[8,512]{1,0:T(8,128)S(1)} %collective-permute-done.3.from_even, f32[8,512]{1,0:T(8,128)S(1)} %collective-permute-done.4.from_odd, ...), custom_call_target="tpu_custom_call" | custom-call | tf_op jit(solution)/shard_map/stats/pallas_call | solution.py:462
  68.6 0.0 copy-start
  68.6 0.0 collective-permute-done.other_counts
  68.6 0.0 copy-start.2
  68.6 0.0 collective-permute-done.2.received
  68.6 0.0 collective-permute-done.1.filled_other
  68.6 0.5 copy-done.2
  69.1 3.0 %join.1 = (bf16[512,3072]{1,0:T(8,128)(2,1)}, bf16[128,3072]{1,0:T(8,128)(2,1)}) custom-call(s32[1,8]{1,0:T(1,128)} %counts.5, s32[1,8]{1,0:T(1,128)} %copy-done.2, s32[1,8]{1,0:T(1,128)} %even.3, s32[1,8]{1,0:T(1,128)} %flags.1, bf16[512,3072]{1,0:T(8,128)(2,1)} %get-tuple-element.14.rows_in, ...), custom_call_target="tpu_custom_call", output_to_operand_aliasing={{0}: (4, {})} | custom-call | tf_op jit(solution)/shard_map/join/pallas_call | solution.py:475
  72.1 2.0 %collective-permute-start.6 = (bf16[128,3072]{1,0:T(8,128)(2,1)}, bf16[128,3072]{1,0:T(8,128)(2,1)S(1)}, u32[]{:S(2)}, u32[]{:S(2)}) collective-permute-start(bf16[128,3072]{1,0:T(8,128)(2,1)} %get-tuple-element.21), channel_id=1, source_target_pairs={{32,64},{64,32},{96,128},{128,96},{160,192},{192,160},{33,65},{65,... | collective-permute-start | bytes 2359304 | tf_op jit(solution)/shard_map/ppermute | solution.py:415
  74.2 0.0 copy-done
  74.2 15.5 %all_to_all.15 = f32[32,8,128]{2,1,0:T(8,128)S(1)} all-to-all(f32[32,8,128]{2,1,0:T(8,128)S(1)} %bitcast.19), channel_id=1, replica_groups=mesh['temp'=8,'dom'=32] {'dom'}, dimensions={0} | all-to-all | bytes 262144 | tf_op jit(solution)/shard_map/all_to_all | solution.py:411
  89.7 1.6 %final.1 = (f32[1,512]{1,0:T(1,128)}, f32[1]{0:T(128)}) custom-call(f32[1,512]{1,0:T(1,128)} %get-tuple-element.19.later.updated, f32[256,128]{1,0:T(8,128)S(1)} %bitcast.13), custom_call_target="tpu_custom_call" | custom-call | tf_op jit(solution)/shard_map/final/pallas_call | solution.py:471
  91.3 0.0 collective-permute-done.6.received
  91.3 1.4 %odd.5 = bf16[512,3072]{1,0:T(8,128)(2,1)} custom-call(s32[1,8]{1,0:T(1,128)} %flags.1, bf16[512,3072]{1,0:T(8,128)(2,1)} %get-tuple-element.20.rows_in, bf16[128,3072]{1,0:T(8,128)(2,1)S(1)} %collective-permute-done.6.received), custom_call_target="tpu_custom_call", output_to_operand_aliasing={{}: (1, {})} | custom-call | tf_op jit(solution)/shard_map/odd/pallas_call | solution.py:495
Async XLA Ops:
  8.5 26.6 %all-to-all-start = ((bf16[32,8,896]{2,1,0:T(8,128)(2,1)}), bf16[32,8,896]{2,1,0:T(8,128)(2,1)S(1)}, u32[]{:S(2)}, u32[]{:S(2)}) async-start(bf16[32,8,896]{2,1,0:T(8,128)(2,1)} %bitcast.17), calls=%async_computation | async-start | bytes 917504 | tf_op jit(solution)/shard_map/all_to_all | solution.py:411
  19.9 44.5 %copy-start.1 = (s32[1,8]{1,0:T(1,128)S(1)}, s32[1,8]{1,0:T(1,128)}, u32[]{:S(2)}) copy-start(s32[1,8]{1,0:T(1,128)} %counts.5) | copy-start | bytes 100
  37.2 21.3 %all-to-all-start.1 = ((bf16[32,8,768]{2,1,0:T(8,128)(2,1)}), bf16[32,8,768]{2,1,0:T(8,128)(2,1)S(1)}, u32[]{:S(2)}, u32[]{:S(2)}) async-start(bf16[32,8,768]{2,1,0:T(8,128)(2,1)} %bitcast.18), calls=%async_computation.1 | async-start | bytes 786432 | tf_op jit(solution)/shard_map/all_to_all | solution.py:411
  44.7 23.9 %collective-permute-start.2 = (bf16[128,3072]{1,0:T(8,128)(2,1)}, bf16[128,3072]{1,0:T(8,128)(2,1)S(1)}, u32[]{:S(2)}, u32[]{:S(2)}) collective-permute-start(bf16[128,3072]{1,0:T(8,128)(2,1)} %get-tuple-element.17), channel_id=1, source_target_pairs={{0,32},{32,0},{64,96},{96,64},{128,160},{160,128},{192,224},{224,1... | collective-permute-start | bytes 2359304 | tf_op jit(solution)/shard_map/ppermute | solution.py:415
  58.5 10.1 %collective-permute-start.1 = (bf16[256,768]{1,0:T(8,128)(2,1)S(1)}, bf16[256,768]{1,0:T(8,128)(2,1)S(1)}, u32[]{:S(2)}, u32[]{:S(2)}) collective-permute-start(bf16[256,768]{1,0:T(8,128)(2,1)S(1)} %bitcast.11), channel_id=1, source_target_pairs={{0,32},{32,0},{64,96},{96,64},{128,160},{160,128},{192,224},{224,1... | collective-permute-start | bytes 1179656 | tf_op jit(solution)/shard_map/ppermute | solution.py:415
  58.5 5.9 %collective-permute-start.5 = (f32[8,512]{1,0:T(8,128)}, f32[8,512]{1,0:T(8,128)S(1)}, u32[]{:S(2)}, u32[]{:S(2)}) collective-permute-start(f32[8,512]{1,0:T(8,128)} %get-tuple-element.18.own), channel_id=1, source_target_pairs={{0,64},{96,32},{64,128},{160,96},{128,192},{224,160},{1,65},{97,33... | collective-permute-start | bytes 49160 | tf_op jit(solution)/shard_map/ppermute | solution.py:415
  61.7 5.3 %collective-permute-start.4 = (f32[8,512]{1,0:T(8,128)}, f32[8,512]{1,0:T(8,128)S(1)}, u32[]{:S(2)}, u32[]{:S(2)}) collective-permute-start(f32[8,512]{1,0:T(8,128)} %get-tuple-element.18.own), channel_id=1, source_target_pairs={{32,64},{64,32},{96,128},{128,96},{160,192},{192,160},{33,65},{65,... | collective-permute-start | bytes 49160 | tf_op jit(solution)/shard_map/ppermute | solution.py:415
  63.6 3.3 %collective-permute-start.3 = (f32[8,512]{1,0:T(8,128)}, f32[8,512]{1,0:T(8,128)S(1)}, u32[]{:S(2)}, u32[]{:S(2)}) collective-permute-start(f32[8,512]{1,0:T(8,128)} %get-tuple-element.18.own), channel_id=1, source_target_pairs={{0,32},{32,0},{64,96},{96,64},{128,160},{160,128},{192,224},{224,1... | collective-permute-start | bytes 49160 | tf_op jit(solution)/shard_map/ppermute | solution.py:415
  64.4 4.2 %collective-permute-start = (s32[1,8]{1,0:T(1,128)S(1)}, s32[1,8]{1,0:T(1,128)S(1)}, u32[]{:S(2)}, u32[]{:S(2)}) collective-permute-start(s32[1,8]{1,0:T(1,128)S(1)} %copy-done.1), channel_id=1, source_target_pairs={{0,32},{32,0},{64,96},{96,64},{128,160},{160,128},{192,224},{224,1... | collective-permute-start | bytes 104 | tf_op jit(solution)/shard_map/ppermute | solution.py:415
  68.6 5.6 %copy-start = (f32[256,128]{1,0:T(8,128)S(1)}, f32[256,128]{1,0:T(8,128)}, u32[]{:S(2)}) copy-start(f32[256,128]{1,0:T(8,128)} %get-tuple-element.22) | copy-start | bytes 393220
  68.6 0.5 copy-start.2
  72.1 19.2 %collective-permute-start.6 = (bf16[128,3072]{1,0:T(8,128)(2,1)}, bf16[128,3072]{1,0:T(8,128)(2,1)S(1)}, u32[]{:S(2)}, u32[]{:S(2)}) collective-permute-start(bf16[128,3072]{1,0:T(8,128)(2,1)} %get-tuple-element.21), channel_id=1, source_target_pairs={{32,64},{64,32},{96,128},{128,96},{160,192},{192,160},{33,65},{65,... | collective-permute-start | bytes 2359304 | tf_op jit(solution)/shard_map/ppermute | solution.py:415

commit v4 on v3

--- a/solution.py
+++ b/solution.py
@@ -238,10 +238,11 @@
     level = jnp.where(vacant, lay(got[5:6] + got[6:7] + got[7:8]), scalars[1:2, :])
     row = lax.broadcasted_iota(jnp.int32, (TILE, total), 0)
     table = jnp.where(row == 0, log_det, jnp.where(row == 1, level, weight))
-    mine[...] = jnp.where(row == 3, spread(pairs, total).astype(F32), table)
-
-
-def stats_kernel(even, odd, inverse_temp, own, from_even, from_odd, from_both, updated, stats):
+    table = jnp.where(row == 3, spread(pairs, total).astype(F32), table)
+    mine[...] = jnp.where(row == 4, find(counts, 0).astype(F32), table)
+
+
+def stats_kernel(even, odd, inverse_temp, own, from_even, from_odd, from_both, updated, stats, marks):
     total = own.shape[1]
     take_even, take_odd = spread(even, total) == 1, spread(odd, total) == 1
     beyond = from_odd[3:4, :] > 0.5
@@ -251,6 +252,12 @@
         swapped = jnp.where(take_even, from_even[line, :], own[line, :])
         return jnp.where(take_odd, jnp.where(beyond, from_both[line, :], from_odd[line, :]), swapped)
 
+    for i, line in enumerate((from_even, from_odd, from_both)):
+        marks[0, i] = jnp.max(line[4:5, :]).astype(jnp.int32)
+    slots = odd.shape[1]
+    slot_of = lax.broadcasted_iota(jnp.int32, (1, total), 1) // (total // slots)
+    for i, slot in enumerate(find_two(odd)):
+        marks[0, 3 + i] = jnp.max(jnp.where(beyond & (slot_of == slot), 1.0, 0.0)).astype(jnp.int32)
     new = own[2:3, :] + settle(0) - inverse_temp[0] * settle(1)
     updated[...] = new
     peak = jnp.max(new, axis=1, keepdims=True)
@@ -278,17 +285,57 @@
     return ref.at[pl.ds(pl.multiple_of(slot * block_rows, block_rows), block_rows), :]
 
 
+def go_all(copies):
+    for go, copy in copies:
+
+        @pl.when(go)
+        def _():
+            copy.start()
+
+
+def wait_all(copies):
+    for go, copy in copies:
+
+        @pl.when(go)
+        def _():
+            copy.wait()
+
+
+def next_kernel(even, odd, rows, received, packed, sems):
+    block_rows = packed.shape[0] // SWAPS
+    slots = even.shape[1]
+    pair = find_two(even)
+    parts = [slice(i * block_rows, (i + 1) * block_rows) for i in range(SWAPS)]
+    copies = []
+    odd_pair = find_two(odd)
+    for i, slot in enumerate(odd_pair):
+        source = at_slot(rows, jnp.minimum(slot, slots - 1), block_rows)
+        go = (slot < slots) & (slot != pair[0]) & (slot != pair[1])
+        copies.append((go, pltpu.make_async_copy(source, packed.at[parts[i], :], sems.at[i])))
+    go_all(copies)
+    for i, slot in enumerate(odd_pair):
+        for j in range(SWAPS):
+
+            @pl.when((slot < slots) & (slot == pair[j]))
+            def _():
+                packed[parts[i], :] = received[parts[j], :]
+
+    wait_all(copies)
+
+
 def join_kernel(
-    counts, other_counts, even, odd, rows_in, filled, filled_other, received, later, rows, packed, sems
+    counts, even, odd, marks, rows_in, filled, late_even, late_odd, late_both, from_even, from_odd, rows, sems
 ):
-    del rows_in, later
-    block_rows = packed.shape[0] // SWAPS
+    del rows_in
+    block_rows = from_even.shape[0] // SWAPS
     width = filled.shape[1]
     slots = counts.shape[1]
-    vacant, other_vacant = find(counts, 0), find(other_counts, 0)
+    vacant = find(counts, 0)
     pair, odd_pair = find_two(even), find_two(odd)
-    parts = [slice(i * block_rows, (i + 1) * block_rows) for i in range(SWAPS)]
     copies = []
+
+    def has(chosen, slot):
+        return (slot >= 0) & (slot < slots) & ((slot == chosen[0]) | (slot == chosen[1]))
 
     def spill(go, source, slot, sem):
         to = at_slot(rows, jnp.clip(slot, 0, slots - 1), block_rows)
@@ -297,66 +344,30 @@
             column = to.at[:, c * width : (c + 1) * width]
             copies.append((go, pltpu.make_async_copy(part, column, sems.at[sem + c])))
 
-    def hold(go, source, i):
-        @pl.when(go)
-        def _():
-            for c in range(4):
-                packed[parts[i], c * width : (c + 1) * width] = source[c * block_rows : (c + 1) * block_rows, :]
-
-    spill((vacant >= 0) & (vacant != pair[0]) & (vacant != pair[1]), filled, vacant, 0)
-    spill((other_vacant >= 0) & ((other_vacant == pair[0]) | (other_vacant == pair[1])), filled_other, other_vacant, 4)
+    def place(go, source, i, slot, sem):
+        part = source.at[i * block_rows : (i + 1) * block_rows, :]
+        to = at_slot(rows, jnp.minimum(slot, slots - 1), block_rows)
+        copies.append((go, pltpu.make_async_copy(part, to, sems.at[sem])))
+
+    even_vacant, odd_vacant, both_vacant = marks[0, 0], marks[0, 1], marks[0, 2]
+    free = jnp.logical_not(has(pair, vacant) | has(odd_pair, vacant))
+    spill((vacant >= 0) & free, filled, vacant, 0)
+    spill(has(pair, even_vacant) & jnp.logical_not(has(odd_pair, even_vacant)), late_even, even_vacant, 4)
     for i, slot in enumerate(pair):
-        to = at_slot(rows, jnp.minimum(slot, slots - 1), block_rows)
-        go = (slot < slots) & (slot != other_vacant)
-        copies.append((go, pltpu.make_async_copy(received.at[parts[i], :], to, sems.at[8 + i])))
+        go = (slot < slots) & (slot != even_vacant) & jnp.logical_not(has(odd_pair, slot))
+        place(go, from_even, i, slot, 16 + i)
+    near, far = False, False
     for i, slot in enumerate(odd_pair):
-        swapped = (slot == pair[0]) | (slot == pair[1])
-        source = at_slot(rows, jnp.minimum(slot, slots - 1), block_rows)
-        go = (slot < slots) & (slot != vacant) & jnp.logical_not(swapped)
-        copies.append((go, pltpu.make_async_copy(source, packed.at[parts[i], :], sems.at[8 + SWAPS + i])))
-    for go, copy in copies:
-
-        @pl.when(go)
-        def _():
-            copy.start()
-
-    for i, slot in enumerate(odd_pair):
-        swapped = (slot == pair[0]) | (slot == pair[1])
-        hold((slot == vacant) & jnp.logical_not(swapped), filled, i)
-        hold((slot < slots) & swapped & (slot == other_vacant), filled_other, i)
-        for j in range(SWAPS):
-
-            @pl.when((slot < slots) & (slot == pair[j]) & (slot != other_vacant))
-            def _():
-                packed[parts[i], :] = received[parts[j], :]
-
-    for go, copy in copies:
-
-        @pl.when(go)
-        def _():
-            copy.wait()
-
-
-def last_kernel(flags, rows_in, received, rows, sems):
-    del rows_in
-    block_rows = received.shape[0] // SWAPS
-    slots = flags.shape[1]
-    copies = []
-    for i, slot in enumerate(find_two(flags)):
-        source = received.at[i * block_rows : (i + 1) * block_rows, :]
-        to = at_slot(rows, jnp.minimum(slot, slots - 1), block_rows)
-        copies.append((slot < slots, pltpu.make_async_copy(source, to, sems.at[i])))
-    for go, copy in copies:
-
-        @pl.when(go)
-        def _():
-            copy.start()
-
-    for go, copy in copies:
-
-        @pl.when(go)
-        def _():
-            copy.wait()
+        beyond = marks[0, 3 + i] == 1
+        live = slot < slots
+        near_hit = live & jnp.logical_not(beyond) & (slot == odd_vacant)
+        far_hit = live & beyond & (slot == both_vacant)
+        near, far = near | near_hit, far | far_hit
+        place(live & jnp.logical_not(near_hit | far_hit), from_odd, i, slot, 16 + SWAPS + i)
+    spill(near, late_odd, odd_vacant, 8)
+    spill(far, late_both, both_vacant, 12)
+    go_all(copies)
+    wait_all(copies)
 
 
 def per_device(
@@ -434,8 +445,19 @@
     even = [(i, i + 1 - 2 * (i % 2)) for i in range(groups)]
     odd = [(i, i - 1 + 2 * (i % 2)) for i in range(1, groups - 1)]
     both = [(even[source][1], target) for source, target in odd]
-    received = swap(packed, even)
-    other_counts = swap(offspring, even)
+    from_even_rows = swap(packed, even)
+    follow = pl.pallas_call(
+        next_kernel,
+        out_shape=pack,
+        in_specs=[SMEM, SMEM, ANY, VMEM],
+        out_specs=VMEM,
+        scratch_shapes=[pltpu.SemaphoreType.DMA((SWAPS,))],
+        compiler_params=pltpu.CompilerParams(vmem_limit_bytes=8 << 20),
+        name="next",
+    )
+    from_even_rows = inside(from_even_rows)
+    packed = follow(even_pairs, odd_pairs, done, from_even_rows)
+    from_odd_rows = inside(swap(packed, odd))
 
     me = lax.axis_index("dom").astype(jnp.int32).reshape(1)
     routed, mine = pl.pallas_call(
@@ -444,6 +466,7 @@
         in_specs=[SMEM, SMEM, SMEM, VMEM, VMEM, VMEM],
         out_specs=(VMEM, VMEM),
         scratch_shapes=[pltpu.VMEM((held_rows, LANES), F32)],
+        compiler_params=pltpu.CompilerParams(vmem_limit_bytes=16 << 20),
         name="route",
     )(me, offspring, even_pairs, log_weights, inside(held), scalars)
     filled = exchange(routed)
@@ -453,54 +476,51 @@
     from_both = swap(mine, both)
     settle = pl.pallas_call(
         stats_kernel,
-        out_shape=(shape((1, total), F32), shape((held_rows, LANES), F32)),
+        out_shape=(
+            shape((1, total), F32),
+            shape((held_rows, LANES), F32),
+            shape((1, TILE), jnp.int32),
+        ),
         in_specs=[SMEM, SMEM, SMEM, VMEM, VMEM, VMEM, VMEM],
-        out_specs=(VMEM, VMEM),
+        out_specs=(VMEM, VMEM, SMEM),
+        compiler_params=pltpu.CompilerParams(vmem_limit_bytes=8 << 20),
         name="stats",
     )
     lines = [inside(line) for line in (from_even, from_odd, from_both)]
-    updated, stats = settle(even_pairs, odd_pairs, inverse_temp, mine, *lines)
+    updated, stats, marks = settle(even_pairs, odd_pairs, inverse_temp, mine, *lines)
     stats = exchange(stats)
     close = pl.pallas_call(
         functools.partial(final_kernel, float(total * dom_count)),
         out_shape=(shape((1, total), F32), shape((1,), F32)),
         in_specs=[VMEM, VMEM],
         out_specs=(VMEM, SMEM),
+        compiler_params=pltpu.CompilerParams(vmem_limit_bytes=8 << 20),
         name="final",
     )
     new_log_weights, log_ess = close(updated, inside(stats))
 
-    whole = shape((total, features), BF16)
-    filled_other = swap(filled, even)
-    done, packed = pl.pallas_call(
+    late = [inside(swap(filled, pairs)) for pairs in (even, odd, both)]
+    join = pl.pallas_call(
         join_kernel,
-        out_shape=(whole, pack),
-        in_specs=[SMEM] * 4 + [ANY] + [VMEM] * 3 + [ANY],
-        out_specs=(ANY, VMEM),
-        scratch_shapes=[pltpu.SemaphoreType.DMA((8 + 2 * SWAPS,))],
+        out_shape=shape((total, features), BF16),
+        in_specs=[SMEM] * 4 + [ANY] + [VMEM] * 6,
+        out_specs=ANY,
+        scratch_shapes=[pltpu.SemaphoreType.DMA((16 + 2 * SWAPS,))],
         input_output_aliases={4: 0},
+        compiler_params=pltpu.CompilerParams(vmem_limit_bytes=8 << 20),
         name="join",
-    )(
+    )
+    done = join(
         offspring,
-        other_counts,
         even_pairs,
         odd_pairs,
+        marks,
         done,
         inside(filled),
-        inside(filled_other),
-        inside(received),
-        updated,
-    )
-    received = swap(packed, odd)
-    done = pl.pallas_call(
-        last_kernel,
-        out_shape=whole,
-        in_specs=[SMEM, ANY, VMEM],
-        out_specs=ANY,
-        scratch_shapes=[pltpu.SemaphoreType.DMA((SWAPS,))],
-        input_output_aliases={1: 0},
-        name="odd",
-    )(odd_pairs, done, inside(received))
+        *late,
+        from_even_rows,
+        from_odd_rows,
+    )
     return done.reshape(1, total, features), new_log_weights, log_ess
 
 
@@ -521,4 +541,6 @@
     )
     out_specs = (P("temp", "dom", None), P("temp", "dom"), P("temp"))
 
-    return jax.shard_map(per_device, mesh=mesh, in_specs=in_specs, out_specs=out_specs, check_vma=False)
+    return jax.shard_map(
+        per_device, mesh=mesh, in_specs=in_specs, out_specs=out_specs, check_vma=False
+    )

time: 94.6 us -> 101 us (1.068)
  starting transfers between devices: 26.7 us -> 31.2 us
  Pallas kernels: 30.5 us -> 27.7 us
  waiting for transfers between devices: 18.1 us -> 20.4 us
  local copies, waits for them, and re-layouts: 0.49 us -> 2.62 us
  blocking collectives: 15.5 us -> 16.6 us
    ppermute x7 -> x8, waiting for transfers between devices: 2 us -> 8.48 us  [swap(): return lax.ppermute(x, 'temp', pairs)]
    ppermute x7 -> x8, starting transfers between devices: 7.92 us -> 12.1 us  [swap(): return lax.ppermute(x, 'temp', pairs)]
    all_to_all x2, waiting for transfers between devices: 16.1 us -> 11.9 us  [exchange(): cut = lax.all_to_all(cut, 'dom', 0, 0, tiled=True)]
    unnamed x6 -> x12, local copies, waits for them, and re-layouts: 0.49 us -> 2.62 us
    pallas_call x3, Pallas kernels: 6.06 us -> 4.01 us  [the longest x1 1.91 us: per_device(): join(offspring, even_pairs, odd_pairs, marks, done, inside(filled), *late...]
    all_to_all x1, blocking collectives: 15.5 us -> 16.6 us  [exchange(): cut = lax.all_to_all(cut, 'dom', 0, 0, tiled=True)]
  transfers between devices with their start and end apart: 9 -> 10, of which waited for: 3 -> 5; matrix products, arithmetic and copies ran while one was open for 0% -> 0% of each run, Pallas kernels for 17% -> 18%
where the time goes in v4:
time: 101 us; the launch traced here: 99.9 us
  starting transfers between devices  31.2 us (31%)
  Pallas kernels  27.7 us (27%)
  waiting for transfers between devices  20.4 us (20%)
  blocking collectives  16.6 us (16%)
  local copies, waits for them, and re-layouts  2.62 us (3%)
  between operations  1.5 us (1%)
    all_to_all x2, starting transfers between devices, exchange(): cut = lax.all_to_all(cut, 'dom', 0, 0, tiled=True)  19 us
    all_to_all x1, blocking collectives, exchange(): cut = lax.all_to_all(cut, 'dom', 0, 0, tiled=True)  16.6 us
    pallas_call x1, Pallas kernels, per_device(): pl.pallas_call(rows_kernel, out_shape=(shape((total, features), BF16), sh...  13.1 us
    ppermute x8, starting transfers between devices, swap(): return lax.ppermute(x, 'temp', pairs)  12.1 us
    all_to_all x2, waiting for transfers between devices, exchange(): cut = lax.all_to_all(cut, 'dom', 0, 0, tiled=True)  11.9 us
    ppermute x8, waiting for transfers between devices, swap(): return lax.ppermute(x, 'temp', pairs)  8.48 us
    pallas_call x1, Pallas kernels, per_device(): pl.pallas_call(spare_kernel, out_shape=shape((held_rows, width + LANES),...  7.9 us
    unnamed x12, local copies, waits for them, and re-layouts  2.62 us
  transfers between devices with their start and end apart: 10, of which 5 were waited for; matrix products, arithmetic and copies ran while one was open for 0% of the time, Pallas kernels for 18%

profile of v4, /device:TPU:16, one launch (start us, length us, event | category | flops | bytes accessed | tf_op | source)
XLA Modules:
  0.0 99.9 jit_solution(8370904344319640707)
XLA Ops:
  0.6 7.9 %spare.1 = bf16[256,896]{1,0:T(8,128)(2,1)} custom-call(s32[1,8]{1,0:T(1,128)} %counts.5, f32[1,512]{1,0:T(1,128)} %log_weights.3, f32[1,512]{1,0:T(1,128)} %bitcast.21, bf16[512,3072]{1,0:T(8,128)(2,1)} %bitcast.18, bf16[1536,512]{1,0:T(8,128)(2,1)} %w0.3, bf16[512,512]{1,0:T(8,128)(2,1)} %w1.3, bf16[512,3072]{1,0:T(8,128)(2,1)} %w2.3, ...), custom_call_target="tpu_custom_call" | custom-call | flops 671088640 | bytes 8912896 | tf_op jit(solution)/shard_map/spare/pallas_call | solution.py:408
  8.5 11.3 %all-to-all-start = ((bf16[32,8,896]{2,1,0:T(8,128)(2,1)}), bf16[32,8,896]{2,1,0:T(8,128)(2,1)S(1)}, u32[]{:S(2)}, u32[]{:S(2)}) async-start(bf16[32,8,896]{2,1,0:T(8,128)(2,1)} %bitcast.20), calls=%async_computation | async-start | bytes 917504 | tf_op jit(solution)/shard_map/all_to_all | solution.py:422
  19.9 0.0 copy-start.2
  19.9 0.0 copy-start.3
  19.9 0.0 copy-start.4
  19.9 0.0 copy-start.5
  19.9 13.1 %rows.1 = (bf16[512,3072]{1,0:T(8,128)(2,1)}, f32[8,512]{1,0:T(8,128)}, bf16[128,3072]{1,0:T(8,128)(2,1)}) custom-call(s32[1,8]{1,0:T(1,128)} %even.5, f32[1,512]{1,0:T(1,128)} %bitcast.22, bf16[512,3072]{1,0:T(8,128)(2,1)} %bitcast.19, bf16[1536,512]{1,0:T(8,128)(2,1)} %w0.3, bf16[512,512]{1,0:T(8,128)(2,1)} %w1.3, bf16[512,3072]{1,0:T(8,128)(2,1)} %w2.3, ...), custom_call_target="tpu_custom_call" | custom-call | flops 5368709120 | bytes 8912896 | tf_op jit(solution)/shard_map/rows/pallas_call | solution.py:430
  33.0 0.1 collective-permute-start.6
  33.1 2.1 %all-to-all-done = bf16[32,8,896]{2,1,0:T(8,128)(2,1)S(1)} async-done(((bf16[32,8,896]{2,1,0:T(8,128)(2,1)}), bf16[32,8,896]{2,1,0:T(8,128)(2,1)S(1)}, u32[]{:S(2)}, u32[]{:S(2)}) %all-to-all-start) | async-done | bytes 458784 | tf_op jit(solution)/shard_map/all_to_all | solution.py:422
  35.2 0.0 copy-done.2
  35.2 0.0 copy-done.3
  35.2 0.0 copy-done.4
  35.2 0.0 copy-start.1
  35.2 0.7 copy-done.1
  35.9 1.8 %route.1 = (bf16[256,768]{1,0:T(8,128)(2,1)}, f32[8,512]{1,0:T(8,128)S(1)}) custom-call(s32[1]{0:T(128)} %bitcast.me, s32[1,8]{1,0:T(1,128)S(1)} %copy-done.4, s32[1,8]{1,0:T(1,128)S(1)} %copy-done.3, f32[1,512]{1,0:T(1,128)S(1)} %copy-done.2, bf16[256,896]{1,0:T(8,128)(2,1)S(1)} %bitcast.11, f32[8,512]{1,0:T(8,128)S(1)} %copy-done.1), custom_call_target="tpu_custom_call" | custom-call | tf_op jit(solution)/shard_map/route/pallas_call | solution.py:463
  37.7 7.7 %all-to-all-start.1 = ((bf16[32,8,768]{2,1,0:T(8,128)(2,1)}), bf16[32,8,768]{2,1,0:T(8,128)(2,1)S(1)}, u32[]{:S(2)}, u32[]{:S(2)}) async-start(bf16[32,8,768]{2,1,0:T(8,128)(2,1)} %bitcast.5), calls=%async_computation.1 | async-start | bytes 786432 | tf_op jit(solution)/shard_map/all_to_all | solution.py:422
  45.4 0.0 collective-permute-done.6.received.from_even
  45.4 0.0 copy-done.5
  45.5 0.0 copy-start
  45.5 1.9 %copy-done = bf16[512,3072]{1,0:T(8,128)(2,1)S(1)} copy-done((bf16[512,3072]{1,0:T(8,128)(2,1)S(1)}, bf16[512,3072]{1,0:T(8,128)(2,1)}, u32[]{:S(2)}) %copy-start) | copy-done | bytes 3145752
  47.3 0.8 next.1
  48.2 2.2 %collective-permute-start.7 = (bf16[128,3072]{1,0:T(8,128)(2,1)S(1)}, bf16[128,3072]{1,0:T(8,128)(2,1)S(1)}, u32[]{:S(2)}, u32[]{:S(2)}) collective-permute-start(bf16[128,3072]{1,0:T(8,128)(2,1)S(1)} %next.1), channel_id=1, source_target_pairs={{32,64},{64,32},{96,128},{128,96},{160,192},{192,160},{33,65},{65,... | collective-permute-start | bytes 2359304 | tf_op jit(solution)/shard_map/ppermute | solution.py:426
  50.3 9.8 %all-to-all-done.1 = bf16[32,8,768]{2,1,0:T(8,128)(2,1)S(1)} async-done(((bf16[32,8,768]{2,1,0:T(8,128)(2,1)}), bf16[32,8,768]{2,1,0:T(8,128)(2,1)S(1)}, u32[]{:S(2)}, u32[]{:S(2)}) %all-to-all-start.1) | async-done | bytes 393248 | tf_op jit(solution)/shard_map/all_to_all | solution.py:422
  60.1 3.2 %collective-permute-start.5 = (bf16[256,768]{1,0:T(8,128)(2,1)S(1)}, bf16[256,768]{1,0:T(8,128)(2,1)S(1)}, u32[]{:S(2)}, u32[]{:S(2)}) collective-permute-start(bf16[256,768]{1,0:T(8,128)(2,1)S(1)} %bitcast.12), channel_id=1, source_target_pairs={{0,64},{96,32},{64,128},{160,96},{128,192},{224,160},{1,65},{97,33... | collective-permute-start | bytes 1179656 | tf_op jit(solution)/shard_map/ppermute | solution.py:426
  63.3 1.9 %collective-permute-start.4 = (bf16[256,768]{1,0:T(8,128)(2,1)S(1)}, bf16[256,768]{1,0:T(8,128)(2,1)S(1)}, u32[]{:S(2)}, u32[]{:S(2)}) collective-permute-start(bf16[256,768]{1,0:T(8,128)(2,1)S(1)} %bitcast.13), channel_id=1, source_target_pairs={{32,64},{64,32},{96,128},{128,96},{160,192},{192,160},{33,65},{65,... | collective-permute-start | bytes 1179656 | tf_op jit(solution)/shard_map/ppermute | solution.py:426
  65.3 0.1 collective-permute-start.3
  65.4 1.9 %collective-permute-start.2 = (f32[8,512]{1,0:T(8,128)S(1)}, f32[8,512]{1,0:T(8,128)S(1)}, u32[]{:S(2)}, u32[]{:S(2)}) collective-permute-start(f32[8,512]{1,0:T(8,128)S(1)} %get-tuple-element.14.own), channel_id=1, source_target_pairs={{0,64},{96,32},{64,128},{160,96},{128,192},{224,160},{1,65},{97,33... | collective-permute-start | bytes 49160 | tf_op jit(solution)/shard_map/ppermute | solution.py:426
  67.3 5.2 %collective-permute-done.2.from_both = f32[8,512]{1,0:T(8,128)S(1)} collective-permute-done((f32[8,512]{1,0:T(8,128)S(1)}, f32[8,512]{1,0:T(8,128)S(1)}, u32[]{:S(2)}, u32[]{:S(2)}) %collective-permute-start.2) | collective-permute-done | bytes 16416 | tf_op jit(solution)/shard_map/ppermute | solution.py:426
  72.4 1.9 %collective-permute-start.1 = (f32[8,512]{1,0:T(8,128)S(1)}, f32[8,512]{1,0:T(8,128)S(1)}, u32[]{:S(2)}, u32[]{:S(2)}) collective-permute-start(f32[8,512]{1,0:T(8,128)S(1)} %get-tuple-element.14.own), channel_id=1, source_target_pairs={{32,64},{64,32},{96,128},{128,96},{160,192},{192,160},{33,65},{65,... | collective-permute-start | bytes 49160 | tf_op jit(solution)/shard_map/ppermute | solution.py:426
  74.4 3.1 %collective-permute-done.1.from_odd = f32[8,512]{1,0:T(8,128)S(1)} collective-permute-done((f32[8,512]{1,0:T(8,128)S(1)}, f32[8,512]{1,0:T(8,128)S(1)}, u32[]{:S(2)}, u32[]{:S(2)}) %collective-permute-start.1) | collective-permute-done | bytes 16416 | tf_op jit(solution)/shard_map/ppermute | solution.py:426
  77.5 0.9 collective-permute-start
  79.0 0.2 collective-permute-done.from_even
  79.2 1.3 %stats.1 = (f32[1,512]{1,0:T(1,128)S(1)}, f32[256,128]{1,0:T(8,128)S(1)}, s32[1,8]{1,0:T(1,128)S(1)}) custom-call(s32[1,8]{1,0:T(1,128)S(1)} %copy-done.3, s32[1,8]{1,0:T(1,128)S(1)} %copy-done.5, f32[1]{0:T(128)S(6)} %copy.17.inverse_temp, f32[8,512]{1,0:T(8,128)S(1)} %get-tuple-element.14.own, f32[8,512]{1,0:T(8,128)S(1)} %collective-permute-done.from_even, ...), custom_call_target="tpu_custom_call" | custom-call | tf_op jit(solution)/shard_map/stats/pallas_call | solution.py:490
  80.5 16.6 %all_to_all.15 = f32[32,8,128]{2,1,0:T(8,128)S(1)} all-to-all(f32[32,8,128]{2,1,0:T(8,128)S(1)} %bitcast.17), channel_id=1, replica_groups=mesh['temp'=8,'dom'=32] {'dom'}, dimensions={0} | all-to-all | bytes 262144 | tf_op jit(solution)/shard_map/all_to_all | solution.py:422
  97.1 0.9 final.1
  98.0 0.0 collective-permute-done.7.from_odd
  98.0 0.0 collective-permute-done.5.late_both
  98.0 0.0 collective-permute-done.4.late_odd
  98.0 0.0 collective-permute-done.3.late_even
  98.0 1.9 %join.1 = bf16[512,3072]{1,0:T(8,128)(2,1)} custom-call(s32[1,8]{1,0:T(1,128)S(1)} %copy-done.4, s32[1,8]{1,0:T(1,128)S(1)} %copy-done.3, s32[1,8]{1,0:T(1,128)S(1)} %copy-done.5, s32[1,8]{1,0:T(1,128)S(1)} %get-tuple-element.15.marks, bf16[512,3072]{1,0:T(8,128)(2,1)} %get-tuple-element.16.rows.rows_in, ...), custom_call_target="tpu_custom_call", output_to_operand_aliasing={{}: (4, {})} | custom-call | tf_op jit(solution)/shard_map/join/pallas_call | solution.py:513
Async XLA Ops:
  8.5 26.6 %all-to-all-start = ((bf16[32,8,896]{2,1,0:T(8,128)(2,1)}), bf16[32,8,896]{2,1,0:T(8,128)(2,1)S(1)}, u32[]{:S(2)}, u32[]{:S(2)}) async-start(bf16[32,8,896]{2,1,0:T(8,128)(2,1)} %bitcast.20), calls=%async_computation | async-start | bytes 917504 | tf_op jit(solution)/shard_map/all_to_all | solution.py:422
  19.9 15.3 %copy-start.2 = (f32[1,512]{1,0:T(1,128)S(1)}, f32[1,512]{1,0:T(1,128)}, u32[]{:S(2)}) copy-start(f32[1,512]{1,0:T(1,128)} %log_weights.3) | copy-start | bytes 6148
  19.9 15.3 %copy-start.3 = (s32[1,8]{1,0:T(1,128)S(1)}, s32[1,8]{1,0:T(1,128)}, u32[]{:S(2)}) copy-start(s32[1,8]{1,0:T(1,128)} %even.5) | copy-start | bytes 100
  19.9 15.3 %copy-start.4 = (s32[1,8]{1,0:T(1,128)S(1)}, s32[1,8]{1,0:T(1,128)}, u32[]{:S(2)}) copy-start(s32[1,8]{1,0:T(1,128)} %counts.5) | copy-start | bytes 100
  19.9 25.5 %copy-start.5 = (s32[1,8]{1,0:T(1,128)S(1)}, s32[1,8]{1,0:T(1,128)}, u32[]{:S(2)}) copy-start(s32[1,8]{1,0:T(1,128)} %odd.5) | copy-start | bytes 100
  33.0 12.5 %collective-permute-start.6 = (bf16[128,3072]{1,0:T(8,128)(2,1)}, bf16[128,3072]{1,0:T(8,128)(2,1)S(1)}, u32[]{:S(2)}, u32[]{:S(2)}) collective-permute-start(bf16[128,3072]{1,0:T(8,128)(2,1)} %get-tuple-element.18), channel_id=1, source_target_pairs={{0,32},{32,0},{64,96},{96,64},{128,160},{160,128},{192,224},{224,1... | collective-permute-start | bytes 2359304 | tf_op jit(solution)/shard_map/ppermute | solution.py:426
  35.2 0.7 copy-start.1
  37.7 22.4 %all-to-all-start.1 = ((bf16[32,8,768]{2,1,0:T(8,128)(2,1)}), bf16[32,8,768]{2,1,0:T(8,128)(2,1)S(1)}, u32[]{:S(2)}, u32[]{:S(2)}) async-start(bf16[32,8,768]{2,1,0:T(8,128)(2,1)} %bitcast.5), calls=%async_computation.1 | async-start | bytes 786432 | tf_op jit(solution)/shard_map/all_to_all | solution.py:422
  45.5 1.9 %copy-start = (bf16[512,3072]{1,0:T(8,128)(2,1)S(1)}, bf16[512,3072]{1,0:T(8,128)(2,1)}, u32[]{:S(2)}) copy-start(bf16[512,3072]{1,0:T(8,128)(2,1)} %get-tuple-element.16.rows.rows_in) | copy-start | bytes 9437188
  48.2 49.8 %collective-permute-start.7 = (bf16[128,3072]{1,0:T(8,128)(2,1)S(1)}, bf16[128,3072]{1,0:T(8,128)(2,1)S(1)}, u32[]{:S(2)}, u32[]{:S(2)}) collective-permute-start(bf16[128,3072]{1,0:T(8,128)(2,1)S(1)} %next.1), channel_id=1, source_target_pairs={{32,64},{64,32},{96,128},{128,96},{160,192},{192,160},{33,65},{65,... | collective-permute-start | bytes 2359304 | tf_op jit(solution)/shard_map/ppermute | solution.py:426
  60.1 37.8 %collective-permute-start.5 = (bf16[256,768]{1,0:T(8,128)(2,1)S(1)}, bf16[256,768]{1,0:T(8,128)(2,1)S(1)}, u32[]{:S(2)}, u32[]{:S(2)}) collective-permute-start(bf16[256,768]{1,0:T(8,128)(2,1)S(1)} %bitcast.12), channel_id=1, source_target_pairs={{0,64},{96,32},{64,128},{160,96},{128,192},{224,160},{1,65},{97,33... | collective-permute-start | bytes 1179656 | tf_op jit(solution)/shard_map/ppermute | solution.py:426
  63.3 34.7 %collective-permute-start.4 = (bf16[256,768]{1,0:T(8,128)(2,1)S(1)}, bf16[256,768]{1,0:T(8,128)(2,1)S(1)}, u32[]{:S(2)}, u32[]{:S(2)}) collective-permute-start(bf16[256,768]{1,0:T(8,128)(2,1)S(1)} %bitcast.13), channel_id=1, source_target_pairs={{32,64},{64,32},{96,128},{128,96},{160,192},{192,160},{33,65},{65,... | collective-permute-start | bytes 1179656 | tf_op jit(solution)/shard_map/ppermute | solution.py:426
  65.3 32.7 %collective-permute-start.3 = (bf16[256,768]{1,0:T(8,128)(2,1)S(1)}, bf16[256,768]{1,0:T(8,128)(2,1)S(1)}, u32[]{:S(2)}, u32[]{:S(2)}) collective-permute-start(bf16[256,768]{1,0:T(8,128)(2,1)S(1)} %bitcast.14), channel_id=1, source_target_pairs={{0,32},{32,0},{64,96},{96,64},{128,160},{160,128},{192,224},{224,1... | collective-permute-start | bytes 1179656 | tf_op jit(solution)/shard_map/ppermute | solution.py:426
  65.4 7.1 %collective-permute-start.2 = (f32[8,512]{1,0:T(8,128)S(1)}, f32[8,512]{1,0:T(8,128)S(1)}, u32[]{:S(2)}, u32[]{:S(2)}) collective-permute-start(f32[8,512]{1,0:T(8,128)S(1)} %get-tuple-element.14.own), channel_id=1, source_target_pairs={{0,64},{96,32},{64,128},{160,96},{128,192},{224,160},{1,65},{97,33... | collective-permute-start | bytes 49160 | tf_op jit(solution)/shard_map/ppermute | solution.py:426
  72.4 5.0 %collective-permute-start.1 = (f32[8,512]{1,0:T(8,128)S(1)}, f32[8,512]{1,0:T(8,128)S(1)}, u32[]{:S(2)}, u32[]{:S(2)}) collective-permute-start(f32[8,512]{1,0:T(8,128)S(1)} %get-tuple-element.14.own), channel_id=1, source_target_pairs={{32,64},{64,32},{96,128},{128,96},{160,192},{192,160},{33,65},{65,... | collective-permute-start | bytes 49160 | tf_op jit(solution)/shard_map/ppermute | solution.py:426
  77.5 1.7 %collective-permute-start = (f32[8,512]{1,0:T(8,128)S(1)}, f32[8,512]{1,0:T(8,128)S(1)}, u32[]{:S(2)}, u32[]{:S(2)}) collective-permute-start(f32[8,512]{1,0:T(8,128)S(1)} %get-tuple-element.14.own), channel_id=1, source_target_pairs={{0,32},{32,0},{64,96},{96,64},{128,160},{160,128},{192,224},{224,1... | collective-permute-start | bytes 49160 | tf_op jit(solution)/shard_map/ppermute | solution.py:426

commit v5 on v4

--- a/solution.py
+++ b/solution.py
@@ -31,6 +31,10 @@
 
 def inside(x):
     return pltpu.with_memory_space_constraint(x, pltpu.VMEM)
+
+
+def outside(x):
+    return pltpu.with_memory_space_constraint(x, pltpu.HBM)
 
 
 def mul(a, b):
@@ -456,7 +460,7 @@
         name="next",
     )
     from_even_rows = inside(from_even_rows)
-    packed = follow(even_pairs, odd_pairs, done, from_even_rows)
+    packed = follow(even_pairs, odd_pairs, outside(done), from_even_rows)
     from_odd_rows = inside(swap(packed, odd))
 
     me = lax.axis_index("dom").astype(jnp.int32).reshape(1)
@@ -468,7 +472,7 @@
         scratch_shapes=[pltpu.VMEM((held_rows, LANES), F32)],
         compiler_params=pltpu.CompilerParams(vmem_limit_bytes=16 << 20),
         name="route",
-    )(me, offspring, even_pairs, log_weights, inside(held), scalars)
+    )(me, offspring, even_pairs, log_weights, inside(held), outside(scalars))
     filled = exchange(routed)
 
     from_even = swap(mine, even)

time: 101 us -> 99.9 us (0.989)
  local copies, waits for them, and re-layouts: 2.62 us -> 0.03 us
  waiting for transfers between devices: 20.4 us -> 21.5 us
    unnamed x12 -> x8, local copies, waits for them, and re-layouts: 2.62 us -> 0.03 us
    all_to_all x2, waiting for transfers between devices: 11.9 us -> 13 us  [exchange(): cut = lax.all_to_all(cut, 'dom', 0, 0, tiled=True)]
  transfers between devices with their start and end apart: 10 -> 10, of which waited for: 5 -> 5; matrix products, arithmetic and copies ran while one was open for 0% -> 0% of each run, Pallas kernels for 18% -> 19%
where the time goes in v5:
time: 99.9 us; the launch traced here: 99 us
  starting transfers between devices  31.2 us (31%)
  Pallas kernels  28.6 us (29%)
  waiting for transfers between devices  21.5 us (22%)
  blocking collectives  16.2 us (16%)
  between operations  1.48 us (1%)
    all_to_all x2, starting transfers between devices, exchange(): cut = lax.all_to_all(cut, 'dom', 0, 0, tiled=True)  19 us
    all_to_all x1, blocking collectives, exchange(): cut = lax.all_to_all(cut, 'dom', 0, 0, tiled=True)  16.2 us
    pallas_call x1, Pallas kernels, per_device(): pl.pallas_call(rows_kernel, out_shape=(shape((total, features), BF16), sh...  13 us
    all_to_all x2, waiting for transfers between devices, exchange(): cut = lax.all_to_all(cut, 'dom', 0, 0, tiled=True)  13 us
    ppermute x8, starting transfers between devices, swap(): return lax.ppermute(x, 'temp', pairs)  12.1 us
    ppermute x8, waiting for transfers between devices, swap(): return lax.ppermute(x, 'temp', pairs)  8.48 us
    pallas_call x1, Pallas kernels, per_device(): pl.pallas_call(spare_kernel, out_shape=shape((held_rows, width + LANES),...  7.91 us
  transfers between devices with their start and end apart: 10, of which 5 were waited for; matrix products, arithmetic and copies ran while one was open for 0% of the time, Pallas kernels for 19%

profile of v5, /device:TPU:16, one launch (start us, length us, event | category | flops | bytes accessed | tf_op | source)
XLA Modules:
  0.0 99.0 jit_solution(42984746107834393)
XLA Ops:
  0.6 7.9 %spare.1 = bf16[256,896]{1,0:T(8,128)(2,1)} custom-call(s32[1,8]{1,0:T(1,128)} %counts.5, f32[1,512]{1,0:T(1,128)} %log_weights.3, f32[1,512]{1,0:T(1,128)} %bitcast.21, bf16[512,3072]{1,0:T(8,128)(2,1)} %bitcast.18, bf16[1536,512]{1,0:T(8,128)(2,1)} %w0.3, bf16[512,512]{1,0:T(8,128)(2,1)} %w1.3, bf16[512,3072]{1,0:T(8,128)(2,1)} %w2.3, ...), custom_call_target="tpu_custom_call" | custom-call | flops 671088640 | bytes 8912896 | tf_op jit(solution)/shard_map/spare/pallas_call | solution.py:412
  8.5 11.3 %all-to-all-start = ((bf16[32,8,896]{2,1,0:T(8,128)(2,1)}), bf16[32,8,896]{2,1,0:T(8,128)(2,1)S(1)}, u32[]{:S(2)}, u32[]{:S(2)}) async-start(bf16[32,8,896]{2,1,0:T(8,128)(2,1)} %bitcast.20), calls=%async_computation | async-start | bytes 917504 | tf_op jit(solution)/shard_map/all_to_all | solution.py:426
  19.9 0.0 copy-start
  19.9 0.0 copy-start.1
  19.9 0.0 copy-start.2
  19.9 0.0 copy-start.3
  19.9 13.0 %rows.1 = (bf16[512,3072]{1,0:T(8,128)(2,1)}, f32[8,512]{1,0:T(8,128)}, bf16[128,3072]{1,0:T(8,128)(2,1)}) custom-call(s32[1,8]{1,0:T(1,128)} %even.5, f32[1,512]{1,0:T(1,128)} %bitcast.22, bf16[512,3072]{1,0:T(8,128)(2,1)} %bitcast.19, bf16[1536,512]{1,0:T(8,128)(2,1)} %w0.3, bf16[512,512]{1,0:T(8,128)(2,1)} %w1.3, bf16[512,3072]{1,0:T(8,128)(2,1)} %w2.3, ...), custom_call_target="tpu_custom_call" | custom-call | flops 5368709120 | bytes 8912896 | tf_op jit(solution)/shard_map/rows/pallas_call | solution.py:434
  33.0 0.1 collective-permute-start.6
  33.1 2.1 %all-to-all-done = bf16[32,8,896]{2,1,0:T(8,128)(2,1)S(1)} async-done(((bf16[32,8,896]{2,1,0:T(8,128)(2,1)}), bf16[32,8,896]{2,1,0:T(8,128)(2,1)S(1)}, u32[]{:S(2)}, u32[]{:S(2)}) %all-to-all-start) | async-done | bytes 458784 | tf_op jit(solution)/shard_map/all_to_all | solution.py:426
  35.2 0.0 copy-done
  35.2 0.0 copy-done.1
  35.2 0.0 copy-done.2
  35.2 2.0 %route.1 = (bf16[256,768]{1,0:T(8,128)(2,1)}, f32[8,512]{1,0:T(8,128)S(1)}) custom-call(s32[1]{0:T(128)} %bitcast.me, s32[1,8]{1,0:T(1,128)S(1)} %copy-done.2, s32[1,8]{1,0:T(1,128)S(1)} %copy-done.1, f32[1,512]{1,0:T(1,128)S(1)} %copy-done, bf16[256,896]{1,0:T(8,128)(2,1)S(1)} %bitcast.10, f32[8,512]{1,0:T(8,128)} %get-tuple-element.13.scalars), custom_call_target="tpu_custom_call" | custom-call | tf_op jit(solution)/shard_map/route/pallas_call | solution.py:467
  37.2 7.7 %all-to-all-start.1 = ((bf16[32,8,768]{2,1,0:T(8,128)(2,1)}), bf16[32,8,768]{2,1,0:T(8,128)(2,1)S(1)}, u32[]{:S(2)}, u32[]{:S(2)}) async-start(bf16[32,8,768]{2,1,0:T(8,128)(2,1)} %bitcast.5), calls=%async_computation.1 | async-start | bytes 786432 | tf_op jit(solution)/shard_map/all_to_all | solution.py:426
  44.9 0.0 collective-permute-done.6.received.from_even
  44.9 0.0 copy-done.3
  44.9 1.6 %next.1 = bf16[128,3072]{1,0:T(8,128)(2,1)S(1)} custom-call(s32[1,8]{1,0:T(1,128)S(1)} %copy-done.1, s32[1,8]{1,0:T(1,128)S(1)} %copy-done.3, bf16[512,3072]{1,0:T(8,128)(2,1)} %get-tuple-element.16.rows.rows_in, bf16[128,3072]{1,0:T(8,128)(2,1)S(1)} %collective-permute-done.6.received.from_even), custom_call_target="tpu_custom_call" | custom-call | tf_op jit(solution)/shard_map/next/pallas_call | solution.py:463
  46.5 2.2 %collective-permute-start.7 = (bf16[128,3072]{1,0:T(8,128)(2,1)S(1)}, bf16[128,3072]{1,0:T(8,128)(2,1)S(1)}, u32[]{:S(2)}, u32[]{:S(2)}) collective-permute-start(bf16[128,3072]{1,0:T(8,128)(2,1)S(1)} %next.1), channel_id=1, source_target_pairs={{32,64},{64,32},{96,128},{128,96},{160,192},{192,160},{33,65},{65,... | collective-permute-start | bytes 2359304 | tf_op jit(solution)/shard_map/ppermute | solution.py:430
  48.7 10.9 %all-to-all-done.1 = bf16[32,8,768]{2,1,0:T(8,128)(2,1)S(1)} async-done(((bf16[32,8,768]{2,1,0:T(8,128)(2,1)}), bf16[32,8,768]{2,1,0:T(8,128)(2,1)S(1)}, u32[]{:S(2)}, u32[]{:S(2)}) %all-to-all-start.1) | async-done | bytes 393248 | tf_op jit(solution)/shard_map/all_to_all | solution.py:426
  59.6 3.2 %collective-permute-start.5 = (bf16[256,768]{1,0:T(8,128)(2,1)S(1)}, bf16[256,768]{1,0:T(8,128)(2,1)S(1)}, u32[]{:S(2)}, u32[]{:S(2)}) collective-permute-start(bf16[256,768]{1,0:T(8,128)(2,1)S(1)} %bitcast.11), channel_id=1, source_target_pairs={{0,64},{96,32},{64,128},{160,96},{128,192},{224,160},{1,65},{97,33... | collective-permute-start | bytes 1179656 | tf_op jit(solution)/shard_map/ppermute | solution.py:430
  62.8 1.9 %collective-permute-start.4 = (bf16[256,768]{1,0:T(8,128)(2,1)S(1)}, bf16[256,768]{1,0:T(8,128)(2,1)S(1)}, u32[]{:S(2)}, u32[]{:S(2)}) collective-permute-start(bf16[256,768]{1,0:T(8,128)(2,1)S(1)} %bitcast.12), channel_id=1, source_target_pairs={{32,64},{64,32},{96,128},{128,96},{160,192},{192,160},{33,65},{65,... | collective-permute-start | bytes 1179656 | tf_op jit(solution)/shard_map/ppermute | solution.py:430
  64.7 0.1 collective-permute-start.3
  64.8 1.9 %collective-permute-start.2 = (f32[8,512]{1,0:T(8,128)S(1)}, f32[8,512]{1,0:T(8,128)S(1)}, u32[]{:S(2)}, u32[]{:S(2)}) collective-permute-start(f32[8,512]{1,0:T(8,128)S(1)} %get-tuple-element.14.own), channel_id=1, source_target_pairs={{0,64},{96,32},{64,128},{160,96},{128,192},{224,160},{1,65},{97,33... | collective-permute-start | bytes 49160 | tf_op jit(solution)/shard_map/ppermute | solution.py:430
  66.8 5.2 %collective-permute-done.2.from_both = f32[8,512]{1,0:T(8,128)S(1)} collective-permute-done((f32[8,512]{1,0:T(8,128)S(1)}, f32[8,512]{1,0:T(8,128)S(1)}, u32[]{:S(2)}, u32[]{:S(2)}) %collective-permute-start.2) | collective-permute-done | bytes 16416 | tf_op jit(solution)/shard_map/ppermute | solution.py:430
  71.9 1.9 %collective-permute-start.1 = (f32[8,512]{1,0:T(8,128)S(1)}, f32[8,512]{1,0:T(8,128)S(1)}, u32[]{:S(2)}, u32[]{:S(2)}) collective-permute-start(f32[8,512]{1,0:T(8,128)S(1)} %get-tuple-element.14.own), channel_id=1, source_target_pairs={{32,64},{64,32},{96,128},{128,96},{160,192},{192,160},{33,65},{65,... | collective-permute-start | bytes 49160 | tf_op jit(solution)/shard_map/ppermute | solution.py:430
  73.8 3.1 %collective-permute-done.1.from_odd = f32[8,512]{1,0:T(8,128)S(1)} collective-permute-done((f32[8,512]{1,0:T(8,128)S(1)}, f32[8,512]{1,0:T(8,128)S(1)}, u32[]{:S(2)}, u32[]{:S(2)}) %collective-permute-start.1) | collective-permute-done | bytes 16416 | tf_op jit(solution)/shard_map/ppermute | solution.py:430
  77.0 0.9 collective-permute-start
  78.5 0.2 collective-permute-done.from_even
  78.7 1.3 %stats.1 = (f32[1,512]{1,0:T(1,128)S(1)}, f32[256,128]{1,0:T(8,128)S(1)}, s32[1,8]{1,0:T(1,128)S(1)}) custom-call(s32[1,8]{1,0:T(1,128)S(1)} %copy-done.1, s32[1,8]{1,0:T(1,128)S(1)} %copy-done.3, f32[1]{0:T(128)S(6)} %copy.17.inverse_temp, f32[8,512]{1,0:T(8,128)S(1)} %get-tuple-element.14.own, f32[8,512]{1,0:T(8,128)S(1)} %collective-permute-done.from_even, ...), custom_call_target="tpu_custom_call" | custom-call | tf_op jit(solution)/shard_map/stats/pallas_call | solution.py:494
  80.0 16.2 %all_to_all.15 = f32[32,8,128]{2,1,0:T(8,128)S(1)} all-to-all(f32[32,8,128]{2,1,0:T(8,128)S(1)} %bitcast.16), channel_id=1, replica_groups=mesh['temp'=8,'dom'=32] {'dom'}, dimensions={0} | all-to-all | bytes 262144 | tf_op jit(solution)/shard_map/all_to_all | solution.py:426
  96.2 0.9 final.1
  97.1 0.0 collective-permute-done.7.from_odd
  97.1 0.0 collective-permute-done.5.late_both
  97.1 0.0 collective-permute-done.4.late_odd
  97.1 0.0 collective-permute-done.3.late_even
  97.1 1.9 %join.1 = bf16[512,3072]{1,0:T(8,128)(2,1)} custom-call(s32[1,8]{1,0:T(1,128)S(1)} %copy-done.2, s32[1,8]{1,0:T(1,128)S(1)} %copy-done.1, s32[1,8]{1,0:T(1,128)S(1)} %copy-done.3, s32[1,8]{1,0:T(1,128)S(1)} %get-tuple-element.15.marks, bf16[512,3072]{1,0:T(8,128)(2,1)} %get-tuple-element.16.rows.rows_in, ...), custom_call_target="tpu_custom_call", output_to_operand_aliasing={{}: (4, {})} | custom-call | tf_op jit(solution)/shard_map/join/pallas_call | solution.py:517
Async XLA Ops:
  8.5 26.6 %all-to-all-start = ((bf16[32,8,896]{2,1,0:T(8,128)(2,1)}), bf16[32,8,896]{2,1,0:T(8,128)(2,1)S(1)}, u32[]{:S(2)}, u32[]{:S(2)}) async-start(bf16[32,8,896]{2,1,0:T(8,128)(2,1)} %bitcast.20), calls=%async_computation | async-start | bytes 917504 | tf_op jit(solution)/shard_map/all_to_all | solution.py:426
  19.9 15.3 %copy-start = (f32[1,512]{1,0:T(1,128)S(1)}, f32[1,512]{1,0:T(1,128)}, u32[]{:S(2)}) copy-start(f32[1,512]{1,0:T(1,128)} %log_weights.3) | copy-start | bytes 6148
  19.9 15.3 %copy-start.1 = (s32[1,8]{1,0:T(1,128)S(1)}, s32[1,8]{1,0:T(1,128)}, u32[]{:S(2)}) copy-start(s32[1,8]{1,0:T(1,128)} %even.5) | copy-start | bytes 100
  19.9 15.3 %copy-start.2 = (s32[1,8]{1,0:T(1,128)S(1)}, s32[1,8]{1,0:T(1,128)}, u32[]{:S(2)}) copy-start(s32[1,8]{1,0:T(1,128)} %counts.5) | copy-start | bytes 100
  19.9 25.0 %copy-start.3 = (s32[1,8]{1,0:T(1,128)S(1)}, s32[1,8]{1,0:T(1,128)}, u32[]{:S(2)}) copy-start(s32[1,8]{1,0:T(1,128)} %odd.5) | copy-start | bytes 100
  33.0 11.9 %collective-permute-start.6 = (bf16[128,3072]{1,0:T(8,128)(2,1)}, bf16[128,3072]{1,0:T(8,128)(2,1)S(1)}, u32[]{:S(2)}, u32[]{:S(2)}) collective-permute-start(bf16[128,3072]{1,0:T(8,128)(2,1)} %get-tuple-element.18), channel_id=1, source_target_pairs={{0,32},{32,0},{64,96},{96,64},{128,160},{160,128},{192,224},{224,1... | collective-permute-start | bytes 2359304 | tf_op jit(solution)/shard_map/ppermute | solution.py:430
  37.2 22.4 %all-to-all-start.1 = ((bf16[32,8,768]{2,1,0:T(8,128)(2,1)}), bf16[32,8,768]{2,1,0:T(8,128)(2,1)S(1)}, u32[]{:S(2)}, u32[]{:S(2)}) async-start(bf16[32,8,768]{2,1,0:T(8,128)(2,1)} %bitcast.5), calls=%async_computation.1 | async-start | bytes 786432 | tf_op jit(solution)/shard_map/all_to_all | solution.py:426
  46.5 50.6 %collective-permute-start.7 = (bf16[128,3072]{1,0:T(8,128)(2,1)S(1)}, bf16[128,3072]{1,0:T(8,128)(2,1)S(1)}, u32[]{:S(2)}, u32[]{:S(2)}) collective-permute-start(bf16[128,3072]{1,0:T(8,128)(2,1)S(1)} %next.1), channel_id=1, source_target_pairs={{32,64},{64,32},{96,128},{128,96},{160,192},{192,160},{33,65},{65,... | collective-permute-start | bytes 2359304 | tf_op jit(solution)/shard_map/ppermute | solution.py:430
  59.6 37.5 %collective-permute-start.5 = (bf16[256,768]{1,0:T(8,128)(2,1)S(1)}, bf16[256,768]{1,0:T(8,128)(2,1)S(1)}, u32[]{:S(2)}, u32[]{:S(2)}) collective-permute-start(bf16[256,768]{1,0:T(8,128)(2,1)S(1)} %bitcast.11), channel_id=1, source_target_pairs={{0,64},{96,32},{64,128},{160,96},{128,192},{224,160},{1,65},{97,33... | collective-permute-start | bytes 1179656 | tf_op jit(solution)/shard_map/ppermute | solution.py:430
  62.8 34.3 %collective-permute-start.4 = (bf16[256,768]{1,0:T(8,128)(2,1)S(1)}, bf16[256,768]{1,0:T(8,128)(2,1)S(1)}, u32[]{:S(2)}, u32[]{:S(2)}) collective-permute-start(bf16[256,768]{1,0:T(8,128)(2,1)S(1)} %bitcast.12), channel_id=1, source_target_pairs={{32,64},{64,32},{96,128},{128,96},{160,192},{192,160},{33,65},{65,... | collective-permute-start | bytes 1179656 | tf_op jit(solution)/shard_map/ppermute | solution.py:430
  64.7 32.4 %collective-permute-start.3 = (bf16[256,768]{1,0:T(8,128)(2,1)S(1)}, bf16[256,768]{1,0:T(8,128)(2,1)S(1)}, u32[]{:S(2)}, u32[]{:S(2)}) collective-permute-start(bf16[256,768]{1,0:T(8,128)(2,1)S(1)} %bitcast.13), channel_id=1, source_target_pairs={{0,32},{32,0},{64,96},{96,64},{128,160},{160,128},{192,224},{224,1... | collective-permute-start | bytes 1179656 | tf_op jit(solution)/shard_map/ppermute | solution.py:430
  64.8 7.1 %collective-permute-start.2 = (f32[8,512]{1,0:T(8,128)S(1)}, f32[8,512]{1,0:T(8,128)S(1)}, u32[]{:S(2)}, u32[]{:S(2)}) collective-permute-start(f32[8,512]{1,0:T(8,128)S(1)} %get-tuple-element.14.own), channel_id=1, source_target_pairs={{0,64},{96,32},{64,128},{160,96},{128,192},{224,160},{1,65},{97,33... | collective-permute-start | bytes 49160 | tf_op jit(solution)/shard_map/ppermute | solution.py:430
  71.9 5.0 %collective-permute-start.1 = (f32[8,512]{1,0:T(8,128)S(1)}, f32[8,512]{1,0:T(8,128)S(1)}, u32[]{:S(2)}, u32[]{:S(2)}) collective-permute-start(f32[8,512]{1,0:T(8,128)S(1)} %get-tuple-element.14.own), channel_id=1, source_target_pairs={{32,64},{64,32},{96,128},{128,96},{160,192},{192,160},{33,65},{65,... | collective-permute-start | bytes 49160 | tf_op jit(solution)/shard_map/ppermute | solution.py:430
  77.0 1.7 %collective-permute-start = (f32[8,512]{1,0:T(8,128)S(1)}, f32[8,512]{1,0:T(8,128)S(1)}, u32[]{:S(2)}, u32[]{:S(2)}) collective-permute-start(f32[8,512]{1,0:T(8,128)S(1)} %get-tuple-element.14.own), channel_id=1, source_target_pairs={{0,32},{32,0},{64,96},{96,64},{128,160},{160,128},{192,224},{224,1... | collective-permute-start | bytes 49160 | tf_op jit(solution)/shard_map/ppermute | solution.py:430

commit v6 on v3

--- a/solution.py
+++ b/solution.py
@@ -31,6 +31,10 @@
 
 def inside(x):
     return pltpu.with_memory_space_constraint(x, pltpu.VMEM)
+
+
+def outside(x):
+    return pltpu.with_memory_space_constraint(x, pltpu.HBM)
 
 
 def mul(a, b):
@@ -123,7 +127,7 @@
         particles.at[pl.ds(pl.multiple_of(slot * block_rows, block_rows), block_rows), :], rows, row_sem
     )
     own.start()
-    for copy in copies:
+    for copy in copies[:3]:
         copy.start()
     own.wait()
     width = rows.shape[1] // 4
@@ -136,9 +140,13 @@
             out[c * block_rows : (c + 1) * block_rows, start : start + size] = moved[:, done : done + size]
             done += size
 
-    log_det, level = step_rows(
-        rows, scratch, read_out[...], lambda i: copies[i].wait(), keep, width
-    )
+    def ready(i):
+        copies[i].wait()
+        if i == 0:
+            copies[3].start()
+            copies[4].start()
+
+    log_det, level = step_rows(rows, scratch, read_out[...], ready, keep, width)
     for c in range(2):
         out[c * block_rows : (c + 1) * block_rows, :width] = rows[:, c * width : (c + 1) * width]
     lane = lax.broadcasted_iota(jnp.int32, (block_rows, LANES), 1)
@@ -444,8 +452,9 @@
         in_specs=[SMEM, SMEM, SMEM, VMEM, VMEM, VMEM],
         out_specs=(VMEM, VMEM),
         scratch_shapes=[pltpu.VMEM((held_rows, LANES), F32)],
+        compiler_params=pltpu.CompilerParams(vmem_limit_bytes=16 << 20),
         name="route",
-    )(me, offspring, even_pairs, log_weights, inside(held), scalars)
+    )(me, offspring, even_pairs, log_weights, inside(held), outside(scalars))
     filled = exchange(routed)
 
     from_even = swap(mine, even)
@@ -456,6 +465,7 @@
         out_shape=(shape((1, total), F32), shape((held_rows, LANES), F32)),
         in_specs=[SMEM, SMEM, SMEM, VMEM, VMEM, VMEM, VMEM],
         out_specs=(VMEM, VMEM),
+        compiler_params=pltpu.CompilerParams(vmem_limit_bytes=8 << 20),
         name="stats",
     )
     lines = [inside(line) for line in (from_even, from_odd, from_both)]
@@ -466,6 +476,7 @@
         out_shape=(shape((1, total), F32), shape((1,), F32)),
         in_specs=[VMEM, VMEM],
         out_specs=(VMEM, SMEM),
+        compiler_params=pltpu.CompilerParams(vmem_limit_bytes=8 << 20),
         name="final",
     )
     new_log_weights, log_ess = close(updated, inside(stats))
@@ -479,13 +490,14 @@
         out_specs=(ANY, VMEM),
         scratch_shapes=[pltpu.SemaphoreType.DMA((8 + 2 * SWAPS,))],
         input_output_aliases={4: 0},
+        compiler_params=pltpu.CompilerParams(vmem_limit_bytes=8 << 20),
         name="join",
     )(
         offspring,
         other_counts,
         even_pairs,
         odd_pairs,
-        done,
+        outside(done),
         inside(filled),
         inside(filled_other),
         inside(received),
@@ -499,8 +511,9 @@
         out_specs=ANY,
         scratch_shapes=[pltpu.SemaphoreType.DMA((SWAPS,))],
         input_output_aliases={1: 0},
+        compiler_params=pltpu.CompilerParams(vmem_limit_bytes=8 << 20),
         name="odd",
-    )(odd_pairs, done, inside(received))
+    )(odd_pairs, outside(done), inside(received))
     return done.reshape(1, total, features), new_log_weights, log_ess
 
 

time: 94.6 us -> 90.9 us (0.961)
  Pallas kernels: 30.5 us -> 27.5 us
    pallas_call x1, Pallas kernels: 3.03 us -> 2.02 us  [per_device(): pl.pallas_call(join_kernel, out_shape=(whole, pack), in_specs=[SMEM] * 4...]
  transfers between devices with their start and end apart: 9 -> 9, of which waited for: 3 -> 3; matrix products, arithmetic and copies ran while one was open for 0% -> 0% of each run, Pallas kernels for 17% -> 16%
where the time goes in v6:
time: 90.9 us; the launch traced here: 89.1 us
  Pallas kernels  27.5 us (30%)
  starting transfers between devices  26.9 us (30%)
  waiting for transfers between devices  17.8 us (20%)
  blocking collectives  15.5 us (17%)
  between operations  1.46 us (2%)
    all_to_all x2, starting transfers between devices, exchange(): cut = lax.all_to_all(cut, 'dom', 0, 0, tiled=True)  18.9 us
    all_to_all x2, waiting for transfers between devices, exchange(): cut = lax.all_to_all(cut, 'dom', 0, 0, tiled=True)  16 us
    all_to_all x1, blocking collectives, exchange(): cut = lax.all_to_all(cut, 'dom', 0, 0, tiled=True)  15.5 us
    pallas_call x1, Pallas kernels, per_device(): pl.pallas_call(rows_kernel, out_shape=(shape((total, features), BF16), sh...  13 us
    ppermute x7, starting transfers between devices, swap(): return lax.ppermute(x, 'temp', pairs)  7.92 us
    pallas_call x1, Pallas kernels, per_device(): pl.pallas_call(spare_kernel, out_shape=shape((held_rows, width + LANES),...  7.43 us
    pallas_call x1, Pallas kernels, per_device(): pl.pallas_call(join_kernel, out_shape=(whole, pack), in_specs=[SMEM] * 4...  2.02 us
    pallas_call x1, Pallas kernels, per_device(): pl.pallas_call(route_kernel, out_shape=(shape((held_rows, width), BF16),...  1.99 us
  transfers between devices with their start and end apart: 9, of which 3 were waited for; matrix products, arithmetic and copies ran while one was open for 0% of the time, Pallas kernels for 16%

profile of v6, /device:TPU:16, one launch (start us, length us, event | category | flops | bytes accessed | tf_op | source)
XLA Modules:
  0.0 89.1 jit_solution(11612441861715633911)
XLA Ops:
  0.6 7.4 %spare.1 = bf16[256,896]{1,0:T(8,128)(2,1)} custom-call(s32[1,8]{1,0:T(1,128)} %counts.5, f32[1,512]{1,0:T(1,128)} %log_weights.3, f32[1,512]{1,0:T(1,128)} %bitcast.19, bf16[512,3072]{1,0:T(8,128)(2,1)} %bitcast.16, bf16[1536,512]{1,0:T(8,128)(2,1)} %w0.3, bf16[512,512]{1,0:T(8,128)(2,1)} %w1.3, bf16[512,3072]{1,0:T(8,128)(2,1)} %w2.3, ...), custom_call_target="tpu_custom_call" | custom-call | flops 671088640 | bytes 8912896 | tf_op jit(solution)/shard_map/spare/pallas_call | solution.py:405
  8.1 11.3 %all-to-all-start = ((bf16[32,8,896]{2,1,0:T(8,128)(2,1)}), bf16[32,8,896]{2,1,0:T(8,128)(2,1)S(1)}, u32[]{:S(2)}, u32[]{:S(2)}) async-start(bf16[32,8,896]{2,1,0:T(8,128)(2,1)} %bitcast.18), calls=%async_computation | async-start | bytes 917504 | tf_op jit(solution)/shard_map/all_to_all | solution.py:419
  19.4 0.0 copy-start
  19.4 0.0 copy-start.1
  19.4 0.0 copy-start.2
  19.4 0.0 copy-start.3
  19.5 13.0 %rows.1 = (bf16[512,3072]{1,0:T(8,128)(2,1)}, f32[8,512]{1,0:T(8,128)}, bf16[128,3072]{1,0:T(8,128)(2,1)}) custom-call(s32[1,8]{1,0:T(1,128)} %even.3, f32[1,512]{1,0:T(1,128)} %bitcast.20, bf16[512,3072]{1,0:T(8,128)(2,1)} %bitcast.17, bf16[1536,512]{1,0:T(8,128)(2,1)} %w0.3, bf16[512,512]{1,0:T(8,128)(2,1)} %w1.3, bf16[512,3072]{1,0:T(8,128)(2,1)} %w2.3, ...), custom_call_target="tpu_custom_call" | custom-call | flops 5368709120 | bytes 8912896 | tf_op jit(solution)/shard_map/rows/pallas_call | solution.py:427
  32.5 2.2 %all-to-all-done = bf16[32,8,896]{2,1,0:T(8,128)(2,1)S(1)} async-done(((bf16[32,8,896]{2,1,0:T(8,128)(2,1)}), bf16[32,8,896]{2,1,0:T(8,128)(2,1)S(1)}, u32[]{:S(2)}, u32[]{:S(2)}) %all-to-all-start) | async-done | bytes 458784 | tf_op jit(solution)/shard_map/all_to_all | solution.py:419
  34.7 0.0 copy-done
  34.7 0.0 copy-done.1
  34.7 0.0 copy-done.2
  34.7 2.0 %route.1 = (bf16[256,768]{1,0:T(8,128)(2,1)}, f32[8,512]{1,0:T(8,128)S(1)}) custom-call(s32[1]{0:T(128)} %bitcast.2.me, s32[1,8]{1,0:T(1,128)S(1)} %copy-done.1, s32[1,8]{1,0:T(1,128)S(1)} %copy-done.2, f32[1,512]{1,0:T(1,128)S(1)} %copy-done, bf16[256,896]{1,0:T(8,128)(2,1)S(1)} %bitcast.10, f32[8,512]{1,0:T(8,128)} %get-tuple-element.15.scalars), custom_call_target="tpu_custom_call" | custom-call | tf_op jit(solution)/shard_map/route/pallas_call | solution.py:449
  36.7 7.6 %all-to-all-start.1 = ((bf16[32,8,768]{2,1,0:T(8,128)(2,1)}), bf16[32,8,768]{2,1,0:T(8,128)(2,1)S(1)}, u32[]{:S(2)}, u32[]{:S(2)}) async-start(bf16[32,8,768]{2,1,0:T(8,128)(2,1)} %bitcast.5), calls=%async_computation.1 | async-start | bytes 786432 | tf_op jit(solution)/shard_map/all_to_all | solution.py:419
  44.3 0.1 collective-permute-start.2
  44.4 13.8 %all-to-all-done.1 = bf16[32,8,768]{2,1,0:T(8,128)(2,1)S(1)} async-done(((bf16[32,8,768]{2,1,0:T(8,128)(2,1)}), bf16[32,8,768]{2,1,0:T(8,128)(2,1)S(1)}, u32[]{:S(2)}, u32[]{:S(2)}) %all-to-all-start.1) | async-done | bytes 393248 | tf_op jit(solution)/shard_map/all_to_all | solution.py:419
  58.2 0.0 collective-permute-start.1
  58.2 3.2 %collective-permute-start.5 = (f32[8,512]{1,0:T(8,128)S(1)}, f32[8,512]{1,0:T(8,128)S(1)}, u32[]{:S(2)}, u32[]{:S(2)}) collective-permute-start(f32[8,512]{1,0:T(8,128)S(1)} %get-tuple-element.18.own), channel_id=1, source_target_pairs={{0,64},{96,32},{64,128},{160,96},{128,192},{224,160},{1,65},{97,33... | collective-permute-start | bytes 49160 | tf_op jit(solution)/shard_map/ppermute | solution.py:423
  61.4 1.9 %collective-permute-start.4 = (f32[8,512]{1,0:T(8,128)S(1)}, f32[8,512]{1,0:T(8,128)S(1)}, u32[]{:S(2)}, u32[]{:S(2)}) collective-permute-start(f32[8,512]{1,0:T(8,128)S(1)} %get-tuple-element.18.own), channel_id=1, source_target_pairs={{32,64},{64,32},{96,128},{128,96},{160,192},{192,160},{33,65},{65,... | collective-permute-start | bytes 49160 | tf_op jit(solution)/shard_map/ppermute | solution.py:423
  63.3 0.1 collective-permute-start.3
  64.1 0.0 collective-permute-done.5.from_both
  64.1 0.6 collective-permute-start
  64.7 1.8 %collective-permute-done.4.from_odd = f32[8,512]{1,0:T(8,128)S(1)} collective-permute-done((f32[8,512]{1,0:T(8,128)S(1)}, f32[8,512]{1,0:T(8,128)S(1)}, u32[]{:S(2)}, u32[]{:S(2)}) %collective-permute-start.4) | collective-permute-done | bytes 16416 | tf_op jit(solution)/shard_map/ppermute | solution.py:423
  66.4 0.0 collective-permute-done.3.from_even
  66.4 0.0 copy-done.3
  66.4 0.7 stats.1
  67.2 0.0 collective-permute-done.other_counts
  67.2 0.0 collective-permute-done.2.received
  67.2 0.0 collective-permute-done.1.filled_other
  67.2 2.0 %join.1 = (bf16[512,3072]{1,0:T(8,128)(2,1)}, bf16[128,3072]{1,0:T(8,128)(2,1)S(1)}) custom-call(s32[1,8]{1,0:T(1,128)S(1)} %copy-done.1, s32[1,8]{1,0:T(1,128)S(1)} %collective-permute-done.other_counts, s32[1,8]{1,0:T(1,128)S(1)} %copy-done.2, s32[1,8]{1,0:T(1,128)S(1)} %copy-done.3, ...), custom_call_target="tpu_custom_call", output_to_operand_aliasing={{0}: (4, {})} | custom-call | tf_op jit(solution)/shard_map/join/pallas_call | solution.py:486
  69.3 2.0 %collective-permute-start.6 = (bf16[128,3072]{1,0:T(8,128)(2,1)S(1)}, bf16[128,3072]{1,0:T(8,128)(2,1)S(1)}, u32[]{:S(2)}, u32[]{:S(2)}) collective-permute-start(bf16[128,3072]{1,0:T(8,128)(2,1)S(1)} %get-tuple-element.21), channel_id=1, source_target_pairs={{32,64},{64,32},{96,128},{128,96},{160,192},{192,160},{33,65},{65,... | collective-permute-start | bytes 2359304 | tf_op jit(solution)/shard_map/ppermute | solution.py:423
  71.3 15.5 %all_to_all.15 = f32[32,8,128]{2,1,0:T(8,128)S(1)} all-to-all(f32[32,8,128]{2,1,0:T(8,128)S(1)} %bitcast.14), channel_id=1, replica_groups=mesh['temp'=8,'dom'=32] {'dom'}, dimensions={0} | all-to-all | bytes 262144 | tf_op jit(solution)/shard_map/all_to_all | solution.py:419
  86.9 0.9 %final.1 = (f32[1,512]{1,0:T(1,128)}, f32[1]{0:T(128)}) custom-call(f32[1,512]{1,0:T(1,128)S(1)} %get-tuple-element.19.later.updated, f32[256,128]{1,0:T(8,128)S(1)} %bitcast.13), custom_call_target="tpu_custom_call" | custom-call | tf_op jit(solution)/shard_map/final/pallas_call | solution.py:482
  87.8 0.0 collective-permute-done.6.received
  87.8 1.3 %odd.5 = bf16[512,3072]{1,0:T(8,128)(2,1)} custom-call(s32[1,8]{1,0:T(1,128)S(1)} %copy-done.3, bf16[512,3072]{1,0:T(8,128)(2,1)} %get-tuple-element.20.rows_in, bf16[128,3072]{1,0:T(8,128)(2,1)S(1)} %collective-permute-done.6.received), custom_call_target="tpu_custom_call", output_to_operand_aliasing={{}: (1, {})} | custom-call | tf_op jit(solution)/shard_map/odd/pallas_call | solution.py:507
Async XLA Ops:
  8.1 26.6 %all-to-all-start = ((bf16[32,8,896]{2,1,0:T(8,128)(2,1)}), bf16[32,8,896]{2,1,0:T(8,128)(2,1)S(1)}, u32[]{:S(2)}, u32[]{:S(2)}) async-start(bf16[32,8,896]{2,1,0:T(8,128)(2,1)} %bitcast.18), calls=%async_computation | async-start | bytes 917504 | tf_op jit(solution)/shard_map/all_to_all | solution.py:419
  19.4 15.3 %copy-start = (f32[1,512]{1,0:T(1,128)S(1)}, f32[1,512]{1,0:T(1,128)}, u32[]{:S(2)}) copy-start(f32[1,512]{1,0:T(1,128)} %log_weights.3) | copy-start | bytes 6148
  19.4 15.3 %copy-start.1 = (s32[1,8]{1,0:T(1,128)S(1)}, s32[1,8]{1,0:T(1,128)}, u32[]{:S(2)}) copy-start(s32[1,8]{1,0:T(1,128)} %counts.5) | copy-start | bytes 100
  19.4 15.3 %copy-start.2 = (s32[1,8]{1,0:T(1,128)S(1)}, s32[1,8]{1,0:T(1,128)}, u32[]{:S(2)}) copy-start(s32[1,8]{1,0:T(1,128)} %even.3) | copy-start | bytes 100
  19.4 47.0 %copy-start.3 = (s32[1,8]{1,0:T(1,128)S(1)}, s32[1,8]{1,0:T(1,128)}, u32[]{:S(2)}) copy-start(s32[1,8]{1,0:T(1,128)} %flags.1) | copy-start | bytes 100
  36.7 21.5 %all-to-all-start.1 = ((bf16[32,8,768]{2,1,0:T(8,128)(2,1)}), bf16[32,8,768]{2,1,0:T(8,128)(2,1)S(1)}, u32[]{:S(2)}, u32[]{:S(2)}) async-start(bf16[32,8,768]{2,1,0:T(8,128)(2,1)} %bitcast.5), calls=%async_computation.1 | async-start | bytes 786432 | tf_op jit(solution)/shard_map/all_to_all | solution.py:419
  44.3 22.9 %collective-permute-start.2 = (bf16[128,3072]{1,0:T(8,128)(2,1)}, bf16[128,3072]{1,0:T(8,128)(2,1)S(1)}, u32[]{:S(2)}, u32[]{:S(2)}) collective-permute-start(bf16[128,3072]{1,0:T(8,128)(2,1)} %get-tuple-element.17), channel_id=1, source_target_pairs={{0,32},{32,0},{64,96},{96,64},{128,160},{160,128},{192,224},{224,1... | collective-permute-start | bytes 2359304 | tf_op jit(solution)/shard_map/ppermute | solution.py:423
  58.2 9.0 %collective-permute-start.1 = (bf16[256,768]{1,0:T(8,128)(2,1)S(1)}, bf16[256,768]{1,0:T(8,128)(2,1)S(1)}, u32[]{:S(2)}, u32[]{:S(2)}) collective-permute-start(bf16[256,768]{1,0:T(8,128)(2,1)S(1)} %bitcast.11), channel_id=1, source_target_pairs={{0,32},{32,0},{64,96},{96,64},{128,160},{160,128},{192,224},{224,1... | collective-permute-start | bytes 1179656 | tf_op jit(solution)/shard_map/ppermute | solution.py:423
  58.2 5.9 %collective-permute-start.5 = (f32[8,512]{1,0:T(8,128)S(1)}, f32[8,512]{1,0:T(8,128)S(1)}, u32[]{:S(2)}, u32[]{:S(2)}) collective-permute-start(f32[8,512]{1,0:T(8,128)S(1)} %get-tuple-element.18.own), channel_id=1, source_target_pairs={{0,64},{96,32},{64,128},{160,96},{128,192},{224,160},{1,65},{97,33... | collective-permute-start | bytes 49160 | tf_op jit(solution)/shard_map/ppermute | solution.py:423
  61.4 5.1 %collective-permute-start.4 = (f32[8,512]{1,0:T(8,128)S(1)}, f32[8,512]{1,0:T(8,128)S(1)}, u32[]{:S(2)}, u32[]{:S(2)}) collective-permute-start(f32[8,512]{1,0:T(8,128)S(1)} %get-tuple-element.18.own), channel_id=1, source_target_pairs={{32,64},{64,32},{96,128},{128,96},{160,192},{192,160},{33,65},{65,... | collective-permute-start | bytes 49160 | tf_op jit(solution)/shard_map/ppermute | solution.py:423
  63.3 3.1 %collective-permute-start.3 = (f32[8,512]{1,0:T(8,128)S(1)}, f32[8,512]{1,0:T(8,128)S(1)}, u32[]{:S(2)}, u32[]{:S(2)}) collective-permute-start(f32[8,512]{1,0:T(8,128)S(1)} %get-tuple-element.18.own), channel_id=1, source_target_pairs={{0,32},{32,0},{64,96},{96,64},{128,160},{160,128},{192,224},{224,1... | collective-permute-start | bytes 49160 | tf_op jit(solution)/shard_map/ppermute | solution.py:423
  64.1 3.1 %collective-permute-start = (s32[1,8]{1,0:T(1,128)S(1)}, s32[1,8]{1,0:T(1,128)S(1)}, u32[]{:S(2)}, u32[]{:S(2)}) collective-permute-start(s32[1,8]{1,0:T(1,128)S(1)} %copy-done.1), channel_id=1, source_target_pairs={{0,32},{32,0},{64,96},{96,64},{128,160},{160,128},{192,224},{224,1... | collective-permute-start | bytes 104 | tf_op jit(solution)/shard_map/ppermute | solution.py:423
  69.3 18.5 %collective-permute-start.6 = (bf16[128,3072]{1,0:T(8,128)(2,1)S(1)}, bf16[128,3072]{1,0:T(8,128)(2,1)S(1)}, u32[]{:S(2)}, u32[]{:S(2)}) collective-permute-start(bf16[128,3072]{1,0:T(8,128)(2,1)S(1)} %get-tuple-element.21), channel_id=1, source_target_pairs={{32,64},{64,32},{96,128},{128,96},{160,192},{192,160},{33,65},{65,... | collective-permute-start | bytes 2359304 | tf_op jit(solution)/shard_map/ppermute | solution.py:423

commit v7 on v6

--- a/solution.py
+++ b/solution.py
@@ -116,20 +116,25 @@
 
 
 def spare_kernel(
-    counts, log_weights, read_out, particles, w0, w1, w2, w3, w4, out, rows, s0, s1, s2, s3, s4, sems, row_sem
+    counts_in, log_weights_in, read_out_in, particles, w0, w1, w2, w3, w4,
+    out, rows, s0, s1, s2, s3, s4, counts, log_weights, read_out, sems, row_sem, small_sem
 ):
     scratch = (s0, s1, s2, s3, s4)
     copies = fetches((w0, w1, w2, w3, w4), scratch, sems)
+    small = fetches((counts_in, log_weights_in, read_out_in), (counts, log_weights, read_out), small_sem)
+    for copy in (*small, *copies[:3]):
+        copy.start()
     block_rows = rows.shape[0]
+    small[0].wait()
     spare, vacant = find(counts, 2), find(counts, 0)
     slot = jnp.maximum(spare, 0)
     own = pltpu.make_async_copy(
         particles.at[pl.ds(pl.multiple_of(slot * block_rows, block_rows), block_rows), :], rows, row_sem
     )
     own.start()
-    for copy in copies[:3]:
-        copy.start()
     own.wait()
+    small[1].wait()
+    small[2].wait()
     width = rows.shape[1] // 4
 
     def keep(at, moved):
@@ -211,7 +216,7 @@
     moved_out.wait()
 
 
-def route_kernel(me, counts, pairs, log_weights, held, scalars, out, mine, tags):
+def route_kernel(held, out, tags):
     size = held.shape[0]
     width = out.shape[1]
     tag = held[:, width:]
@@ -230,6 +235,10 @@
     pick = jnp.where(hit, 1.0, 0.0).astype(BF16)
     out[...] = mul(pick, held[:, :width]).astype(BF16)
     tags[...] = mul(pick, tag)
+
+
+def lines_kernel(me, counts, pairs, log_weights, tags, scalars, mine):
+    half = LANES // 2
     got = tags[pl.ds(pl.multiple_of(me[0] * TILE, TILE), TILE), :]
     total = log_weights.shape[1]
 
@@ -405,11 +414,18 @@
     pieces = pl.pallas_call(
         spare_kernel,
         out_shape=shape((held_rows, width + LANES), BF16),
-        in_specs=[SMEM, VMEM, VMEM, ANY] + [ANY] * 5,
+        in_specs=[ANY] * 9,
         out_specs=VMEM,
         scratch_shapes=[pltpu.VMEM((block_rows, features), BF16)]
         + weight_scratch
-        + [pltpu.SemaphoreType.DMA((5,)), pltpu.SemaphoreType.DMA(())],
+        + [
+            pltpu.SMEM(offspring.shape, offspring.dtype),
+            pltpu.VMEM(log_weights.shape, F32),
+            pltpu.VMEM(read_out.shape, F32),
+            pltpu.SemaphoreType.DMA((5,)),
+            pltpu.SemaphoreType.DMA(()),
+            pltpu.SemaphoreType.DMA((3,)),
+        ],
         cost_estimate=cost(block_rows),
         name="spare",
     )(offspring, log_weights, read_out, rows, *weights)
@@ -446,15 +462,23 @@
     other_counts = swap(offspring, even)
 
     me = lax.axis_index("dom").astype(jnp.int32).reshape(1)
-    routed, mine = pl.pallas_call(
+    routed, tags = pl.pallas_call(
         route_kernel,
-        out_shape=(shape((held_rows, width), BF16), shape((TILE, total), F32)),
-        in_specs=[SMEM, SMEM, SMEM, VMEM, VMEM, VMEM],
+        out_shape=(shape((held_rows, width), BF16), shape((held_rows, LANES), F32)),
+        in_specs=[VMEM],
         out_specs=(VMEM, VMEM),
-        scratch_shapes=[pltpu.VMEM((held_rows, LANES), F32)],
         compiler_params=pltpu.CompilerParams(vmem_limit_bytes=16 << 20),
         name="route",
-    )(me, offspring, even_pairs, log_weights, inside(held), outside(scalars))
+    )(inside(held))
+    lay = pl.pallas_call(
+        lines_kernel,
+        out_shape=shape((TILE, total), F32),
+        in_specs=[SMEM, SMEM, SMEM, VMEM, VMEM, VMEM],
+        out_specs=VMEM,
+        compiler_params=pltpu.CompilerParams(vmem_limit_bytes=8 << 20),
+        name="lines",
+    )
+    mine = lay(me, offspring, even_pairs, log_weights, tags, outside(scalars))
     filled = exchange(routed)
 
     from_even = swap(mine, even)
@@ -534,4 +558,6 @@
     )
     out_specs = (P("temp", "dom", None), P("temp", "dom"), P("temp"))
 
-    return jax.shard_map(per_device, mesh=mesh, in_specs=in_specs, out_specs=out_specs, check_vma=False)
+    return jax.shard_map(
+        per_device, mesh=mesh, in_specs=in_specs, out_specs=out_specs, check_vma=False
+    )

time: 90.9 us -> 92.6 us (1.019)
  blocking collectives: 15.5 us -> 46.5 us
  waiting for transfers between devices: 17.8 us -> 2.68 us
  starting transfers between devices: 26.9 us -> 13.7 us
    all_to_all x1 -> x2, blocking collectives: 15.5 us -> 46.5 us  [exchange(): cut = lax.all_to_all(cut, 'dom', 0, 0, tiled=True)]
    all_to_all x2 -> x1, waiting for transfers between devices: 16 us -> 0.88 us  [exchange(): cut = lax.all_to_all(cut, 'dom', 0, 0, tiled=True)]
    all_to_all x2 -> x1, starting transfers between devices: 18.9 us -> 5.76 us  [exchange(): cut = lax.all_to_all(cut, 'dom', 0, 0, tiled=True)]
  transfers between devices with their start and end apart: 9 -> 8, of which waited for: 3 -> 2; matrix products, arithmetic and copies ran while one was open for 0% -> 0% of each run, Pallas kernels for 16% -> 17%
where the time goes in v7:
time: 92.6 us; the launch traced here: 91.4 us
  blocking collectives  46.5 us (50%)
  Pallas kernels  27 us (29%)
  starting transfers between devices  13.7 us (15%)
  waiting for transfers between devices  2.68 us (3%)
  between operations  1.45 us (2%)
    all_to_all x2, blocking collectives, exchange(): cut = lax.all_to_all(cut, 'dom', 0, 0, tiled=True)  46.5 us
    pallas_call x1, Pallas kernels, per_device(): pl.pallas_call(rows_kernel, out_shape=(shape((total, features), BF16), sh...  13.1 us
    ppermute x7, starting transfers between devices, swap(): return lax.ppermute(x, 'temp', pairs)  7.94 us
    pallas_call x1, Pallas kernels, per_device(): pl.pallas_call(spare_kernel, out_shape=shape((held_rows, width + LANES),...  6.92 us
    all_to_all x1, starting transfers between devices, exchange(): cut = lax.all_to_all(cut, 'dom', 0, 0, tiled=True)  5.76 us
    pallas_call x1, Pallas kernels, per_device(): pl.pallas_call(join_kernel, out_shape=(whole, pack), in_specs=[SMEM] * 4...  2.02 us
  transfers between devices with their start and end apart: 8, of which 2 were waited for; matrix products, arithmetic and copies ran while one was open for 0% of the time, Pallas kernels for 17%

profile of v7, /device:TPU:16, one launch (start us, length us, event | category | flops | bytes accessed | tf_op | source)
XLA Modules:
  0.0 91.4 jit_solution(9051285303016457302)
XLA Ops:
  0.6 6.9 %spare.1 = bf16[256,896]{1,0:T(8,128)(2,1)} custom-call(s32[1,8]{1,0:T(1,128)} %counts.3, f32[1,512]{1,0:T(1,128)} %log_weights.1, f32[1,512]{1,0:T(1,128)} %bitcast.19, bf16[512,3072]{1,0:T(8,128)(2,1)} %bitcast.16, bf16[1536,512]{1,0:T(8,128)(2,1)} %w0.3, bf16[512,512]{1,0:T(8,128)(2,1)} %w1.3, bf16[512,3072]{1,0:T(8,128)(2,1)} %w2.3, ...), custom_call_target="tpu_custom_call" | custom-call | flops 671088640 | bytes 8912896 | tf_op jit(solution)/shard_map/spare/pallas_call | solution.py:414
  7.6 26.6 %all_to_all.15 = bf16[32,8,896]{2,1,0:T(8,128)(2,1)S(1)} all-to-all(bf16[32,8,896]{2,1,0:T(8,128)(2,1)} %bitcast.18), channel_id=1, replica_groups=mesh['temp'=8,'dom'=32] {'dom'}, dimensions={0} | all-to-all | bytes 917504 | tf_op jit(solution)/shard_map/all_to_all | solution.py:435
  34.2 1.2 %route.1 = (bf16[256,768]{1,0:T(8,128)(2,1)}, f32[256,128]{1,0:T(8,128)S(1)}) custom-call(bf16[256,896]{1,0:T(8,128)(2,1)S(1)} %bitcast.10), custom_call_target="tpu_custom_call" | custom-call | tf_op jit(solution)/shard_map/route/pallas_call | solution.py:465
  35.4 5.8 %all-to-all-start.1 = ((bf16[32,8,768]{2,1,0:T(8,128)(2,1)}), bf16[32,8,768]{2,1,0:T(8,128)(2,1)S(1)}, u32[]{:S(2)}, u32[]{:S(2)}) async-start(bf16[32,8,768]{2,1,0:T(8,128)(2,1)} %bitcast.4), calls=%async_computation.1 | async-start | bytes 786432 | tf_op jit(solution)/shard_map/all_to_all | solution.py:435
  41.2 0.0 copy-start
  41.2 0.0 copy-start.1
  41.2 0.0 copy-start.2
  41.2 0.0 copy-start.3
  41.3 13.1 %rows.1 = (bf16[512,3072]{1,0:T(8,128)(2,1)}, f32[8,512]{1,0:T(8,128)}, bf16[128,3072]{1,0:T(8,128)(2,1)}) custom-call(s32[1,8]{1,0:T(1,128)} %even.3, f32[1,512]{1,0:T(1,128)} %bitcast.20, bf16[512,3072]{1,0:T(8,128)(2,1)} %bitcast.17, bf16[1536,512]{1,0:T(8,128)(2,1)} %w0.3, bf16[512,512]{1,0:T(8,128)(2,1)} %w1.3, bf16[512,3072]{1,0:T(8,128)(2,1)} %w2.3, ...), custom_call_target="tpu_custom_call" | custom-call | flops 5368709120 | bytes 8912896 | tf_op jit(solution)/shard_map/rows/pallas_call | solution.py:443
  54.3 0.1 collective-permute-start.2
  54.4 0.9 all-to-all-done.1
  55.3 0.0 collective-permute-start.1
  55.3 0.0 copy-done
  55.3 0.0 copy-done.1
  55.3 0.0 copy-done.2
  55.3 0.8 lines.1.own
  56.1 3.2 %collective-permute-start.5 = (f32[8,512]{1,0:T(8,128)S(1)}, f32[8,512]{1,0:T(8,128)S(1)}, u32[]{:S(2)}, u32[]{:S(2)}) collective-permute-start(f32[8,512]{1,0:T(8,128)S(1)} %lines.1.own), channel_id=1, source_target_pairs={{0,64},{96,32},{64,128},{160,96},{128,192},{224,160},{1,65},{97,33... | collective-permute-start | bytes 49160 | tf_op jit(solution)/shard_map/ppermute | solution.py:439
  59.3 1.9 %collective-permute-start.4 = (f32[8,512]{1,0:T(8,128)S(1)}, f32[8,512]{1,0:T(8,128)S(1)}, u32[]{:S(2)}, u32[]{:S(2)}) collective-permute-start(f32[8,512]{1,0:T(8,128)S(1)} %lines.1.own), channel_id=1, source_target_pairs={{32,64},{64,32},{96,128},{128,96},{160,192},{192,160},{33,65},{65,... | collective-permute-start | bytes 49160 | tf_op jit(solution)/shard_map/ppermute | solution.py:439
  61.3 0.1 collective-permute-start.3
  62.0 0.0 collective-permute-done.5.from_both
  62.0 0.6 collective-permute-start
  62.6 1.8 %collective-permute-done.4.from_odd = f32[8,512]{1,0:T(8,128)S(1)} collective-permute-done((f32[8,512]{1,0:T(8,128)S(1)}, f32[8,512]{1,0:T(8,128)S(1)}, u32[]{:S(2)}, u32[]{:S(2)}) %collective-permute-start.4) | collective-permute-done | bytes 16416 | tf_op jit(solution)/shard_map/ppermute | solution.py:439
  64.4 0.0 collective-permute-done.3.from_even
  64.4 0.0 copy-done.3
  64.4 0.7 stats.1
  65.2 0.0 collective-permute-done.other_counts
  65.2 0.0 collective-permute-done.2.received
  65.2 0.0 collective-permute-done.1.filled_other
  65.2 2.0 %join.1 = (bf16[512,3072]{1,0:T(8,128)(2,1)}, bf16[128,3072]{1,0:T(8,128)(2,1)S(1)}) custom-call(s32[1,8]{1,0:T(1,128)S(1)} %copy-done.1, s32[1,8]{1,0:T(1,128)S(1)} %collective-permute-done.other_counts, s32[1,8]{1,0:T(1,128)S(1)} %copy-done.2, s32[1,8]{1,0:T(1,128)S(1)} %copy-done.3, ...), custom_call_target="tpu_custom_call", output_to_operand_aliasing={{0}: (4, {})} | custom-call | tf_op jit(solution)/shard_map/join/pallas_call | solution.py:510
  67.2 2.0 %collective-permute-start.6 = (bf16[128,3072]{1,0:T(8,128)(2,1)S(1)}, bf16[128,3072]{1,0:T(8,128)(2,1)S(1)}, u32[]{:S(2)}, u32[]{:S(2)}) collective-permute-start(bf16[128,3072]{1,0:T(8,128)(2,1)S(1)} %get-tuple-element.21), channel_id=1, source_target_pairs={{32,64},{64,32},{96,128},{128,96},{160,192},{192,160},{33,65},{65,... | collective-permute-start | bytes 2359304 | tf_op jit(solution)/shard_map/ppermute | solution.py:439
  69.3 19.9 %all_to_all.16 = f32[32,8,128]{2,1,0:T(8,128)S(1)} all-to-all(f32[32,8,128]{2,1,0:T(8,128)S(1)} %bitcast.14), channel_id=1, replica_groups=mesh['temp'=8,'dom'=32] {'dom'}, dimensions={0} | all-to-all | bytes 262144 | tf_op jit(solution)/shard_map/all_to_all | solution.py:435
  89.1 0.9 final.1
  90.1 0.0 collective-permute-done.6.received
  90.1 1.3 %odd.5 = bf16[512,3072]{1,0:T(8,128)(2,1)} custom-call(s32[1,8]{1,0:T(1,128)S(1)} %copy-done.3, bf16[512,3072]{1,0:T(8,128)(2,1)} %get-tuple-element.20.rows_in, bf16[128,3072]{1,0:T(8,128)(2,1)S(1)} %collective-permute-done.6.received), custom_call_target="tpu_custom_call", output_to_operand_aliasing={{}: (1, {})} | custom-call | tf_op jit(solution)/shard_map/odd/pallas_call | solution.py:531
Async XLA Ops:
  35.4 19.9 %all-to-all-start.1 = ((bf16[32,8,768]{2,1,0:T(8,128)(2,1)}), bf16[32,8,768]{2,1,0:T(8,128)(2,1)S(1)}, u32[]{:S(2)}, u32[]{:S(2)}) async-start(bf16[32,8,768]{2,1,0:T(8,128)(2,1)} %bitcast.4), calls=%async_computation.1 | async-start | bytes 786432 | tf_op jit(solution)/shard_map/all_to_all | solution.py:435
  41.2 14.1 %copy-start = (f32[1,512]{1,0:T(1,128)S(1)}, f32[1,512]{1,0:T(1,128)}, u32[]{:S(2)}) copy-start(f32[1,512]{1,0:T(1,128)} %log_weights.1) | copy-start | bytes 6148
  41.2 14.1 %copy-start.1 = (s32[1,8]{1,0:T(1,128)S(1)}, s32[1,8]{1,0:T(1,128)}, u32[]{:S(2)}) copy-start(s32[1,8]{1,0:T(1,128)} %counts.3) | copy-start | bytes 100
  41.2 14.1 %copy-start.2 = (s32[1,8]{1,0:T(1,128)S(1)}, s32[1,8]{1,0:T(1,128)}, u32[]{:S(2)}) copy-start(s32[1,8]{1,0:T(1,128)} %even.3) | copy-start | bytes 100
  41.2 23.2 %copy-start.3 = (s32[1,8]{1,0:T(1,128)S(1)}, s32[1,8]{1,0:T(1,128)}, u32[]{:S(2)}) copy-start(s32[1,8]{1,0:T(1,128)} %flags.1) | copy-start | bytes 100
  54.3 10.8 %collective-permute-start.2 = (bf16[128,3072]{1,0:T(8,128)(2,1)}, bf16[128,3072]{1,0:T(8,128)(2,1)S(1)}, u32[]{:S(2)}, u32[]{:S(2)}) collective-permute-start(bf16[128,3072]{1,0:T(8,128)(2,1)} %get-tuple-element.16), channel_id=1, source_target_pairs={{0,32},{32,0},{64,96},{96,64},{128,160},{160,128},{192,224},{224,1... | collective-permute-start | bytes 2359304 | tf_op jit(solution)/shard_map/ppermute | solution.py:439
  55.3 9.9 %collective-permute-start.1 = (bf16[256,768]{1,0:T(8,128)(2,1)S(1)}, bf16[256,768]{1,0:T(8,128)(2,1)S(1)}, u32[]{:S(2)}, u32[]{:S(2)}) collective-permute-start(bf16[256,768]{1,0:T(8,128)(2,1)S(1)} %bitcast.11), channel_id=1, source_target_pairs={{0,32},{32,0},{64,96},{96,64},{128,160},{160,128},{192,224},{224,1... | collective-permute-start | bytes 1179656 | tf_op jit(solution)/shard_map/ppermute | solution.py:439
  56.1 5.9 %collective-permute-start.5 = (f32[8,512]{1,0:T(8,128)S(1)}, f32[8,512]{1,0:T(8,128)S(1)}, u32[]{:S(2)}, u32[]{:S(2)}) collective-permute-start(f32[8,512]{1,0:T(8,128)S(1)} %lines.1.own), channel_id=1, source_target_pairs={{0,64},{96,32},{64,128},{160,96},{128,192},{224,160},{1,65},{97,33... | collective-permute-start | bytes 49160 | tf_op jit(solution)/shard_map/ppermute | solution.py:439
  59.3 5.1 %collective-permute-start.4 = (f32[8,512]{1,0:T(8,128)S(1)}, f32[8,512]{1,0:T(8,128)S(1)}, u32[]{:S(2)}, u32[]{:S(2)}) collective-permute-start(f32[8,512]{1,0:T(8,128)S(1)} %lines.1.own), channel_id=1, source_target_pairs={{32,64},{64,32},{96,128},{128,96},{160,192},{192,160},{33,65},{65,... | collective-permute-start | bytes 49160 | tf_op jit(solution)/shard_map/ppermute | solution.py:439
  61.3 3.1 %collective-permute-start.3 = (f32[8,512]{1,0:T(8,128)S(1)}, f32[8,512]{1,0:T(8,128)S(1)}, u32[]{:S(2)}, u32[]{:S(2)}) collective-permute-start(f32[8,512]{1,0:T(8,128)S(1)} %lines.1.own), channel_id=1, source_target_pairs={{0,32},{32,0},{64,96},{96,64},{128,160},{160,128},{192,224},{224,1... | collective-permute-start | bytes 49160 | tf_op jit(solution)/shard_map/ppermute | solution.py:439
  62.0 3.1 %collective-permute-start = (s32[1,8]{1,0:T(1,128)S(1)}, s32[1,8]{1,0:T(1,128)S(1)}, u32[]{:S(2)}, u32[]{:S(2)}) collective-permute-start(s32[1,8]{1,0:T(1,128)S(1)} %copy-done.1), channel_id=1, source_target_pairs={{0,32},{32,0},{64,96},{96,64},{128,160},{160,128},{192,224},{224,1... | collective-permute-start | bytes 104 | tf_op jit(solution)/shard_map/ppermute | solution.py:439
  67.2 22.9 %collective-permute-start.6 = (bf16[128,3072]{1,0:T(8,128)(2,1)S(1)}, bf16[128,3072]{1,0:T(8,128)(2,1)S(1)}, u32[]{:S(2)}, u32[]{:S(2)}) collective-permute-start(bf16[128,3072]{1,0:T(8,128)(2,1)S(1)} %get-tuple-element.21), channel_id=1, source_target_pairs={{32,64},{64,32},{96,128},{128,96},{160,192},{192,160},{33,65},{65,... | collective-permute-start | bytes 2359304 | tf_op jit(solution)/shard_map/ppermute | solution.py:439
